TPU v7x, 32 devices: a whole 2x2x4 slice. The times are simulated.
32 devices in a mesh: rows: 16 (over z, y, core), tm: 2 (over x).
Axes of the slice: x: 2, y: 2, z: 4, core: 2. Of those that a mesh axis runs over, the one named last changes fastest.
Arguments:
- tokens: bfloat16 [16, 1024, 1024], P('rows', 'tm')
- cotangent: float32 [16, 1024, 1024], P('rows', 'tm'), may hold values from -6 to 6
- segment_ids: int32 [16, 1024], P('rows', 'tm'), may hold values from 0 to 5, never falling along the last dimension, each value on 1 to 341 neighbouring positions
- rel_bucket: int32 [513], replicated, may hold values from 0 to 127, as said below
- ffn1_in: bfloat16 [1024, 4096], P('rows'), may hold values from -0.1875 to 0.1875
- ffn1_out: bfloat16 [4096, 1024], P('rows'), may hold values from -0.09375 to 0.09375
- qkv_weight: bfloat16 [1024, 3072], P('rows'), may hold values from -0.1875 to 0.1875
- attn_out: bfloat16 [1024, 1024], P('rows'), may hold values from -0.75 to 0.75
- glu_in: bfloat16 [1024, 2048], P('rows'), may hold values from -0.1875 to 0.1875
- conv_out: bfloat16 [1024, 1024], P('rows'), may hold values from -0.1875 to 0.1875
- ffn2_in: bfloat16 [1024, 4096], P('rows'), may hold values from -0.1875 to 0.1875
- ffn2_out: bfloat16 [4096, 1024], P('rows'), may hold values from -0.09375 to 0.09375
- gains: bfloat16 [6, 1024], P(None, 'rows'), may hold values from 0.5 to 1.5
- shifts: bfloat16 [14, 1024], P(None, 'rows'), may hold values from -2 to 2
- ffn_bias: bfloat16 [2, 4096], P(None, 'rows'), may hold values from -2 to 2
- conv_kernel: bfloat16 [5, 1024], P(None, 'rows'), may hold values from -3 to 3
- rel_table: bfloat16 [1024], P('rows'), may hold values from -4 to 4
Outputs:
- output: float32 [16, 1024, 1024], P('rows', 'tm')
- tokens_grad: float32 [16, 1024, 1024], P('rows', 'tm')
- ffn1_in_grad: float32 [1024, 4096], P('rows')
- ffn1_out_grad: float32 [4096, 1024], P('rows')
- qkv_weight_grad: float32 [1024, 3072], P('rows')
- attn_out_grad: float32 [1024, 1024], P('rows')
- glu_in_grad: float32 [1024, 2048], P('rows')
- conv_out_grad: float32 [1024, 1024], P('rows')
- ffn2_in_grad: float32 [1024, 4096], P('rows')
- ffn2_out_grad: float32 [4096, 1024], P('rows')
- gains_grad: float32 [6, 1024], P(None, 'rows')
- shifts_grad: float32 [14, 1024], P(None, 'rows')
- ffn_bias_grad: float32 [2, 4096], P(None, 'rows')
- conv_kernel_grad: float32 [5, 1024], P(None, 'rows')
- rel_table_grad: float32 [1024], P('rows')
Inputs may be any that keep to these rules, and one draw needn't show every extreme that they name: `segment_ids`: within a row the ids never fall; every utterance has 1 to 341 frames, the longest exactly that. `rel_bucket`: never falls from distance -256 to +256; 0 at -256 and 127 at +256.
All inputs are finite; a program needn't handle non-finite values.
Results may differ from a plain program's by a relative error of at most 0.035.
Values may be sent and summed in bfloat16 or wider, within the bound.
A program may use at most 320 MiB of HBM per device.

v0:
```python
import functools
import math

import jax
import jax.numpy as jnp
import numpy as np
from jax import lax
from jax.experimental import pallas as pl
from jax.experimental.pallas import tpu as pltpu
from jax.sharding import PartitionSpec as P

HEADS = 8
KSIZE = 5
NB = 128
MAXD = 256


EPS = 1e-05
NEG = -1e30
HIGH = lax.Precision.HIGHEST


MESH = pl.DeviceIdType.MESH
ANY = pl.ANY


def place():
    r = lax.axis_index("rows")
    t = lax.axis_index("tm")
    return r, t, lax.rem(r, 2), lax.rem(r // 2, 2), r // 4


def remote(src, dst, send, recv, rows, tm):
    pltpu.make_async_remote_copy(
        src_ref=src, dst_ref=dst, send_sem=send, recv_sem=recv,
        device_id=(rows, tm), device_id_type=MESH,
    ).start()


def landed(ref, sem):
    pltpu.make_async_copy(ref, ref, sem).wait()


def greet(peers):
    barrier = pltpu.get_barrier_semaphore()
    for rows, tm in peers:
        pl.semaphore_signal(barrier, inc=1, device_id=(rows, tm), device_id_type=MESH)
    pl.semaphore_wait(barrier, len(peers))


def link_peers():
    r, t, c, y, z = place()
    return [(r + 1 - 2 * c, t), (r + 2 - 4 * y, t), (lax.rem(r + 4, 16), t), (lax.rem(r + 12, 16), t), (r, 1 - t)]


def loop(n, fn, first=0):
    def one(i, carry):
        fn(i)
        return carry
    lax.fori_loop(first, n, one, 0)


UNIT = 64
EDGE = 24
MIDDLE = UNIT - 2 * EDGE
PLANE = EDGE + MIDDLE


class Gather:
    LEAD = 3
    EVENTS = (("from_z", 1, 0), ("from_y", 0, 0), ("from_z", 2, 1), ("from_y", 1, 1), ("from_x", 0, 1), ("from_z", 3, 2),
              ("from_y", 2, 2), ("from_x", 1, 2), ("from_y", 3, 3), ("from_x", 2, 3), ("from_x", 3, 4))
    LAG = 4

    def __init__(self, full, first, units, sems):
        self.full, self.first, self.units = full, first, units
        self.zr, self.yr, self.xr, self.cr, self.snd = sems
        self.r, self.t, self.c, self.y, self.z = place()
        self.taken = set()

    @staticmethod
    def scratch(units):
        sem = pltpu.SemaphoreType.DMA
        return [sem((units, 4)), sem((units, 4)), sem((units, 8)), sem((units,)), sem((5,))]

    def slot(self, z, y):
        return z * 4 + y * 2 + self.c

    def rows_of(self, unit, start, size):
        return pl.ds(pl.multiple_of((unit + self.first) * UNIT + start, 8), size)

    def inplane(self, slot, unit):
        return self.full.at[slot, self.rows_of(unit, self.t * EDGE, PLANE)]

    def edge(self, slot, unit, tm):
        return self.full.at[slot, self.rows_of(unit, tm * PLANE, EDGE)]

    def to_core(self, ref, unit):
        remote(ref, ref, self.snd.at[4], self.cr.at[unit], self.r + 1 - 2 * self.c, self.t)

    def send_own(self, unit):
        r, t, z = self.r, self.t, self.z
        plane = self.inplane(r, unit)

        @pl.when(z < 3)
        def _():
            remote(plane, plane, self.snd.at[0], self.zr.at[unit, z], r + 4, t)

        @pl.when(z > 0)
        def _():
            remote(plane, plane, self.snd.at[1], self.zr.at[unit, z], r - 4, t)

        remote(plane, plane, self.snd.at[2], self.yr.at[unit, z], self.slot(z, 1 - self.y), t)
        self.to_core(self.full.at[r, self.rows_of(unit, 0, UNIT)], unit)

    def pass_on(self, unit, z, y):
        s = self.slot(z, y)
        part = self.edge(s, unit, self.t)
        remote(part, part, self.snd.at[3], self.xr.at[unit, z * 2 + y], self.r, 1 - self.t)
        self.to_core(self.inplane(s, unit), unit)

    def from_z(self, unit, distance):
        for sign in (-1, 1):
            z = self.z + sign * distance

            @pl.when((z >= 0) & (z <= 3))
            def _(z=z, sign=sign):
                plane = self.inplane(self.slot(z, self.y), unit)
                landed(plane, self.zr.at[unit, z])
                onward = self.z - sign

                @pl.when((onward >= 0) & (onward <= 3))
                def _():
                    remote(plane, plane, self.snd.at[0 if sign < 0 else 1], self.zr.at[unit, z], self.slot(onward, self.y), self.t)

                remote(plane, plane, self.snd.at[2], self.yr.at[unit, z], self.slot(self.z, 1 - self.y), self.t)
                self.pass_on(unit, z, self.y)

    def from_y(self, unit, distance):
        for sign in (-1, 1) if distance else (1,):
            z = self.z + sign * distance

            @pl.when((z >= 0) & (z <= 3))
            def _(z=z):
                landed(self.inplane(self.slot(z, 1 - self.y), unit), self.yr.at[unit, z])
                self.pass_on(unit, z, 1 - self.y)

    def from_x(self, unit, distance):
        for other in (False, True) if distance else (True,):
            y = 1 - self.y if other else self.y
            for sign in (-1, 1) if distance else (1,):
                z = self.z + sign * distance

                @pl.when((z >= 0) & (z <= 3))
                def _(z=z, y=y):
                    part = self.edge(self.slot(z, y), unit, 1 - self.t)
                    landed(part, self.xr.at[unit, z * 2 + y])
                    self.to_core(part, unit)

    def begin(self):
        for unit in range(min(self.LEAD, self.units)):
            self.send_own(unit)

    def tick(self, step):
        for name, distance, lag in self.EVENTS:
            unit = step - lag

            @pl.when((unit >= 0) & (unit < self.units))
            def _(name=name, distance=distance, unit=unit):
                getattr(self, name)(unit, distance)
        unit = step + self.LEAD

        @pl.when(unit < self.units)
        def _():
            self.send_own(unit)

    def run(self, first, last):
        loop(last, self.tick, first)

    def arrived(self, unit):
        self.taken.add(unit)
        landed(self.full.at[0:8, self.rows_of(unit, 0, UNIT)], self.cr.at[unit])

    def finish(self):
        full, units, z = self.full, self.units, self.z
        for unit in range(units):
            if unit not in self.taken:
                self.arrived(unit)
        plane = units * PLANE
        for k in range(4):
            @pl.when(z == k)
            def _(k=k):
                if k < 3:
                    landed(full.at[0:k + 1, 0:plane], self.snd.at[0])
                if k > 0:
                    landed(full.at[0:4 - k, 0:plane], self.snd.at[1])
        landed(full.at[0:4, 0:plane], self.snd.at[2])
        landed(full.at[0:7, 0:units * EDGE], self.snd.at[3])
        landed(full.at[0:8, 0:units * UNIT], self.snd.at[4])


S_EDGE = 16
S_MIDDLE = UNIT - 2 * S_EDGE
S_PLANE = S_EDGE + S_MIDDLE


class Scatter:
    def __init__(self, grads, out, units, bufs, sems):
        self.grads, self.out, self.units = grads, out, units
        self.own, self.obuf, self.cv, self.xv, self.yv, self.zv, self.fv = bufs
        self.load, self.store, self.cr, self.xr, self.yr, self.zr, self.fr, self.snd = sems
        self.r, self.t, self.c, self.y, self.z = place()

    def mine(self):
        return pl.ds(pl.multiple_of(self.t * S_EDGE, 16), S_PLANE)

    def edge(self, tm):
        return pl.ds(pl.multiple_of(tm * S_PLANE, 16), S_EDGE)

    def own_copy(self, unit):
        rows = pl.ds(pl.multiple_of(unit * UNIT, UNIT), UNIT)
        return pltpu.make_async_copy(self.grads.at[:, self.c, rows], self.own.at[lax.rem(unit, 2)], self.load.at[lax.rem(unit, 2)])

    def send_core(self, unit):
        rows = pl.ds(pl.multiple_of(unit * UNIT, UNIT), UNIT)
        remote(self.grads.at[:, 1 - self.c, rows], self.cv.at[unit], self.snd.at[0], self.cr.at[unit], self.r + 1 - 2 * self.c, self.t)

    def add(self, a, b, n):
        def one(i, carry):
            a[i] = (a[i].astype(jnp.float32) + b[i].astype(jnp.float32)).astype(jnp.bfloat16)
            return carry
        lax.fori_loop(0, n, one, 0)

    def sum_core(self, unit):
        cv = self.cv.at[unit]
        landed(cv, self.cr.at[unit])
        self.own_copy(unit).wait()
        self.add(cv, self.own.at[lax.rem(unit, 2)], 8)

        @pl.when(unit + 2 < self.units)
        def _():
            self.own_copy(unit + 2).start()
        remote(cv.at[:, self.edge(1 - self.t)], self.xv.at[unit], self.snd.at[1], self.xr.at[unit], self.r, 1 - self.t)

    def sum_x(self, unit):
        xv, cv = self.xv.at[unit], self.cv.at[unit]
        landed(xv, self.xr.at[unit])
        self.add(cv.at[:, self.edge(self.t)], xv, 8)
        for k in range(4):
            remote(cv.at[k * 2 + 1 - self.y, self.mine()], self.yv.at[unit, k], self.snd.at[2], self.yr.at[unit, k], self.r + 2 - 4 * self.y, self.t)

    def at_z(self, unit, z):
        return self.cv.at[unit, z * 2 + self.y, self.mine()]

    def send_z(self, unit, target, up):
        at = self.at_z(unit, target)
        remote(at, self.zv.at[unit, target + (1 if up else 0)], self.snd.at[3 if up else 4], self.zr.at[unit, target + (1 if up else 0)],
               self.r + (4 if up else -4), self.t)

    def take_z(self, unit, target, below):
        at = self.at_z(unit, target)
        entry = target + (1 if below else 0)
        zv = self.zv.at[unit, entry]
        landed(zv, self.zr.at[unit, entry])
        at[...] = (at[...].astype(jnp.float32) + zv[...].astype(jnp.float32)).astype(jnp.bfloat16)

    def sum_y(self, unit):
        for k in range(4):
            yv = self.yv.at[unit, k]
            landed(yv, self.yr.at[unit, k])
            at = self.at_z(unit, k)
            at[...] = (at[...].astype(jnp.float32) + yv[...].astype(jnp.float32)).astype(jnp.bfloat16)

        @pl.when(self.z == 0)
        def _():
            for target in (3, 2, 1):
                self.send_z(unit, target, True)

        @pl.when(self.z == 3)
        def _():
            for target in (0, 1, 2):
                self.send_z(unit, target, False)

    def hop(self, unit, number):
        for z in range(4):
            @pl.when(self.z == z)
            def _(z=z):
                if number == z:
                    for target in range(3, z - 1, -1):
                        self.take_z(unit, target, True)
                        if target > z:
                            self.send_z(unit, target, True)
                if number == 3 - z:
                    for target in range(0, z + 1):
                        self.take_z(unit, target, False)
                        if target < z:
                            self.send_z(unit, target, False)

    def exchange(self, unit):
        at = self.at_z(unit, self.z)
        remote(at, self.fv.at[unit], self.snd.at[5], self.fr.at[unit], self.r, 1 - self.t)

    def store_copy(self, unit):
        return pltpu.make_async_copy(self.obuf.at[lax.rem(unit, 2)], self.out.at[pl.ds(pl.multiple_of(unit * UNIT, UNIT), UNIT)], self.store.at[lax.rem(unit, 2)])

    def conclude(self, unit):
        fv = self.fv.at[unit]
        landed(fv, self.fr.at[unit])
        at = self.cv.at[unit, self.z * 2 + self.y]

        @pl.when(unit >= 2)
        def _():
            self.store_copy(unit - 2).wait()
        obuf = self.obuf.at[lax.rem(unit, 2)]
        middle = pl.ds(S_EDGE, S_MIDDLE)
        obuf[middle] = at[middle].astype(jnp.float32) + fv[pl.ds(pl.multiple_of(self.t * S_EDGE, 16), S_MIDDLE)].astype(jnp.float32)
        obuf[self.edge(self.t)] = at[self.edge(self.t)].astype(jnp.float32)
        obuf[self.edge(1 - self.t)] = fv[pl.ds(pl.multiple_of((1 - self.t) * S_MIDDLE, 16), S_EDGE)].astype(jnp.float32)
        self.store_copy(unit).start()

    LEAD = 3
    EVENTS = (("sum_core", 0, ()), ("sum_x", 1, ()), ("sum_y", 2, ()), ("hop", 3, (1,)), ("hop", 4, (2,)), ("hop", 5, (3,)), ("exchange", 5, ()), ("conclude", 6, ()))

    def ticks(self):
        return self.units + max(e[1] for e in self.EVENTS)

    def begin(self):
        for unit in range(min(2, self.units)):
            self.own_copy(unit).start()
        for unit in range(min(self.LEAD, self.units)):
            self.send_core(unit)

    def tick(self, step):
        for name, lag, args in self.EVENTS:
            unit = step - lag

            @pl.when((unit >= 0) & (unit < self.units))
            def _(name=name, unit=unit, args=args):
                getattr(self, name)(unit, *args)
        unit = step + self.LEAD

        @pl.when(unit < self.units)
        def _():
            self.send_core(unit)

    def finish(self):
        units, z, grads = self.units, self.z, self.grads
        for unit in range(max(0, units - 2), units):
            self.store_copy(unit).wait()
        landed(grads.at[:, 0, 0:units * UNIT], self.snd.at[0])
        landed(grads.at[:, 0, 0:units * S_EDGE], self.snd.at[1])
        landed(grads.at[0:4, 0, 0:units * S_PLANE], self.snd.at[2])
        for k in range(4):
            @pl.when(z == k)
            def _(k=k):
                if k < 3:
                    landed(grads.at[0:3 - k, 0, 0:units * S_PLANE], self.snd.at[3])
                if k > 0:
                    landed(grads.at[0:k, 0, 0:units * S_PLANE], self.snd.at[4])
        landed(grads.at[0, 0, 0:units * S_PLANE], self.snd.at[5])


def scatter_kernel(units, grads, small, out, small_out, own, obuf, cv, xv, yv, zv, fv, sown, sv, sx, load, store, cr, xr, yr, zr, fr, snd, sload, ssend, srecv, sxsem):
    r, t, c, y, z = place()
    R = lax.axis_size("rows")
    cs = pltpu.make_async_copy(small, sown, sload.at[0])
    cs.start()
    greet([(lax.rem(r + d, R), t) for d in range(1, R)] + [(r, 1 - t)])
    s = Scatter(grads, out, units, (own, obuf, cv, xv, yv, zv, fv), (load, store, cr, xr, yr, zr, fr, snd))
    s.begin()
    cs.wait()
    for d in range(1, R):
        to = lax.rem(r + d, R)
        remote(sown.at[to], sv.at[R - 1 - d], ssend, srecv, to, t)

    def step(i, carry):
        s.tick(i)
        return carry

    lax.fori_loop(0, s.ticks(), step, 0)
    landed(sown.at[0:R - 1], ssend)
    landed(sv.at[0:R - 1], srecv)
    total = sown[r]
    for d in range(R - 1):
        total = total + sv[d]
    sx[0] = total
    pltpu.make_async_remote_copy(src_ref=sx.at[0], dst_ref=sx.at[1], send_sem=sxsem.at[0], recv_sem=sxsem.at[1], device_id=(r, 1 - t), device_id_type=MESH).start()
    landed(sx.at[0], sxsem.at[0])
    landed(sx.at[1], sxsem.at[1])
    sx[0] = sx[0] + sx[1]
    done = pltpu.make_async_copy(sx.at[0], small_out, sload.at[1])
    done.start()
    s.finish()
    done.wait()


def scatter_call(grads, small, cid):
    R, rows, _ = grads.shape
    units = rows // UNIT
    bf = jnp.bfloat16
    return pl.pallas_call(
        functools.partial(scatter_kernel, units),
        out_shape=(jax.ShapeDtypeStruct((rows, 1024), jnp.float32), jax.ShapeDtypeStruct(small.shape[1:], small.dtype)),
        in_specs=[pl.BlockSpec(memory_space=ANY)] * 2,
        out_specs=(pl.BlockSpec(memory_space=ANY), pl.BlockSpec(memory_space=ANY)),
        scratch_shapes=[pltpu.VMEM((2, 8, UNIT, 1024), bf), pltpu.VMEM((2, UNIT, 1024), jnp.float32),
                        pltpu.VMEM((units, 8, UNIT, 1024), bf), pltpu.VMEM((units, 8, S_EDGE, 1024), bf), pltpu.VMEM((units, 4, S_PLANE, 1024), bf),
                        pltpu.VMEM((units, 5, S_PLANE, 1024), bf), pltpu.VMEM((units, S_PLANE, 1024), bf),
                        pltpu.VMEM(small.shape, small.dtype), pltpu.VMEM((R - 1,) + small.shape[1:], small.dtype), pltpu.VMEM((2,) + small.shape[1:], small.dtype),
                        pltpu.SemaphoreType.DMA((2,)), pltpu.SemaphoreType.DMA((2,)), pltpu.SemaphoreType.DMA((units,)), pltpu.SemaphoreType.DMA((units,)),
                        pltpu.SemaphoreType.DMA((units, 4)), pltpu.SemaphoreType.DMA((units, 5)), pltpu.SemaphoreType.DMA((units,)), pltpu.SemaphoreType.DMA((6,)),
                        pltpu.SemaphoreType.DMA((2,)), pltpu.SemaphoreType.DMA, pltpu.SemaphoreType.DMA, pltpu.SemaphoreType.DMA((2,))],
        compiler_params=pltpu.CompilerParams(collective_id=cid, has_side_effects=True, vmem_limit_bytes=67043328),
        name="scatter_grads",
    )(grads.reshape(R // 2, 2, rows, 1024), small)


HALO = 384
FI1, FO1, QKV, ATT, GLU, CONV, FI2, FO2, UNITS = 0, 4, 8, 11, 12, 14, 15, 19, 23
GAIN, SHIFT, BIAS, TAPS, REL = 0, 6, 20, 28, 33
F32, BF16 = jnp.float32, jnp.bfloat16
TILE = 1024
NN = (((1,), (0,)), ((), ()))
NT = (((1,), (1,)), ((), ()))
TN = (((0,), (0,)), ((), ()))
VMEM_LIMIT = 67043328


def dot(a, b, dims=NN):
    return lax.dot_general(a, b, dims, preferred_element_type=F32)


def by_rows(count, size, fn):
    loop(count // size, lambda i: fn(pl.ds(pl.multiple_of(i * size, size), size)))


def by_cols(count, fn):
    loop(count // TILE, lambda i: fn(pl.ds(pl.multiple_of(i * TILE, TILE), TILE)))


def normalized(v):
    centred = v - jnp.mean(v, axis=-1, keepdims=True)
    rs = lax.rsqrt(jnp.mean(centred * centred, axis=-1, keepdims=True) + EPS)
    return centred * rs, rs


def norm_back(w, gain, vhat, rs):
    wg = w * gain
    return rs * (wg - jnp.mean(wg, axis=-1, keepdims=True) - vhat * jnp.mean(wg * vhat, axis=-1, keepdims=True))


def eight(v):
    return jnp.sum(v.reshape(v.shape[0] // 8, 8, v.shape[1]), axis=0)


def sigmoid(v):
    return 1.0 / (1.0 + jnp.exp(-v))


class Weights:
    def __init__(self, full, buf, sems, blocks):
        self.full, self.buf, self.sems, self.blocks = full, buf, sems, blocks
        self.R = full.shape[0]
        self.n = 1024 // self.R

    def copies(self, k):
        unit, kind, index = self.blocks[k]
        n, R = self.n, self.R
        if kind == "in":
            return [(self.full.at[s, (unit + index) * n:(unit + index + 1) * n], self.buf.at[k, s * n:(s + 1) * n]) for s in range(R)]
        return [(self.full.at[index * (R // 4) + s, unit * n:(unit + 4) * n], self.buf.at[k, s * 4 * n:(s + 1) * 4 * n]) for s in range(R // 4)]

    def start(self, *ks):
        for k in ks or range(len(self.blocks)):
            for src, dst in self.copies(k):
                pltpu.make_async_copy(src, dst, self.sems.at[k]).start()

    def wait(self, *ks):
        for k in ks:
            pltpu.make_async_copy(self.buf.at[k], self.buf.at[k], self.sems.at[k]).wait()


class Grads:
    def __init__(self, out, buf, sems):
        self.out, self.buf, self.sems, self.count = out, buf, sems, 0
        self.R = out.shape[0]
        self.n = 1024 // self.R

    def put(self, unit, kind, index, left, right):
        slot = self.count % 2
        buf, n, R = self.buf.at[slot], self.n, self.R
        if self.count >= 2:
            self.wait(slot)

        def cols(c):
            buf[:, c] = dot(left, right(c), TN).astype(BF16)
        by_cols(1024, cols)
        if kind == "in":
            pairs = [(buf.at[s * n:(s + 1) * n], self.out.at[s, (unit + index) * n:(unit + index + 1) * n]) for s in range(R)]
        else:
            pairs = [(buf.at[s * 4 * n:(s + 1) * 4 * n], self.out.at[index * (R // 4) + s, unit * n:(unit + 4) * n]) for s in range(R // 4)]
        for src, dst in pairs:
            pltpu.make_async_copy(src, dst, self.sems.at[slot]).start()
        self.count += 1

    def wait(self, slot):
        pltpu.make_async_copy(self.buf.at[slot], self.buf.at[slot], self.sems.at[slot]).wait()

    def finish(self):
        for slot in range(min(2, self.count)):
            self.wait(slot)


def flipped(x, size):
    m = size
    return x + m - 2 * m * lax.rem(x // m, 2)


def cube_peers():
    r, t = lax.axis_index("rows"), lax.axis_index("tm")
    peers, m = [], 1
    while m < lax.axis_size("rows"):
        peers.append((flipped(r, m), t))
        m *= 2
    m = 1
    while m < lax.axis_size("tm"):
        peers.append((r, flipped(t, m)))
        m *= 2
    return peers


def add_all(send, recv, ssem, rsem):
    for i, (rows, tm) in enumerate(cube_peers()):
        remote(send.at[i], recv.at[i], ssem.at[i], rsem.at[i], rows, tm)
        landed(send.at[i], ssem.at[i])
        landed(recv.at[i], rsem.at[i])
        send[i + 1] = send[i] + recv[i]
    return len(cube_peers())


def edge_peers():
    r, t, T = lax.axis_index("rows"), lax.axis_index("tm"), lax.axis_size("tm")
    return [(r, lax.rem(t + 1, T)), (r, lax.rem(t + T - 1, T))]


def swap_edges(pad, count, sems):
    r, t, T = lax.axis_index("rows"), lax.axis_index("tm"), lax.axis_size("tm")

    @pl.when(t < T - 1)
    def _():
        remote(pad.at[count:count + 8], pad.at[0:8], sems.at[0], sems.at[1], r, t + 1)

    @pl.when(t > 0)
    def _():
        remote(pad.at[8:16], pad.at[count + 8:count + 16], sems.at[2], sems.at[3], r, t - 1)

    @pl.when(t < T - 1)
    def _():
        landed(pad.at[0:8], sems.at[0])
        landed(pad.at[0:8], sems.at[3])

    @pl.when(t > 0)
    def _():
        landed(pad.at[0:8], sems.at[2])
        landed(pad.at[0:8], sems.at[1])


def whole():
    return pl.BlockSpec(memory_space=pltpu.VMEM)


def anywhere():
    return pl.BlockSpec(memory_space=ANY)


def shape(*dims, dtype=F32):
    return jax.ShapeDtypeStruct(dims, dtype)


BLOCKS_A = tuple([(FI1, "in", j) for j in range(4)] + [(FO1, "out", j) for j in range(4)] + [(QKV, "in", j) for j in range(3)])


def norm_tokens(tokens, params, a):
    def norm(rows):
        vhat, _ = normalized(tokens[rows].astype(F32))
        a[rows] = (vhat * params[GAIN:GAIN + 1] + params[SHIFT:SHIFT + 1]).astype(BF16)
    by_rows(tokens.shape[0], 256, norm)


def norm_resid(x1, params, a):
    def norm(rows):
        vhat, _ = normalized(x1[rows])
        a[rows] = (vhat * params[GAIN + 1:GAIN + 2] + params[SHIFT + 1:SHIFT + 2]).astype(BF16)
    by_rows(x1.shape[0], 256, norm)


class Front:
    def __init__(self, w, params, tokens, x1, z1, a, h, zbuf, zsem):
        self.w, self.params, self.tokens, self.x1, self.z1, self.a, self.h, self.zbuf, self.zsem = w, params, tokens, x1, z1, a, h, zbuf, zsem

    def stored(self, slot):
        pltpu.make_async_copy(self.zbuf.at[slot], self.zbuf.at[slot], self.zsem.at[slot]).wait()

    def hidden(self, j):
        slot = j % 2
        self.w.wait(j)
        if j >= 2:
            self.stored(slot)
        z = dot(self.a[...], self.w.buf[j]) + self.params[BIAS + j:BIAS + j + 1]
        self.zbuf[slot] = z
        self.h[j] = (z * sigmoid(z)).astype(BF16)
        pltpu.make_async_copy(self.zbuf.at[slot], self.z1.at[:, j * 1024:(j + 1) * 1024], self.zsem.at[slot]).start()

    def project(self, j):
        self.w.wait(4 + j)
        part = dot(self.h[j], self.w.buf[4 + j])
        if j > 0:
            part = self.x1[...] + part
        if j == 3:
            part = self.tokens[...].astype(F32) + 0.5 * (part + self.params[SHIFT + 6:SHIFT + 7])
        self.x1[...] = part

    def mix(self, block, source, shift, out, rows):
        value = dot(source[...], self.w.buf[8 + block])
        if shift is not None:
            value = value + self.params[shift:shift + 1]
        out[rows] = value.astype(BF16)


def front_kernel(blocks, *refs):
    small, *refs = refs
    ws, refs = refs[:8], refs[8:]
    (tokens, full, params, x1, z1, q, k, v, beside, own, slab, slabs, wbuf, a, h, zbuf,
     load, keep, ssend, srecv, wsem, zsem, esem, *sems) = refs
    r, t, c, y, z = place()
    units, R, count = len(blocks), lax.axis_size("rows"), tokens.shape[0]
    copies = []
    for unit, (w, row, col) in enumerate(blocks):
        cp = pltpu.make_async_copy(ws[w].at[row:row + UNIT, col:col + 1024], own.at[unit * UNIT:(unit + 1) * UNIT], load.at[unit])
        cp.start()
        copies.append(cp)
    cs = pltpu.make_async_copy(small, slab, keep)
    cs.start()
    greet([(lax.rem(r + d, R), t) for d in range(1, R)] + [(r, 1 - t)])
    cs.wait()
    for d in range(1, R):
        remote(slab, slabs.at[r], ssend, srecv, lax.rem(r + d, R), t)
    stored = []
    for unit, cp in enumerate(copies):
        cp.wait()
        put = pltpu.make_async_copy(own.at[unit * UNIT:(unit + 1) * UNIT], full.at[r, unit * UNIT:(unit + 1) * UNIT], load.at[unit])
        put.start()
        stored.append(put)
    for put in stored:
        put.wait()
    g = Gather(full, 0, units, sems)
    g.begin()
    landed(slabs.at[0:R - 1], ssend)
    landed(slabs.at[0:R - 1], srecv)
    slabs[r] = slab[...]
    for pair in range(R // 2):
        params[:, pair * 128:(pair + 1) * 128] = (slabs[2 * pair].astype(F32) + slabs[2 * pair + 1].astype(F32))[0:40]
    for s in range(R):
        rows = slabs[s].astype(F32)
        for b in range(2):
            for part in range(2):
                at = 40 + 2 * b + part
                params[BIAS + 4 * b + s // 4:BIAS + 4 * b + s // 4 + 1, (s % 4) * 256 + part * 128:(s % 4) * 256 + (part + 1) * 128] = rows[at:at + 1]
    w = Weights(full, wbuf, wsem, BLOCKS_A)
    f = Front(w, params, tokens, x1, z1, a, h, zbuf, zsem)
    norm_tokens(tokens, params, a)
    mine, other = pl.ds(pl.multiple_of(t * HALO, 128), count), pl.ds(pl.multiple_of((1 - t) * count, 128), HALO)

    def exchange():
        norm_resid(x1, params, a)
        first = pl.multiple_of((1 - t) * (count - HALO), 128)
        remote(a.at[pl.ds(first, HALO)], beside, esem.at[0], esem.at[1], r, 1 - t)

    def receive():
        landed(beside, esem.at[0])
        landed(beside, esem.at[1])
        f.mix(1, beside, None, k, other)

    work = {5: lambda: f.hidden(0), 6: lambda: f.hidden(1), 7: lambda: f.hidden(2), 8: lambda: f.hidden(3),
            12: lambda: (f.project(0), f.project(1)), 13: lambda: (f.project(2), f.project(3), exchange()),
            14: lambda: (w.wait(8, 9), f.mix(0, a, SHIFT + 7, q, slice(None)), f.mix(1, a, None, k, mine)),
            15: lambda: (w.wait(10), f.mix(2, a, SHIFT + 8, v, mine)), 16: receive, 17: lambda: f.mix(2, beside, SHIFT + 8, v, other)}
    for step in range(18):
        g.tick(step)
        unit = step - g.LAG
        if 0 <= unit < 11:
            g.arrived(unit)
            if unit == 7:
                w.start(4, 5, 6, 7)
            elif unit < 4 or unit > 7:
                w.start(unit)
        if step in work:
            work[step]()
    g.run(18, units + g.LAG)
    g.finish()
    for slot in range(2):
        f.stored(slot)


def front(small, weights, tokens, cid):
    count, R, blocks = tokens.shape[0], lax.axis_size("rows"), []
    near = count + HALO
    for i, weight in enumerate(weights):
        n, cols = weight.shape
        blocks += [(i, row, col) for col in range(0, cols, 1024) for row in range(0, n, UNIT)]
    units, sem = len(blocks), pltpu.SemaphoreType.DMA
    return pl.pallas_call(
        functools.partial(front_kernel, tuple(blocks)),
        out_shape=[shape(R, units * UNIT, 1024, dtype=BF16), shape(40, 1024), shape(count, 1024), shape(count, 4096), shape(count, 1024, dtype=BF16),
                   shape(near, 1024, dtype=BF16), shape(near, 1024, dtype=BF16), shape(HALO, 1024, dtype=BF16)],
        in_specs=[anywhere()] * 9 + [whole()], out_specs=[anywhere(), whole(), whole(), anywhere()] + [whole()] * 4,
        scratch_shapes=[pltpu.VMEM((units * UNIT, 1024), BF16), pltpu.VMEM(small.shape, BF16), pltpu.VMEM((R,) + small.shape, BF16),
                        pltpu.VMEM((11, 1024, 1024), BF16), pltpu.VMEM((count, 1024), BF16), pltpu.VMEM((4, count, 1024), BF16), pltpu.VMEM((2, count, 1024), F32),
                        sem((units,)), sem, sem, sem, sem((11,)), sem((2,)), sem((2,))] + Gather.scratch(units),
        compiler_params=pltpu.CompilerParams(vmem_limit_bytes=VMEM_LIMIT, collective_id=cid, has_side_effects=True),
        name="front",
    )(small, *weights, tokens)


def plain_front_kernel(tokens, params, full, x1, z1, q, k, v, wbuf, a, h, zbuf, wsem, zsem):
    w = Weights(full, wbuf, wsem, BLOCKS_A)
    w.start()
    f = Front(w, params, tokens, x1, z1, a, h, zbuf, zsem)
    norm_tokens(tokens, params, a)
    for j in range(4):
        f.hidden(j)
    for j in range(4):
        f.project(j)
    norm_resid(x1, params, a)
    w.wait(8, 9, 10)
    f.mix(0, a, SHIFT + 7, q, slice(None))
    f.mix(1, a, None, k, slice(None))
    f.mix(2, a, SHIFT + 8, v, slice(None))
    for slot in range(2):
        f.stored(slot)


def plain_front(tokens, params, full):
    count = tokens.shape[0]
    return pl.pallas_call(
        plain_front_kernel,
        out_shape=[shape(count, 1024), shape(count, 4096)] + [shape(count, 1024, dtype=BF16)] * 3,
        in_specs=[whole(), whole(), anywhere()], out_specs=[whole(), anywhere(), whole(), whole(), whole()],
        scratch_shapes=[pltpu.VMEM((11, 1024, 1024), BF16), pltpu.VMEM((count, 1024), BF16), pltpu.VMEM((4, count, 1024), BF16), pltpu.VMEM((2, count, 1024), F32),
                        pltpu.SemaphoreType.DMA((11,)), pltpu.SemaphoreType.DMA((2,))],
        compiler_params=pltpu.CompilerParams(vmem_limit_bytes=VMEM_LIMIT),
        name="front",
    )(tokens, params, full)


QB = 128


def strip_of(window, length):
    return pltpu.roll(jnp.broadcast_to(window, (QB, length)), 0, 1, stride=1, stride_axis=0)


def score_block(q, k, strip, base, b, near, segq, segk, scale):
    start = pl.multiple_of(base - b * QB, 128)
    s = dot(q, k, NT) * scale + strip[:, pl.ds(start, near)]
    return jnp.where(segq == segk, s, NEG), start


def attend_kernel(scale, off, q, k, v, window, segq, segk, o, lse, strip):
    near = k.shape[0]
    strip[...] = strip_of(window[0], window.shape[-1])
    base = near + QB - off[0]

    def block(b):
        rows = pl.ds(pl.multiple_of(b * QB, QB), QB)
        s, _ = score_block(q[rows], k[...], strip, base, b, near, segq[rows], segk[...], scale)
        top = jnp.max(s, axis=-1, keepdims=True)
        p = jnp.exp(s - top)
        total = jnp.sum(p, axis=-1, keepdims=True)
        o[rows] = dot(p.astype(BF16), v[...]) / total
        lse[0, rows] = jnp.broadcast_to(top + jnp.log(total), (QB, 128))
    loop(q.shape[0] // QB, block)


def head_block(n):
    return pl.BlockSpec((n, 128), lambda h, off: (0, h))


def attend(q, k, v, windows, segq, segk, off):
    count, near, length = q.shape[0], k.shape[0], windows.shape[-1]
    return pl.pallas_call(
        functools.partial(attend_kernel, 1.0 / math.sqrt(128)),
        out_shape=[shape(count, 1024), shape(HEADS, count, 128)],
        grid_spec=pltpu.PrefetchScalarGridSpec(
            num_scalar_prefetch=1, grid=(HEADS,),
            in_specs=[head_block(count), head_block(near), head_block(near), pl.BlockSpec((1, 1, length), lambda h, off: (h, 0, 0)),
                      pl.BlockSpec((count, 1), lambda h, off: (0, 0)), pl.BlockSpec((1, near), lambda h, off: (0, 0))],
            out_specs=[head_block(count), pl.BlockSpec((1, count, 128), lambda h, off: (h, 0, 0))],
            scratch_shapes=[pltpu.VMEM((QB, length), F32)]),
        compiler_params=pltpu.CompilerParams(vmem_limit_bytes=VMEM_LIMIT),
        name="attend",
    )(off, q, k, v, windows, segq, segk)


def attend_back_kernel(scale, off, q, k, v, window, segq, segk, o, lse, do, dq, dk, dv, dtable, strip, ds, pb, acc):
    near = k.shape[0]
    length = window.shape[-1]
    strip[...] = strip_of(window[0], length)
    acc[...] = jnp.zeros_like(acc)
    base = near + QB - off[0]

    def block(b):
        rows = pl.ds(pl.multiple_of(b * QB, QB), QB)
        s, start = score_block(q[rows], k[...], strip, base, b, near, segq[rows], segk[...], scale)
        p = jnp.exp(s - lse[0, rows, 0:1])
        delta = jnp.sum(do[rows].astype(F32) * o[rows], axis=-1, keepdims=True)
        d = (p * (dot(do[rows], v[...], NT) - delta)).astype(BF16)
        pb[rows] = p.astype(BF16)
        ds[rows] = d
        dq[rows] = (dot(d, k[...]) * scale).astype(BF16)
        acc[:, pl.ds(start, near)] += d.astype(F32)
    loop(q.shape[0] // QB, block)
    dims = (((0,), (0,)), ((), ()))
    dk[...] = (dot(ds[...], q[...], dims) * scale).astype(BF16)
    dv[...] = dot(pb[...], do[...], dims).astype(BF16)
    rows, size = acc[...], QB
    while size > 1:
        size //= 2
        rows = rows[:size] + pltpu.roll(rows[size:], length - size, 1)
    dtable[0] = rows


def attend_back(q, k, v, windows, segq, segk, off, o, lse, do):
    count, near, length = q.shape[0], k.shape[0], windows.shape[-1]
    return pl.pallas_call(
        functools.partial(attend_back_kernel, 1.0 / math.sqrt(128)),
        out_shape=[shape(count, 1024, dtype=BF16), shape(near, 1024, dtype=BF16), shape(near, 1024, dtype=BF16), shape(HEADS, 1, length)],
        grid_spec=pltpu.PrefetchScalarGridSpec(
            num_scalar_prefetch=1, grid=(HEADS,),
            in_specs=[head_block(count), head_block(near), head_block(near), pl.BlockSpec((1, 1, length), lambda h, off: (h, 0, 0)),
                      pl.BlockSpec((count, 1), lambda h, off: (0, 0)), pl.BlockSpec((1, near), lambda h, off: (0, 0)),
                      head_block(count), pl.BlockSpec((1, count, 128), lambda h, off: (h, 0, 0)), head_block(count)],
            out_specs=[head_block(count), head_block(near), head_block(near), pl.BlockSpec((1, 1, length), lambda h, off: (h, 0, 0))],
            scratch_shapes=[pltpu.VMEM((QB, length), F32), pltpu.VMEM((count, near), BF16), pltpu.VMEM((count, near), BF16), pltpu.VMEM((QB, length), F32)]),
        compiler_params=pltpu.CompilerParams(vmem_limit_bytes=VMEM_LIMIT),
        name="attend_back",
    )(off, q, k, v, windows, segq, segk, o, lse, do)


ROWS = 128


BLOCKS_C = ((ATT, "in", 0), (GLU, "in", 0), (GLU, "in", 1))


def convolve_kernel(x1, o, params, seg, full, x2, c1, c2, u, y, sums, wbuf, a, half, send, recv, wsem, esem, ssem, rsem):
    w = Weights(full, wbuf, wsem, BLOCKS_C)
    w.start()
    count = x1.shape[0]
    u[0:8] = jnp.zeros((8, 1024), F32)
    u[count + 8:count + 16] = jnp.zeros((8, 1024), F32)
    greet(cube_peers() + edge_peers())

    def cast(rows):
        a[rows] = o[rows].astype(BF16)
    by_rows(count, 256, cast)
    w.wait(0)

    def project(c):
        x2[:, c] = x1[:, c] + dot(a[...], wbuf[0, :, c]) + params[SHIFT + 9:SHIFT + 10, c]
    by_cols(1024, project)

    def norm(rows):
        vhat, _ = normalized(x2[rows])
        a[rows] = (vhat * params[GAIN + 2:GAIN + 3] + params[SHIFT + 2:SHIFT + 3]).astype(BF16)
    by_rows(count, 256, norm)
    w.wait(1, 2)

    def gate(c):
        value = dot(a[...], wbuf[1, :, c]) + params[SHIFT + 10:SHIFT + 11, c]
        other = dot(a[...], wbuf[2, :, c]) + params[SHIFT + 11:SHIFT + 12, c]
        c1[:, c] = value
        c2[:, c] = other
        u[8:count + 8, c] = (value * sigmoid(other)).astype(BF16).astype(F32)
    by_cols(1024, gate)
    swap_edges(u, count, esem)
    half[...] = jnp.zeros_like(half)

    def taps(i):
        first = pl.multiple_of(i * ROWS, ROWS)
        here = seg[pl.ds(first + 8, ROWS)]
        total = jnp.zeros((ROWS, 1024), F32)
        block = u[pl.ds(first, ROWS + 16)]
        segs = seg[pl.ds(first, ROWS + 16)]
        for tap in range(KSIZE):
            k = slice(6 + tap, 6 + tap + ROWS)
            total = total + params[TAPS + tap:TAPS + tap + 1] * jnp.where(segs[k] == here, block[k], 0.0)
        y[pl.ds(first, ROWS)] = total
        half[0:8] += eight(total)
        half[8:16] += eight(total * total)
    loop(count // ROWS, taps)
    fold(half, send)
    steps = add_all(send, recv, ssem, rsem)
    sums[...] = send[steps]


def fold(half, send):
    send[0, 0:1] = jnp.sum(half[0:8], axis=0, keepdims=True)
    send[0, 1:2] = jnp.sum(half[8:16], axis=0, keepdims=True)


def reduce_scratch(rows=2):
    steps = (lax.axis_size("rows").bit_length() - 1) + (lax.axis_size("tm").bit_length() - 1)
    return [pltpu.VMEM((steps + 1, rows, 1024), F32), pltpu.VMEM((steps, rows, 1024), F32)], [pltpu.SemaphoreType.DMA((steps,)), pltpu.SemaphoreType.DMA((steps,))]


def convolve(x1, o, params, seg, full, cid):
    count = x1.shape[0]
    bufs, sems = reduce_scratch()
    return pl.pallas_call(
        convolve_kernel,
        out_shape=[shape(count, 1024), shape(count, 1024), shape(count, 1024), shape(count + 16, 1024), shape(count, 1024), shape(2, 1024)],
        in_specs=[whole()] * 4 + [anywhere()], out_specs=[whole()] * 6,
        scratch_shapes=[pltpu.VMEM((3, 1024, 1024), BF16), pltpu.VMEM((count, 1024), BF16), pltpu.VMEM((16, 1024), F32)] + bufs + [pltpu.SemaphoreType.DMA((3,)), pltpu.SemaphoreType.DMA((4,))] + sems,
        compiler_params=pltpu.CompilerParams(vmem_limit_bytes=VMEM_LIMIT, collective_id=cid, has_side_effects=True),
        name="convolve",
    )(x1, o, params, seg, full)


def batch_stats(sums, frames):
    mean = sums[0:1] / frames
    square = sums[1:2] / frames
    return mean, lax.rsqrt(square - mean * mean + EPS)


BLOCKS_D = tuple([(CONV, "in", 0)] + [(FI2, "in", j) for j in range(4)] + [(FO2, "out", j) for j in range(4)])


def middle_kernel(frames, x2, y, sums, cot, params, full, out, g3, dn, totals, small, grads,
                  wbuf, a, e, d, dz, h, z, stage, half, send, recv, wsem, gsem, ssem, rsem):
    w = Weights(full, wbuf, wsem, BLOCKS_D)
    w.start()
    greet(cube_peers())
    g = Grads(grads, stage, gsem)
    count = x2.shape[0]
    mean, inverse = batch_stats(sums, frames)
    small[...] = jnp.zeros_like(small)
    half[...] = jnp.zeros_like(half)

    def active(rows):
        n = (y[rows] - mean) * inverse * params[GAIN + 5:GAIN + 6] + params[SHIFT + 5:SHIFT + 6]
        e[rows] = (n * sigmoid(n)).astype(BF16)
    by_rows(count, 256, active)
    w.wait(0)
    x3 = g3

    def project(c):
        x3[:, c] = x2[:, c] + dot(e[...], wbuf[0, :, c]) + params[SHIFT + 12:SHIFT + 13, c]
    by_cols(1024, project)

    def norm(rows):
        vhat, _ = normalized(x3[rows])
        a[rows] = (vhat * params[GAIN + 3:GAIN + 4] + params[SHIFT + 3:SHIFT + 4]).astype(BF16)
    by_rows(count, 256, norm)
    for j in range(4):
        w.wait(1 + j)

    def hidden(j):
        def cols(c):
            v = dot(a[...], wbuf[1 + j, :, c]) + params[pl.ds(BIAS + 4 + j, 1), c]
            z[j, :, c] = v
            h[j, :, c] = (v * sigmoid(v)).astype(BF16)
        by_cols(1024, cols)
    loop(4, hidden)
    w.wait(5, 6, 7, 8)

    def outward(c):
        acc = dot(h[0], wbuf[5, :, c])
        for j in range(1, 4):
            acc = acc + dot(h[j], wbuf[5 + j, :, c])
        out[:, c] = x3[:, c] + 0.5 * (acc + params[SHIFT + 13:SHIFT + 14, c])
    by_cols(1024, outward)

    def last(rows):
        vhat, rs = normalized(out[rows])
        gain = params[GAIN + 4:GAIN + 5]
        out[rows] = vhat * gain + params[SHIFT + 4:SHIFT + 5]
        ct = cot[rows]
        small[0:8] += eight(ct * vhat)
        small[8:16] += eight(ct)
        g4 = norm_back(ct, gain, vhat, rs)
        dn[rows] = g4
        half = (0.5 * g4).astype(BF16)
        d[rows] = half
        small[16:24] += eight(half.astype(F32))
    by_rows(count, 256, last)

    def back(j):
        def cols(c):
            v = z[j, :, c]
            s = sigmoid(v)
            dh = dot(d[...], wbuf[5 + j, c, :], NT) * (s * (1.0 + v * (1.0 - s)))
            dh = dh.astype(BF16)
            dz[j, :, c] = dh
            small[pl.ds(pl.multiple_of(24 + 8 * j, 8), 8), c] += eight(dh.astype(F32))
        by_cols(1024, cols)
    loop(4, back)
    for j in range(4):
        g.put(FO2, "out", j, h[j], lambda c: d[:, c])
    for j in range(4):
        g.put(FI2, "in", j, a[...], lambda c, j=j: dz[j, :, c])
    da = z.at[0]

    def inward(c):
        acc = dot(dz[0], wbuf[1, c, :], NT)
        for j in range(1, 4):
            acc = acc + dot(dz[j], wbuf[1 + j, c, :], NT)
        da[:, c] = acc
    by_cols(1024, inward)

    def resid(rows):
        vhat, rs = normalized(x3[rows])
        w3 = da[rows]
        small[56:64] += eight(w3 * vhat)
        small[64:72] += eight(w3)
        total = dn[rows] + norm_back(w3, params[GAIN + 3:GAIN + 4], vhat, rs)
        g3[rows] = total
        de = total.astype(BF16)
        d[rows] = de
        small[72:80] += eight(de.astype(F32))
    by_rows(count, 256, resid)
    g.put(CONV, "in", 0, e[...], lambda c: d[:, c])

    def dnorm(c):
        dn[:, c] = dot(d[...], wbuf[0, c, :], NT)
    by_cols(1024, dnorm)

    def finish(rows):
        yhat = (y[rows] - mean) * inverse
        n = yhat * params[GAIN + 5:GAIN + 6] + params[SHIFT + 5:SHIFT + 6]
        s = sigmoid(n)
        v = dn[rows] * (s * (1.0 + n * (1.0 - s)))
        dn[rows] = v
        half[0:8] += eight(v * yhat)
        half[8:16] += eight(v)
    by_rows(count, 256, finish)
    small[80:96] = half[...]
    fold(half, send)
    steps = add_all(send, recv, ssem, rsem)
    totals[...] = send[steps]
    g.finish()


def middle(x2, y, sums, cot, params, full, frames, cid):
    count = x2.shape[0]
    bufs, sems = reduce_scratch()
    return pl.pallas_call(
        functools.partial(middle_kernel, frames),
        out_shape=[shape(count, 1024), shape(count, 1024), shape(count, 1024), shape(2, 1024), shape(96, 1024), shape(*full.shape, dtype=BF16)],
        in_specs=[whole()] * 5 + [anywhere()], out_specs=[whole()] * 5 + [anywhere()],
        scratch_shapes=[pltpu.VMEM((9, 1024, 1024), BF16), pltpu.VMEM((count, 1024), BF16), pltpu.VMEM((count, 1024), BF16), pltpu.VMEM((count, 1024), BF16),
                        pltpu.VMEM((4, count, 1024), BF16), pltpu.VMEM((4, count, 1024), BF16), pltpu.VMEM((4, count, 1024), F32),
                        pltpu.VMEM((2, 1024, 1024), BF16), pltpu.VMEM((16, 1024), F32)] + bufs + [pltpu.SemaphoreType.DMA((9,)), pltpu.SemaphoreType.DMA((2,))] + sems,
        compiler_params=pltpu.CompilerParams(vmem_limit_bytes=VMEM_LIMIT, collective_id=cid, has_side_effects=True),
        name="middle",
    )(x2, y, sums, cot, params, full)


def convolve_back_kernel(frames, dn, y, sums, totals, c1, c2, u, x2, g3, o, params, seg, full, grads_in, g2, dob, small, grads,
                         wbuf, a, d, dc, pad, stage, wsem, gsem, esem):
    w = Weights(full, wbuf, wsem, BLOCKS_C)
    w.start()
    count = x2.shape[0]
    pad[0:8] = jnp.zeros((8, 1024), F32)
    pad[count + 8:count + 16] = jnp.zeros((8, 1024), F32)
    greet(edge_peers())
    g = Grads(grads, stage, gsem)
    mean, inverse = batch_stats(sums, frames)
    gain = params[GAIN + 5:GAIN + 6]
    product = totals[0:1] * gain / frames
    total = totals[1:2] * gain / frames
    small[...] = jnp.zeros_like(small)

    def dy(i):
        rows = pl.ds(pl.multiple_of(i * ROWS, ROWS), ROWS)
        yhat = (y[rows] - mean) * inverse
        v = inverse * (dn[rows] * gain - total - yhat * product)
        pad[pl.ds(pl.multiple_of(i * ROWS + 8, 8), ROWS)] = v.astype(BF16).astype(F32)
        vhat, _ = normalized(x2[rows])
        a[rows] = (vhat * params[GAIN + 2:GAIN + 3] + params[SHIFT + 2:SHIFT + 3]).astype(BF16)
    loop(count // ROWS, dy)
    swap_edges(pad, count, esem)

    def taps(i):
        first = pl.multiple_of(i * ROWS, ROWS)
        rows = pl.ds(first, ROWS)
        block, grad, segs = u[pl.ds(first, ROWS + 16)], pad[pl.ds(first, ROWS + 16)], seg[pl.ds(first, ROWS + 16)]
        here, own = segs[8:ROWS + 8], grad[8:ROWS + 8]
        du = jnp.zeros((ROWS, 1024), F32)
        for tap in range(KSIZE):
            k = slice(6 + tap, 6 + tap + ROWS)
            small[8 * tap:8 * tap + 8] += eight(own * jnp.where(segs[k] == here, block[k], 0.0))
            b = slice(10 - tap, 10 - tap + ROWS)
            du = du + params[TAPS + tap:TAPS + tap + 1] * jnp.where(segs[b] == here, grad[b], 0.0)
        s = sigmoid(c2[rows])
        left = (du * s).astype(BF16)
        right = (du * c1[rows] * s * (1.0 - s)).astype(BF16)
        dc[0, rows] = left
        dc[1, rows] = right
        small[40:48] += eight(left.astype(F32))
        small[48:56] += eight(right.astype(F32))
    loop(count // ROWS, taps)
    w.wait(0, 1, 2)
    da = pad.at[0:count]

    def inward(c):
        da[:, c] = dot(dc[0], wbuf[1, c, :], NT) + dot(dc[1], wbuf[2, c, :], NT)
    by_cols(1024, inward)

    def resid(rows):
        vhat, rs = normalized(x2[rows])
        v = da[rows]
        small[56:64] += eight(v * vhat)
        small[64:72] += eight(v)
        both = g3[rows] + norm_back(v, params[GAIN + 2:GAIN + 3], vhat, rs)
        g2[rows] = both
        dx = both.astype(BF16)
        d[rows] = dx
        small[72:80] += eight(dx.astype(F32))
    by_rows(count, 256, resid)

    def attended(c):
        dob[:, c] = dot(d[...], wbuf[0, c, :], NT).astype(BF16)
    by_cols(1024, attended)
    for j in range(2):
        g.put(GLU, "in", j, a[...], lambda c, j=j: dc[j, :, c])

    def cast(rows):
        a[rows] = o[rows].astype(BF16)
    by_rows(count, 256, cast)
    g.put(ATT, "in", 0, a[...], lambda c: d[:, c])
    g.finish()


def convolve_back(dn, y, sums, totals, c1, c2, u, x2, g3, o, params, seg, full, grads, frames, cid):
    count = x2.shape[0]
    return pl.pallas_call(
        functools.partial(convolve_back_kernel, frames),
        out_shape=[shape(count, 1024), shape(count, 1024, dtype=BF16), shape(80, 1024), shape(*full.shape, dtype=BF16)],
        in_specs=[whole()] * 12 + [anywhere()] * 2, out_specs=[whole()] * 3 + [anywhere()],
        scratch_shapes=[pltpu.VMEM((3, 1024, 1024), BF16), pltpu.VMEM((count, 1024), BF16), pltpu.VMEM((count, 1024), BF16), pltpu.VMEM((2, count, 1024), BF16),
                        pltpu.VMEM((count + 16, 1024), F32), pltpu.VMEM((2, 1024, 1024), BF16),
                        pltpu.SemaphoreType.DMA((3,)), pltpu.SemaphoreType.DMA((2,)), pltpu.SemaphoreType.DMA((4,))],
        input_output_aliases={13: 3},
        compiler_params=pltpu.CompilerParams(vmem_limit_bytes=VMEM_LIMIT, collective_id=cid, has_side_effects=True),
        name="convolve_back",
    )(dn, y, sums, totals, c1, c2, u, x2, g3, o, params, seg, full, grads)


BLOCKS_E = tuple([(QKV, "in", j) for j in range(3)] + [(FO1, "out", j) for j in range(4)] + [(FI1, "in", j) for j in range(4)])


def rear_kernel(halo, tokens, x1, z1, g2, dq, dk, dv, params, full, *refs):
    if halo:
        beside, grads_in, dtok, small, grads, wbuf, a, d, dz, zbuf, hbuf, stage, da, back, got, wsem, zsem, gsem, esem = refs
    else:
        grads_in, dtok, small, grads, wbuf, a, d, dz, zbuf, hbuf, stage, da, wsem, zsem, gsem = refs
    w = Weights(full, wbuf, wsem, BLOCKS_E)
    w.start()
    g = Grads(grads, stage, gsem)
    count = tokens.shape[0]
    for j in range(2):
        pltpu.make_async_copy(z1.at[:, j * 1024:(j + 1) * 1024], zbuf.at[j], zsem.at[j]).start()
    small[...] = jnp.zeros_like(small)
    own = 0
    if halo:
        r, t = lax.axis_index("rows"), lax.axis_index("tm")
        greet([(r, 1 - t)])
        own, other = pl.multiple_of(t * HALO, 128), pl.multiple_of((1 - t) * count, 128)
        w.wait(1, 2)

        def outside(c):
            back[:, c] = (dot(dk[pl.ds(other, HALO)], wbuf[1, c, :], NT) + dot(dv[pl.ds(other, HALO)], wbuf[2, c, :], NT)).astype(BF16)
        by_cols(1024, outside)
        remote(back, got, esem.at[0], esem.at[1], r, 1 - t)
        w.wait(0)
    else:
        w.wait(0, 1, 2)
    mine = pl.ds(own, count)

    def inside(c):
        da[:, c] = dot(dq[...], wbuf[0, c, :], NT) + dot(dk[mine], wbuf[1, c, :], NT) + dot(dv[mine], wbuf[2, c, :], NT)
    by_cols(1024, inside)

    def norm(rows):
        vhat, _ = normalized(x1[rows])
        a[rows] = (vhat * params[GAIN + 1:GAIN + 2] + params[SHIFT + 1:SHIFT + 2]).astype(BF16)
        small[0:8] += eight(dq[rows].astype(F32))
    by_rows(count, 256, norm)

    def values(rows):
        small[8:16] += eight(dv[rows].astype(F32))
    by_rows(dv.shape[0], 128, values)
    g.put(QKV, "in", 0, a[...], lambda c: dq[:, c])
    if halo:
        for j, grad in ((1, dk), (2, dv)):
            slot = g.count % 2
            buf, n, R = stage.at[slot], g.n, g.R
            if g.count >= 2:
                g.wait(slot)

            def cols(c, grad=grad, buf=buf):
                buf[:, c] = (dot(a[...], grad[mine, c], TN) + dot(beside[...], grad[pl.ds(other, HALO), c], TN)).astype(BF16)
            by_cols(1024, cols)
            for s in range(R):
                pltpu.make_async_copy(buf.at[s * n:(s + 1) * n], grads.at[s, (QKV + j) * n:(QKV + j + 1) * n], gsem.at[slot]).start()
            g.count += 1
        landed(back, esem.at[0])
        landed(got, esem.at[1])
        first = pl.multiple_of((1 - t) * (count - HALO), 128)

        def merge(i):
            rows = pl.ds(pl.multiple_of(first + i * 64, 64), 64)
            da[rows] += got[pl.ds(pl.multiple_of(i * 64, 64), 64)].astype(F32)
        loop(HALO // 64, merge)
    else:
        g.put(QKV, "in", 1, a[...], lambda c: dk[:, c])
        g.put(QKV, "in", 2, a[...], lambda c: dv[:, c])

    def resid(rows):
        vhat, rs = normalized(x1[rows])
        v = da[rows]
        small[16:24] += eight(v * vhat)
        small[24:32] += eight(v)
        both = g2[rows] + norm_back(v, params[GAIN + 1:GAIN + 2], vhat, rs)
        dtok[rows] = both
        half = (0.5 * both).astype(BF16)
        d[rows] = half
        small[32:40] += eight(half.astype(F32))
        vhat, _ = normalized(tokens[rows].astype(F32))
        a[rows] = (vhat * params[GAIN:GAIN + 1] + params[SHIFT:SHIFT + 1]).astype(BF16)
    by_rows(count, 256, resid)
    w.wait(3, 4, 5, 6)
    for j in range(4):
        slot = j % 2
        pltpu.make_async_copy(zbuf.at[slot], zbuf.at[slot], zsem.at[slot]).wait()

        def cols(c, j=j, slot=slot):
            v = zbuf[slot, :, c]
            s = sigmoid(v)
            hbuf[:, c] = (v * s).astype(BF16)
            dh = (dot(d[...], wbuf[3 + j, c, :], NT) * (s * (1.0 + v * (1.0 - s)))).astype(BF16)
            dz[j, :, c] = dh
            small[40 + 8 * j:48 + 8 * j, c] += eight(dh.astype(F32))
        by_cols(1024, cols)
        if j + 2 < 4:
            pltpu.make_async_copy(z1.at[:, (j + 2) * 1024:(j + 3) * 1024], zbuf.at[slot], zsem.at[slot]).start()
        g.put(FO1, "out", j, hbuf[...], lambda c: d[:, c])
    for j in range(4):
        g.put(FI1, "in", j, a[...], lambda c, j=j: dz[j, :, c])
    w.wait(7, 8, 9, 10)

    def inward(c):
        acc = dot(dz[0], wbuf[7, c, :], NT)
        for j in range(1, 4):
            acc = acc + dot(dz[j], wbuf[7 + j, c, :], NT)
        da[:, c] = acc
    by_cols(1024, inward)

    def last(rows):
        vhat, rs = normalized(tokens[rows].astype(F32))
        v = da[rows]
        small[72:80] += eight(v * vhat)
        small[80:88] += eight(v)
        dtok[rows] = dtok[rows] + norm_back(v, params[GAIN:GAIN + 1], vhat, rs)
    by_rows(count, 256, last)
    g.finish()


def rear(tokens, x1, z1, g2, dq, dk, dv, params, full, beside, grads, cid):
    count = tokens.shape[0]
    halo = beside is not None
    scratch = [pltpu.VMEM((11, 1024, 1024), BF16), pltpu.VMEM((count, 1024), BF16), pltpu.VMEM((count, 1024), BF16), pltpu.VMEM((4, count, 1024), BF16),
               pltpu.VMEM((2, count, 1024), F32), pltpu.VMEM((count, 1024), BF16), pltpu.VMEM((2, 1024, 1024), BF16), pltpu.VMEM((count, 1024), F32)]
    if halo:
        scratch += [pltpu.VMEM((HALO, 1024), BF16), pltpu.VMEM((HALO, 1024), BF16)]
    scratch += [pltpu.SemaphoreType.DMA((11,)), pltpu.SemaphoreType.DMA((2,)), pltpu.SemaphoreType.DMA((2,))]
    if halo:
        scratch.append(pltpu.SemaphoreType.DMA((2,)))
    specs = [whole(), whole(), anywhere()] + [whole()] * 5 + [anywhere()] + ([whole()] if halo else []) + [anywhere()]
    return pl.pallas_call(
        functools.partial(rear_kernel, halo),
        out_shape=[shape(count, 1024), shape(88, 1024), shape(*full.shape, dtype=BF16)],
        in_specs=specs, out_specs=[whole(), whole(), anywhere()], scratch_shapes=scratch,
        input_output_aliases={len(specs) - 1: 2},
        compiler_params=pltpu.CompilerParams(vmem_limit_bytes=VMEM_LIMIT, **({"collective_id": cid, "has_side_effects": True} if halo else {})),
        name="rear",
    )(tokens, x1, z1, g2, dq, dk, dv, params, full, *((beside,) if halo else ()), grads)


def pack_rows(gains, shifts, ffn_bias, conv_kernel, rel_table):
    n = rel_table.shape[0]
    rows = jnp.concatenate([gains, shifts, ffn_bias.reshape(2 * 4, n), conv_kernel, rel_table[None]], axis=0).reshape(-1)
    return jnp.pad(rows, (0, 8 * 384 - rows.shape[0])).reshape(8, 384)


def slab_rows(gains, shifts, ffn_bias, conv_kernel, rel_table):
    rows = jnp.concatenate([gains, shifts, jnp.zeros((8, 64), BF16), conv_kernel, rel_table[None], jnp.zeros((6, 64), BF16)], axis=0)
    zero = jnp.zeros_like(rows)
    odd = lax.rem(lax.axis_index("rows"), 2) == 1
    wide = jnp.concatenate([jnp.where(odd, zero, rows), jnp.where(odd, rows, zero)], axis=1)
    return jnp.concatenate([wide, ffn_bias.reshape(4, 128), jnp.zeros((4, 128), BF16)], axis=0)


def wide_rows(smalls):
    R = smalls.shape[0]
    n = 1024 // R
    rows = smalls.reshape(R, -1)[:, : 34 * n].reshape(R, 34, n).astype(F32)
    flat = rows.transpose(1, 0, 2).reshape(34, 1024)
    bias = rows[:, 20:28].reshape(R, 2, 4 * n).transpose(1, 0, 2).reshape(8, 1024)
    return jnp.concatenate([flat[:20], bias, flat[28:], jnp.zeros((6, 1024), F32)], axis=0)


def slot_rows(rows, R):
    n = 1024 // R
    flat = rows.reshape(34, R, n).transpose(1, 0, 2)
    bias = rows[20:28].reshape(2, R, 4, n).transpose(1, 0, 2, 3).reshape(R, 8, n)
    flat = jnp.concatenate([flat[:, :20], bias, flat[:, 28:]], axis=1).reshape(R, 34 * n)
    return jnp.pad(flat, ((0, 0), (0, 8 * 384 - 34 * n))).reshape(R, 8, 384)


def shard_rows(small, R):
    n = 1024 // R
    rows = small.reshape(-1)[: 34 * n].reshape(34, n)
    return (rows[:6], rows[6:20], rows[20:28].reshape(2, 4 * n), rows[28:33], rows[33])


def pack_weights(weights):
    blocks = []
    for w in weights:
        rows, cols = w.shape
        blocks.append(w.reshape(rows, cols // 1024, 1024).transpose(1, 0, 2).reshape(-1, 1024))
    return jnp.concatenate(blocks, axis=0)


def unpack_shard(shard, weights):
    out, row = [], 0
    for w in weights:
        n, cols = w.shape
        count = n * cols // 1024
        out.append(shard[row : row + count].reshape(cols // 1024, n, 1024).transpose(1, 0, 2).reshape(n, cols))
        row += count
    return tuple(out)


def body(tokens, cotangent, segment_ids, rel_bucket, ffn1_in, ffn1_out, qkv_weight, attn_out, glu_in, conv_out, ffn2_in, ffn2_out,
         gains, shifts, ffn_bias, conv_kernel, rel_table):
    packed_rows, count, width = tokens.shape
    R, T = lax.axis_size("rows"), lax.axis_size("tm")
    t = lax.axis_index("tm")
    links = R == 16 and T == 2 and count == 512
    frames = R * T * count * packed_rows
    weights = (ffn1_in, ffn1_out, qkv_weight, attn_out, glu_in, conv_out, ffn2_in, ffn2_out)
    tok = tokens.reshape(count, width)
    if links:
        full, params, x1, z1, q, k, v, beside = front(slab_rows(gains, shifts, ffn_bias, conv_kernel, rel_table), weights, tok, 0)
    else:
        full = lax.all_gather(pack_weights(weights), "rows", axis=0)
        params = wide_rows(lax.all_gather(pack_rows(gains, shifts, ffn_bias, conv_kernel, rel_table), "rows", axis=0))

    seg_all = lax.all_gather(segment_ids, "tm", axis=1, tiled=True)[0]
    seg_far = jnp.pad(seg_all, (HALO, HALO), constant_values=-1)
    segx = lax.dynamic_slice_in_dim(seg_far, HALO + t * count - 8, count + 16)[:, None]
    segq = segment_ids.reshape(count, 1)
    if links:
        near, off = count + HALO, t * HALO
        segk = lax.dynamic_slice_in_dim(seg_all, t * (count - HALO), near)[None]
    else:
        near, off = T * count, t * count
        segk = seg_all[None]
    length = 2 * near + QB
    places = np.clip(np.arange(length) - (near + QB), -MAXD, MAXD) + MAXD
    before, after = int(np.argmax(places > 0)), int(np.argmax(places >= 2 * MAXD))
    buckets = jnp.concatenate([jnp.broadcast_to(rel_bucket[:1], (before,)), rel_bucket[1 : 2 * MAXD], jnp.broadcast_to(rel_bucket[2 * MAXD :], (length - after,))])
    hot = (buckets[None, :] == jnp.arange(NB, dtype=jnp.int32)[:, None]).astype(F32)
    windows = jnp.dot(params[REL].reshape(HEADS, NB), hot, precision=HIGH).reshape(HEADS, 1, length)
    off = off.astype(jnp.int32).reshape(1)

    if not links:
        x1, z1, q, k, v = plain_front(tok, params, full)
        beside = None
        k = lax.all_gather(k, "tm", axis=0, tiled=True)
        v = lax.all_gather(v, "tm", axis=0, tiled=True)
    o, lse = attend(q, k, v, windows, segq, segk, off)
    x2, c1, c2, u, y, sums = convolve(x1, o, params, segx, full, 3)
    output, g3, dn, totals, small_d, grads = middle(x2, y, sums, cotangent.reshape(count, width), params, full, frames, 4)
    g2, dob, small_c, grads = convolve_back(dn, y, sums, totals, c1, c2, u, x2, g3, o, params, segx, full, grads, frames, 5)
    dq, dk, dv, dtable = attend_back(q, k, v, windows, segq, segk, off, o, lse, dob)
    if not links:
        dk = lax.psum_scatter(dk, "tm", scatter_dimension=0, tiled=True)
        dv = lax.psum_scatter(dv, "tm", scatter_dimension=0, tiled=True)
    dtok, small_e, grads = rear(tok, x1, z1, g2, dq, dk, dv, params, full, beside, grads, 6)

    rel = lax.dot_general(dtable.reshape(HEADS, length), hot, (((1,), (1,)), ((), ())), precision=HIGH).reshape(1, 1024)
    d = jnp.sum(small_d.reshape(12, 8, 1024), axis=1)
    c = jnp.sum(small_c.reshape(10, 8, 1024), axis=1)
    e = jnp.sum(small_e.reshape(11, 8, 1024), axis=1)
    rows = jnp.concatenate([
        e[9:10], e[2:3], c[7:8], d[7:8], d[0:1], d[10:11],
        e[10:11], e[3:4], c[8:9], d[8:9], d[1:2], d[11:12], e[4:5], e[0:2], c[9:10], c[5:7], d[9:10], d[2:3],
        e[5:9], d[3:7], c[0:5], rel])
    if links:
        shard, small = scatter_call(grads, slot_rows(rows, R), 1)
    else:
        shard = lax.psum(lax.psum_scatter(grads, "rows", scatter_dimension=0, tiled=False), "tm").astype(F32)
        small = lax.psum(lax.psum_scatter(slot_rows(rows, R), "rows", scatter_dimension=0, tiled=False), "tm")
    return (output.reshape(tokens.shape), dtok.reshape(tokens.shape)) + unpack_shard(shard, weights) + shard_rows(small, R)


def solution(mesh):
    return jax.shard_map(
        body,
        mesh=mesh,
        in_specs=(
            P("rows", "tm", None),
            P("rows", "tm", None),
            P("rows", "tm"),
            P(),
            P("rows", None),
            P("rows", None),
            P("rows", None),
            P("rows", None),
            P("rows", None),
            P("rows", None),
            P("rows", None),
            P("rows", None),
            P(None, "rows"),
            P(None, "rows"),
            P(None, "rows"),
            P(None, "rows"),
            P("rows"),
        ),
        out_specs=(
            P("rows", "tm", None),
            P("rows", "tm", None),
            P("rows", None),
            P("rows", None),
            P("rows", None),
            P("rows", None),
            P("rows", None),
            P("rows", None),
            P("rows", None),
            P("rows", None),
            P(None, "rows"),
            P(None, "rows"),
            P(None, "rows"),
            P(None, "rows"),
            P("rows"),
        ),
        check_vma=False,
    )
```

profile of v0, /device:TPU:0, one launch (start us, length us, event | category | flops | bytes accessed | tf_op | source)
XLA Modules:
  0.0 727.5 jit_solution(10662777808030915541)
XLA Ops:
  0.7 0.7 reshape.157
  1.4 1.3 fusion.8
  2.7 0.8 slice.149
  3.5 0.6 broadcast_in_dim.43
  4.1 5.4 all_gather.3
  10.2 0.6 broadcast_in_dim.41
  10.9 0.7 concatenate.71
  11.6 3.0 concatenate.68
  14.6 0.7 maximum_maximum_fusion.refs_0_
  15.3 1.5 copy.40.segq
  16.8 0.8 broadcast_in_dim.45.seg
  17.7 211.1 %front.1 = (bf16[16,1472,1024]{2,1,0:T(8,128)(2,1)}, f32[40,1024]{1,0:T(8,128)}, f32[512,1024]{1,0:T(8,128)}, f32[512,4096]{1,0:T(8,128)}, bf16[512,1024]{1,0:T(...) custom-call(bf16[48,128]{1,0:T(8,128)(2,1)} %maximum_maximum_fusion.refs_0_, ...), custom_call_target="tpu_custom_call" | custom-call | tf_op jit(solution)/shard_map/front/pallas_call | solution.py:712
  228.8 0.8 slice.147
  229.6 1.1 fusion.1
  230.7 0.7 reshape.160.window
  231.3 21.5 %attend.1 = (f32[512,1024]{1,0:T(8,128)}, f32[8,512,128]{2,1,0:T(8,128)}) custom-call(s32[1]{0:T(128)} %bitcast.2.off, bf16[512,1024]{1,0:T(8,128)(2,1)} %get-tuple-element.51.q, bf16[896,1024]{1,0:T(8,128)(2,1)} %get-tuple-element.52.k, bf16[896,1024]{1,0:T(8,128)(2,1)} %get-tuple-element.53.v, f32[8,1,1920]{2,1,0:T(1,128)} %reshape.160.window, ...), custom_call_target="tpu_custom_call" | custom-call | tf_op jit(solution)/shard_map/attend/pallas_call | solution.py:791
  252.8 30.7 %convolve.1 = (f32[512,1024]{1,0:T(8,128)}, f32[512,1024]{1,0:T(8,128)}, f32[512,1024]{1,0:T(8,128)}, f32[528,1024]{1,0:T(8,128)}, f32[512,1024]{1,0:T(8,128)}, /*index=5*/f32[2,1024]{1,0:T(2,128)}) custom-call(f32[512,1024]{1,0:T(8,128)} %get-tuple-element.50.x1, f32[512,1024]{1,0:T(8,128)} %get-tuple-element.55.o, f32[40,1024]{1,0:T(8,128)} %get-tuple-element.54.params, ...), custom_call_target="tpu_custom_call" | custom-call | tf_op jit(solution)/shard_map/convolve/pallas_call | solution.py:920
  283.5 62.3 %middle.1 = (f32[512,1024]{1,0:T(8,128)}, f32[512,1024]{1,0:T(8,128)}, f32[512,1024]{1,0:T(8,128)}, f32[2,1024]{1,0:T(2,128)}, f32[96,1024]{1,0:T(8,128)}, /*index=5*/bf16[16,1472,1024]{2,1,0:T(8,128)(2,1)}) custom-call(f32[512,1024]{1,0:T(8,128)} %get-tuple-element.57.x2, f32[512,1024]{1,0:T(8,128)} %get-tuple-element.58.y, ...), custom_call_target="tpu_custom_call" | custom-call | tf_op jit(solution)/shard_map/middle/pallas_call | solution.py:1057
  345.8 1.1 bitcast_reduce_fusion
  347.0 0.6 copy-done.2
  348.2 0.7 concatenate.91
  348.9 33.4 %convolve_back.1 = (f32[512,1024]{1,0:T(8,128)}, bf16[512,1024]{1,0:T(8,128)(2,1)}, f32[80,1024]{1,0:T(8,128)}, bf16[16,1472,1024]{2,1,0:T(8,128)(2,1)}) custom-call(f32[512,1024]{1,0:T(8,128)} %get-tuple-element.62.dn, f32[512,1024]{1,0:T(8,128)} %get-tuple-element.58.y, f32[2,1024]{1,0:T(2,128)} %get-tuple-element.59.sums, ...), custom_call_target="tpu_custom_call", output_to_operand_aliasing={{3}: (13, {})} | custom-call | tf_op jit(solution)/shard_map/convolve_back/pallas_call | solution.py:1147
  382.3 30.6 %attend_back.1 = (bf16[512,1024]{1,0:T(8,128)(2,1)}, bf16[896,1024]{1,0:T(8,128)(2,1)}, bf16[896,1024]{1,0:T(8,128)(2,1)}, f32[8,1,1920]{2,1,0:T(1,128)}) custom-call(s32[1]{0:T(128)} %bitcast.2.off, bf16[512,1024]{1,0:T(8,128)(2,1)} %get-tuple-element.51.q, bf16[896,1024]{1,0:T(8,128)(2,1)} %get-tuple-element.52.k, bf16[896,1024]{1,0:T(8,128)(2,1)} %get-tuple-element.53.v, ...), custom_call_target="tpu_custom_call" | custom-call | tf_op jit(solution)/shard_map/attend_back/pallas_call | solution.py:835
  412.9 2.0 fusion
  414.9 52.4 %rear.1 = (f32[512,1024]{1,0:T(8,128)}, f32[88,1024]{1,0:T(8,128)}, bf16[16,1472,1024]{2,1,0:T(8,128)(2,1)}) custom-call(bf16[512,1024]{1,0:T(8,128)(2,1)} %bitcast.49, f32[512,1024]{1,0:T(8,128)} %get-tuple-element.50.x1, f32[512,4096]{1,0:T(8,128)} %get-tuple-element.61.z1, f32[512,1024]{1,0:T(8,128)} %get-tuple-element.69.g2, ...), custom_call_target="tpu_custom_call", output_to_operand_aliasing={{2}: (10, {})} | custom-call | tf_op jit(solution)/shard_map/rear/pallas_call | solution.py:1291
  467.3 0.8 concatenate.93
  468.0 1.1 bitcast_reduce_fusion.1
  469.6 0.7 pad_maximum_fusion.1
  470.5 1.1 bitcast_reduce_fusion.2
  471.6 1.1 slice_reduce_fusion
  474.1 0.7 copy.54
  474.9 229.7 %scatter_grads.1 = (f32[1472,1024]{1,0:T(8,128)}, f32[8,384]{1,0:T(8,128)}) custom-call(bf16[8,2,1472,1024]{3,2,1,0:T(8,128)(2,1)} %bitcast.47, f32[16,8,384]{2,1,0:T(8,128)} %bitcast.60), custom_call_target="tpu_custom_call" | custom-call | tf_op jit(solution)/shard_map/scatter_grads/pallas_call | solution.py:401
  704.6 0.7 slice_reduce_fusion.16
  705.3 0.7 slice.183
  706.0 0.7 reshape.182
  707.3 0.7 slice.186
  708.6 0.8 slice.184
  710.5 1.1 slice.178
  711.6 0.8 copy.52
  712.5 1.9 fusion.7
  714.3 1.2 slice.176
  715.5 3.9 fusion.6
  719.5 1.0 copy.53
  721.0 1.3 copy.55
  722.4 1.0 copy.51
  723.4 1.3 copy.85
  724.8 1.0 copy-done.1
  725.8 1.3 copy.86
  (76 shorter events, 6.2 us)
Async XLA Ops:
  347.0 0.6 copy-start.2
  347.6 0.6 copy-start.3
  467.2 6.5 copy-start.4
  721.0 2.4 copy-start
  723.4 2.3 copy-start.1
where the time goes:
time: 738 us; the launch traced here: 728 us
  Pallas kernels  672 us (91%)
  local copies, waits for them, and re-layouts  41.2 us (6%)
    pallas_call x1, Pallas kernels, scatter_call(): pl.pallas_call(functools.partial(scatter_kernel, units), out_shape=(jax.S...  230 us
    pallas_call x1, Pallas kernels, front(): pl.pallas_call(functools.partial(front_kernel, tuple(blocks)), out_shape=...  211 us
    pallas_call x1, Pallas kernels, middle(): pl.pallas_call(functools.partial(middle_kernel, frames), out_shape=[shape...  62.3 us
    pallas_call x1, Pallas kernels, rear(): pl.pallas_call(functools.partial(rear_kernel, halo), out_shape=[shape(cou...  52.4 us
    pallas_call x1, Pallas kernels, convolve_back(): pl.pallas_call(functools.partial(convolve_back_kernel, frames), out_shape...  33.4 us
    pallas_call x1, Pallas kernels, convolve(): pl.pallas_call(convolve_kernel, out_shape=[shape(count, 1024), shape(coun...  30.7 us
    pallas_call x1, Pallas kernels, attend_back(): pl.pallas_call(functools.partial(attend_back_kernel, 1.0 / math.sqrt(128)...  30.6 us
    pallas_call x1, Pallas kernels, attend(): pl.pallas_call(functools.partial(attend_kernel, 1.0 / math.sqrt(128)), ou...  21.5 us

commit v1 on v0

--- a/solution.py
+++ b/solution.py
@@ -161,18 +161,24 @@
         for unit in range(min(self.LEAD, self.units)):
             self.send_own(unit)
 
-    def tick(self, step):
-        for name, distance, lag in self.EVENTS:
+    def part(self, step, quarter):
+        bounds = (0, 3, 6, 9, len(self.EVENTS))
+        for name, distance, lag in self.EVENTS[bounds[quarter]:bounds[quarter + 1]]:
             unit = step - lag
 
             @pl.when((unit >= 0) & (unit < self.units))
             def _(name=name, distance=distance, unit=unit):
                 getattr(self, name)(unit, distance)
-        unit = step + self.LEAD
-
-        @pl.when(unit < self.units)
-        def _():
-            self.send_own(unit)
+        if quarter == 3:
+            unit = step + self.LEAD
+
+            @pl.when(unit < self.units)
+            def _():
+                self.send_own(unit)
+
+    def tick(self, step):
+        for quarter in range(4):
+            self.part(step, quarter)
 
     def run(self, first, last):
         loop(last, self.tick, first)
@@ -360,7 +366,7 @@
         landed(grads.at[0, 0, 0:units * S_PLANE], self.snd.at[5])
 
 
-def scatter_kernel(units, grads, small, out, small_out, own, obuf, cv, xv, yv, zv, fv, sown, sv, sx, load, store, cr, xr, yr, zr, fr, snd, sload, ssend, srecv, sxsem):
+def scatter_kernel(units, grads, small, last, out, small_out, last_out, lv, lout, lsem, own, obuf, cv, xv, yv, zv, fv, sown, sv, sx, load, store, cr, xr, yr, zr, fr, snd, sload, ssend, srecv, sxsem):
     r, t, c, y, z = place()
     R = lax.axis_size("rows")
     cs = pltpu.make_async_copy(small, sown, sload.at[0])
@@ -368,12 +374,21 @@
     greet([(lax.rem(r + d, R), t) for d in range(1, R)] + [(r, 1 - t)])
     s = Scatter(grads, out, units, (own, obuf, cv, xv, yv, zv, fv), (load, store, cr, xr, yr, zr, fr, snd))
     s.begin()
+    lc = pltpu.make_async_copy(last, lv.at[0], lsem.at[0])
+    lc.start()
+    lc.wait()
     cs.wait()
     for d in range(1, R):
         to = lax.rem(r + d, R)
         remote(sown.at[to], sv.at[R - 1 - d], ssend, srecv, to, t)
 
+    pieces = last.shape[0] // 16
+
     def step(i, carry):
+        @pl.when((i >= 2) & (i < pieces + 2))
+        def _():
+            rows = pl.ds(pl.multiple_of((i - 2) * 16, 16), 16)
+            remote(lv.at[0, rows], lv.at[1, rows], lsem.at[1], lsem.at[2], r, 1 - t)
         s.tick(i)
         return carry
 
@@ -390,20 +405,27 @@
     sx[0] = sx[0] + sx[1]
     done = pltpu.make_async_copy(sx.at[0], small_out, sload.at[1])
     done.start()
+    landed(lv.at[0], lsem.at[1])
+    landed(lv.at[1], lsem.at[2])
+    lout[...] = lv[0].astype(jnp.float32) + lv[1].astype(jnp.float32)
+    lc = pltpu.make_async_copy(lout, last_out, lsem.at[0])
+    lc.start()
     s.finish()
     done.wait()
-
-
-def scatter_call(grads, small, cid):
+    lc.wait()
+
+
+def scatter_call(grads, small, last, cid):
     R, rows, _ = grads.shape
     units = rows // UNIT
     bf = jnp.bfloat16
     return pl.pallas_call(
         functools.partial(scatter_kernel, units),
-        out_shape=(jax.ShapeDtypeStruct((rows, 1024), jnp.float32), jax.ShapeDtypeStruct(small.shape[1:], small.dtype)),
-        in_specs=[pl.BlockSpec(memory_space=ANY)] * 2,
-        out_specs=(pl.BlockSpec(memory_space=ANY), pl.BlockSpec(memory_space=ANY)),
-        scratch_shapes=[pltpu.VMEM((2, 8, UNIT, 1024), bf), pltpu.VMEM((2, UNIT, 1024), jnp.float32),
+        out_shape=(jax.ShapeDtypeStruct((rows, 1024), jnp.float32), jax.ShapeDtypeStruct(small.shape[1:], small.dtype), jax.ShapeDtypeStruct(last.shape, jnp.float32)),
+        in_specs=[pl.BlockSpec(memory_space=ANY)] * 3,
+        out_specs=(pl.BlockSpec(memory_space=ANY),) * 3,
+        scratch_shapes=[pltpu.VMEM((2,) + last.shape, bf), pltpu.VMEM(last.shape, jnp.float32), pltpu.SemaphoreType.DMA((3,)),
+                        pltpu.VMEM((2, 8, UNIT, 1024), bf), pltpu.VMEM((2, UNIT, 1024), jnp.float32),
                         pltpu.VMEM((units, 8, UNIT, 1024), bf), pltpu.VMEM((units, 8, S_EDGE, 1024), bf), pltpu.VMEM((units, 4, S_PLANE, 1024), bf),
                         pltpu.VMEM((units, 5, S_PLANE, 1024), bf), pltpu.VMEM((units, S_PLANE, 1024), bf),
                         pltpu.VMEM(small.shape, small.dtype), pltpu.VMEM((R - 1,) + small.shape[1:], small.dtype), pltpu.VMEM((2,) + small.shape[1:], small.dtype),
@@ -412,7 +434,7 @@
                         pltpu.SemaphoreType.DMA((2,)), pltpu.SemaphoreType.DMA, pltpu.SemaphoreType.DMA, pltpu.SemaphoreType.DMA((2,))],
         compiler_params=pltpu.CompilerParams(collective_id=cid, has_side_effects=True, vmem_limit_bytes=67043328),
         name="scatter_grads",
-    )(grads.reshape(R // 2, 2, rows, 1024), small)
+    )(grads.reshape(R // 2, 2, rows, 1024), small, last)
 
 
 HALO = 384
@@ -486,7 +508,8 @@
         self.R = out.shape[0]
         self.n = 1024 // self.R
 
-    def put(self, unit, kind, index, left, right):
+    def put(self, unit, kind, index, left, right, out=None):
+        out = self.out if out is None else out
         slot = self.count % 2
         buf, n, R = self.buf.at[slot], self.n, self.R
         if self.count >= 2:
@@ -496,9 +519,9 @@
             buf[:, c] = dot(left, right(c), TN).astype(BF16)
         by_cols(1024, cols)
         if kind == "in":
-            pairs = [(buf.at[s * n:(s + 1) * n], self.out.at[s, (unit + index) * n:(unit + index + 1) * n]) for s in range(R)]
+            pairs = [(buf.at[s * n:(s + 1) * n], out.at[s, (unit + index) * n:(unit + index + 1) * n]) for s in range(R)]
         else:
-            pairs = [(buf.at[s * 4 * n:(s + 1) * 4 * n], self.out.at[index * (R // 4) + s, unit * n:(unit + 4) * n]) for s in range(R // 4)]
+            pairs = [(buf.at[s * 4 * n:(s + 1) * 4 * n], out.at[index * (R // 4) + s, unit * n:(unit + 4) * n]) for s in range(R // 4)]
         for src, dst in pairs:
             pltpu.make_async_copy(src, dst, self.sems.at[slot]).start()
         self.count += 1
@@ -630,7 +653,7 @@
 def front_kernel(blocks, *refs):
     small, *refs = refs
     ws, refs = refs[:8], refs[8:]
-    (tokens, full, params, x1, z1, q, k, v, beside, own, slab, slabs, wbuf, a, h, zbuf,
+    (tokens, hot, segq, segk, full, params, x1, z1, q, k, v, beside, o, lse, windows, own, slab, slabs, table, strip, wbuf, a, h, zbuf,
      load, keep, ssend, srecv, wsem, zsem, esem, *sems) = refs
     r, t, c, y, z = place()
     units, R, count = len(blocks), lax.axis_size("rows"), tokens.shape[0]
@@ -655,20 +678,22 @@
         put.wait()
     g = Gather(full, 0, units, sems)
     g.begin()
-    landed(slabs.at[0:R - 1], ssend)
-    landed(slabs.at[0:R - 1], srecv)
-    slabs[r] = slab[...]
-    for pair in range(R // 2):
-        params[:, pair * 128:(pair + 1) * 128] = (slabs[2 * pair].astype(F32) + slabs[2 * pair + 1].astype(F32))[0:40]
-    for s in range(R):
-        rows = slabs[s].astype(F32)
-        for b in range(2):
-            for part in range(2):
-                at = 40 + 2 * b + part
-                params[BIAS + 4 * b + s // 4:BIAS + 4 * b + s // 4 + 1, (s % 4) * 256 + part * 128:(s % 4) * 256 + (part + 1) * 128] = rows[at:at + 1]
+
+    def take_rows():
+        landed(slabs.at[0:R - 1], ssend)
+        landed(slabs.at[0:R - 1], srecv)
+        slabs[r] = slab[...]
+        for pair in range(R // 2):
+            params[:, pair * 128:(pair + 1) * 128] = (slabs[2 * pair].astype(F32) + slabs[2 * pair + 1].astype(F32))[0:40]
+        for s in range(R):
+            rows = slabs[s].astype(F32)
+            for b in range(2):
+                for part in range(2):
+                    at = 40 + 2 * b + part
+                    params[BIAS + 4 * b + s // 4:BIAS + 4 * b + s // 4 + 1, (s % 4) * 256 + part * 128:(s % 4) * 256 + (part + 1) * 128] = rows[at:at + 1]
+
     w = Weights(full, wbuf, wsem, BLOCKS_A)
     f = Front(w, params, tokens, x1, z1, a, h, zbuf, zsem)
-    norm_tokens(tokens, params, a)
     mine, other = pl.ds(pl.multiple_of(t * HALO, 128), count), pl.ds(pl.multiple_of((1 - t) * count, 128), HALO)
 
     def exchange():
@@ -681,12 +706,27 @@
         landed(beside, esem.at[1])
         f.mix(1, beside, None, k, other)
 
-    work = {5: lambda: f.hidden(0), 6: lambda: f.hidden(1), 7: lambda: f.hidden(2), 8: lambda: f.hidden(3),
-            12: lambda: (f.project(0), f.project(1)), 13: lambda: (f.project(2), f.project(3), exchange()),
-            14: lambda: (w.wait(8, 9), f.mix(0, a, SHIFT + 7, q, slice(None)), f.mix(1, a, None, k, mine)),
-            15: lambda: (w.wait(10), f.mix(2, a, SHIFT + 8, v, mine)), 16: receive, 17: lambda: f.mix(2, beside, SHIFT + 8, v, other)}
+    def bias_rows():
+        for head in range(HEADS):
+            table[head:head + 1] = params[REL:REL + 1, head * NB:(head + 1) * NB].astype(BF16)
+        windows[...] = dot(table[...], hot[...])
+
+    def head_rows(head, b):
+        cols, rows = pl.ds(pl.multiple_of(head * 128, 128), 128), pl.ds(b * QB, QB)
+        if b == 0:
+            strip[...] = strip_of(windows[pl.ds(head, 1)], windows.shape[-1])
+        base = k.shape[0] + QB - t * HALO
+        attend_rows(q[rows, cols], k[:, cols], v[:, cols], strip, base, b, segq[rows], segk[...], o.at[rows, cols], lse.at[head, rows])
+
+    work = {(2, 1): take_rows, (3, 1): lambda: norm_tokens(tokens, params, a), (4, 1): bias_rows, (5, 1): lambda: f.hidden(0), (6, 1): lambda: f.hidden(1), (7, 1): lambda: f.hidden(2), (8, 1): lambda: f.hidden(3),
+            (12, 0): lambda: f.project(0), (12, 2): lambda: f.project(1), (13, 0): lambda: f.project(2), (13, 1): lambda: f.project(3), (13, 2): exchange,
+            (14, 1): lambda: (w.wait(8), f.mix(0, a, SHIFT + 7, q, slice(None))), (14, 3): lambda: (w.wait(9), f.mix(1, a, None, k, mine)),
+            (15, 1): lambda: (w.wait(10), f.mix(2, a, SHIFT + 8, v, mine)), (16, 1): receive, (17, 1): lambda: f.mix(2, beside, SHIFT + 8, v, other)}
     for step in range(18):
-        g.tick(step)
+        for quarter in range(4):
+            g.part(step, quarter)
+            if (step, quarter) in work:
+                work[step, quarter]()
         unit = step - g.LAG
         if 0 <= unit < 11:
             g.arrived(unit)
@@ -694,15 +734,20 @@
                 w.start(4, 5, 6, 7)
             elif unit < 4 or unit > 7:
                 w.start(unit)
-        if step in work:
-            work[step]()
-    g.run(18, units + g.LAG)
+
+    def heads(step):
+        for quarter in range(4):
+            g.part(step, quarter)
+            head_rows(step - 18, quarter)
+    loop(18 + HEADS, heads, 18)
+    g.run(18 + HEADS, units + g.LAG)
     g.finish()
     for slot in range(2):
         f.stored(slot)
 
 
-def front(small, weights, tokens, cid):
+def front(small, weights, tokens, hot, segq, segk, cid):
+    length = hot.shape[1]
     count, R, blocks = tokens.shape[0], lax.axis_size("rows"), []
     near = count + HALO
     for i, weight in enumerate(weights):
@@ -712,14 +757,15 @@
     return pl.pallas_call(
         functools.partial(front_kernel, tuple(blocks)),
         out_shape=[shape(R, units * UNIT, 1024, dtype=BF16), shape(40, 1024), shape(count, 1024), shape(count, 4096), shape(count, 1024, dtype=BF16),
-                   shape(near, 1024, dtype=BF16), shape(near, 1024, dtype=BF16), shape(HALO, 1024, dtype=BF16)],
-        in_specs=[anywhere()] * 9 + [whole()], out_specs=[anywhere(), whole(), whole(), anywhere()] + [whole()] * 4,
-        scratch_shapes=[pltpu.VMEM((units * UNIT, 1024), BF16), pltpu.VMEM(small.shape, BF16), pltpu.VMEM((R,) + small.shape, BF16),
+                   shape(near, 1024, dtype=BF16), shape(near, 1024, dtype=BF16), shape(HALO, 1024, dtype=BF16),
+                   shape(count, 1024), shape(HEADS, count, 128), shape(HEADS, length)],
+        in_specs=[anywhere()] * 9 + [whole()] * 4, out_specs=[anywhere(), whole(), whole(), anywhere()] + [whole()] * 7,
+        scratch_shapes=[pltpu.VMEM((units * UNIT, 1024), BF16), pltpu.VMEM(small.shape, BF16), pltpu.VMEM((R,) + small.shape, BF16), pltpu.VMEM((HEADS, NB), BF16), pltpu.VMEM((QB, length), F32),
                         pltpu.VMEM((11, 1024, 1024), BF16), pltpu.VMEM((count, 1024), BF16), pltpu.VMEM((4, count, 1024), BF16), pltpu.VMEM((2, count, 1024), F32),
                         sem((units,)), sem, sem, sem, sem((11,)), sem((2,)), sem((2,))] + Gather.scratch(units),
         compiler_params=pltpu.CompilerParams(vmem_limit_bytes=VMEM_LIMIT, collective_id=cid, has_side_effects=True),
         name="front",
-    )(small, *weights, tokens)
+    )(small, *weights, tokens, hot, segq, segk)
 
 
 def plain_front_kernel(tokens, params, full, x1, z1, q, k, v, wbuf, a, h, zbuf, wsem, zsem):
@@ -766,19 +812,26 @@
     return jnp.where(segq == segk, s, NEG), start
 
 
-def attend_kernel(scale, off, q, k, v, window, segq, segk, o, lse, strip):
+SCALE = 1.0 / math.sqrt(128)
+
+
+def attend_rows(q, k, v, strip, base, b, segq, segk, o, lse):
+    s, _ = score_block(q, k, strip, base, b, k.shape[0], segq, segk, SCALE)
+    top = jnp.max(s, axis=-1, keepdims=True)
+    p = jnp.exp(s - top)
+    total = jnp.sum(p, axis=-1, keepdims=True)
+    o[...] = dot(p.astype(BF16), v) / total
+    lse[...] = jnp.broadcast_to(top + jnp.log(total), (QB, 128))
+
+
+def attend_kernel(off, q, k, v, window, segq, segk, o, lse, strip):
     near = k.shape[0]
     strip[...] = strip_of(window[0], window.shape[-1])
     base = near + QB - off[0]
 
     def block(b):
         rows = pl.ds(pl.multiple_of(b * QB, QB), QB)
-        s, _ = score_block(q[rows], k[...], strip, base, b, near, segq[rows], segk[...], scale)
-        top = jnp.max(s, axis=-1, keepdims=True)
-        p = jnp.exp(s - top)
-        total = jnp.sum(p, axis=-1, keepdims=True)
-        o[rows] = dot(p.astype(BF16), v[...]) / total
-        lse[0, rows] = jnp.broadcast_to(top + jnp.log(total), (QB, 128))
+        attend_rows(q[rows], k[...], v[...], strip, base, b, segq[rows], segk[...], o.at[rows], lse.at[0, rows])
     loop(q.shape[0] // QB, block)
 
 
@@ -789,7 +842,7 @@
 def attend(q, k, v, windows, segq, segk, off):
     count, near, length = q.shape[0], k.shape[0], windows.shape[-1]
     return pl.pallas_call(
-        functools.partial(attend_kernel, 1.0 / math.sqrt(128)),
+        attend_kernel,
         out_shape=[shape(count, 1024), shape(HEADS, count, 128)],
         grid_spec=pltpu.PrefetchScalarGridSpec(
             num_scalar_prefetch=1, grid=(HEADS,),
@@ -936,7 +989,7 @@
 BLOCKS_D = tuple([(CONV, "in", 0)] + [(FI2, "in", j) for j in range(4)] + [(FO2, "out", j) for j in range(4)])
 
 
-def middle_kernel(frames, x2, y, sums, cot, params, full, out, g3, dn, totals, small, grads,
+def middle_kernel(frames, x2, y, sums, cot, params, full, out, g3, dn, totals, small, grads, grads_b,
                   wbuf, a, e, d, dz, h, z, stage, half, send, recv, wsem, gsem, ssem, rsem):
     w = Weights(full, wbuf, wsem, BLOCKS_D)
     w.start()
@@ -1006,7 +1059,7 @@
         by_cols(1024, cols)
     loop(4, back)
     for j in range(4):
-        g.put(FO2, "out", j, h[j], lambda c: d[:, c])
+        g.put(0, "out", j, h[j], lambda c: d[:, c], grads_b)
     for j in range(4):
         g.put(FI2, "in", j, a[...], lambda c, j=j: dz[j, :, c])
     da = z.at[0]
@@ -1056,8 +1109,8 @@
     bufs, sems = reduce_scratch()
     return pl.pallas_call(
         functools.partial(middle_kernel, frames),
-        out_shape=[shape(count, 1024), shape(count, 1024), shape(count, 1024), shape(2, 1024), shape(96, 1024), shape(*full.shape, dtype=BF16)],
-        in_specs=[whole()] * 5 + [anywhere()], out_specs=[whole()] * 5 + [anywhere()],
+        out_shape=[shape(count, 1024), shape(count, 1024), shape(count, 1024), shape(2, 1024), shape(96, 1024), shape(full.shape[0], FO2 * 1024 // full.shape[0], 1024, dtype=BF16), shape(full.shape[0], 4096 // full.shape[0], 1024, dtype=BF16)],
+        in_specs=[whole()] * 5 + [anywhere()], out_specs=[whole()] * 5 + [anywhere()] * 2,
         scratch_shapes=[pltpu.VMEM((9, 1024, 1024), BF16), pltpu.VMEM((count, 1024), BF16), pltpu.VMEM((count, 1024), BF16), pltpu.VMEM((count, 1024), BF16),
                         pltpu.VMEM((4, count, 1024), BF16), pltpu.VMEM((4, count, 1024), BF16), pltpu.VMEM((4, count, 1024), F32),
                         pltpu.VMEM((2, 1024, 1024), BF16), pltpu.VMEM((16, 1024), F32)] + bufs + [pltpu.SemaphoreType.DMA((9,)), pltpu.SemaphoreType.DMA((2,))] + sems,
@@ -1146,7 +1199,7 @@
     count = x2.shape[0]
     return pl.pallas_call(
         functools.partial(convolve_back_kernel, frames),
-        out_shape=[shape(count, 1024), shape(count, 1024, dtype=BF16), shape(80, 1024), shape(*full.shape, dtype=BF16)],
+        out_shape=[shape(count, 1024), shape(count, 1024, dtype=BF16), shape(80, 1024), shape(*grads.shape, dtype=BF16)],
         in_specs=[whole()] * 12 + [anywhere()] * 2, out_specs=[whole()] * 3 + [anywhere()],
         scratch_shapes=[pltpu.VMEM((3, 1024, 1024), BF16), pltpu.VMEM((count, 1024), BF16), pltpu.VMEM((count, 1024), BF16), pltpu.VMEM((2, count, 1024), BF16),
                         pltpu.VMEM((count + 16, 1024), F32), pltpu.VMEM((2, 1024, 1024), BF16),
@@ -1290,7 +1343,7 @@
     specs = [whole(), whole(), anywhere()] + [whole()] * 5 + [anywhere()] + ([whole()] if halo else []) + [anywhere()]
     return pl.pallas_call(
         functools.partial(rear_kernel, halo),
-        out_shape=[shape(count, 1024), shape(88, 1024), shape(*full.shape, dtype=BF16)],
+        out_shape=[shape(count, 1024), shape(88, 1024), shape(*grads.shape, dtype=BF16)],
         in_specs=specs, out_specs=[whole(), whole(), anywhere()], scratch_shapes=scratch,
         input_output_aliases={len(specs) - 1: 2},
         compiler_params=pltpu.CompilerParams(vmem_limit_bytes=VMEM_LIMIT, **({"collective_id": cid, "has_side_effects": True} if halo else {})),
@@ -1361,13 +1414,6 @@
     links = R == 16 and T == 2 and count == 512
     frames = R * T * count * packed_rows
     weights = (ffn1_in, ffn1_out, qkv_weight, attn_out, glu_in, conv_out, ffn2_in, ffn2_out)
-    tok = tokens.reshape(count, width)
-    if links:
-        full, params, x1, z1, q, k, v, beside = front(slab_rows(gains, shifts, ffn_bias, conv_kernel, rel_table), weights, tok, 0)
-    else:
-        full = lax.all_gather(pack_weights(weights), "rows", axis=0)
-        params = wide_rows(lax.all_gather(pack_rows(gains, shifts, ffn_bias, conv_kernel, rel_table), "rows", axis=0))
-
     seg_all = lax.all_gather(segment_ids, "tm", axis=1, tiled=True)[0]
     seg_far = jnp.pad(seg_all, (HALO, HALO), constant_values=-1)
     segx = lax.dynamic_slice_in_dim(seg_far, HALO + t * count - 8, count + 16)[:, None]
@@ -1383,17 +1429,26 @@
     before, after = int(np.argmax(places > 0)), int(np.argmax(places >= 2 * MAXD))
     buckets = jnp.concatenate([jnp.broadcast_to(rel_bucket[:1], (before,)), rel_bucket[1 : 2 * MAXD], jnp.broadcast_to(rel_bucket[2 * MAXD :], (length - after,))])
     hot = (buckets[None, :] == jnp.arange(NB, dtype=jnp.int32)[:, None]).astype(F32)
-    windows = jnp.dot(params[REL].reshape(HEADS, NB), hot, precision=HIGH).reshape(HEADS, 1, length)
     off = off.astype(jnp.int32).reshape(1)
+    tok = tokens.reshape(count, width)
+    if links:
+        full, params, x1, z1, q, k, v, beside, o, lse, windows = front(slab_rows(gains, shifts, ffn_bias, conv_kernel, rel_table), weights, tok, hot.astype(BF16), segq, segk, 0)
+        windows = windows.reshape(HEADS, 1, length)
+    else:
+        full = lax.all_gather(pack_weights(weights), "rows", axis=0)
+        params = wide_rows(lax.all_gather(pack_rows(gains, shifts, ffn_bias, conv_kernel, rel_table), "rows", axis=0))
+
+        windows = jnp.dot(params[REL].reshape(HEADS, NB), hot, precision=HIGH).reshape(HEADS, 1, length)
 
     if not links:
         x1, z1, q, k, v = plain_front(tok, params, full)
         beside = None
         k = lax.all_gather(k, "tm", axis=0, tiled=True)
         v = lax.all_gather(v, "tm", axis=0, tiled=True)
-    o, lse = attend(q, k, v, windows, segq, segk, off)
+        o, lse = attend(q, k, v, windows, segq, segk, off)
     x2, c1, c2, u, y, sums = convolve(x1, o, params, segx, full, 3)
-    output, g3, dn, totals, small_d, grads = middle(x2, y, sums, cotangent.reshape(count, width), params, full, frames, 4)
+    output, g3, dn, totals, small_d, grads, grads_b = middle(x2, y, sums, cotangent.reshape(count, width), params, full, frames, 4)
+    last = lax.psum_scatter(grads_b, "rows", scatter_dimension=0, tiled=False)
     g2, dob, small_c, grads = convolve_back(dn, y, sums, totals, c1, c2, u, x2, g3, o, params, segx, full, grads, frames, 5)
     dq, dk, dv, dtable = attend_back(q, k, v, windows, segq, segk, off, o, lse, dob)
     if not links:
@@ -1410,11 +1465,12 @@
         e[10:11], e[3:4], c[8:9], d[8:9], d[1:2], d[11:12], e[4:5], e[0:2], c[9:10], c[5:7], d[9:10], d[2:3],
         e[5:9], d[3:7], c[0:5], rel])
     if links:
-        shard, small = scatter_call(grads, slot_rows(rows, R), 1)
+        shard, small, last = scatter_call(grads, slot_rows(rows, R), last, 1)
     else:
         shard = lax.psum(lax.psum_scatter(grads, "rows", scatter_dimension=0, tiled=False), "tm").astype(F32)
         small = lax.psum(lax.psum_scatter(slot_rows(rows, R), "rows", scatter_dimension=0, tiled=False), "tm")
-    return (output.reshape(tokens.shape), dtok.reshape(tokens.shape)) + unpack_shard(shard, weights) + shard_rows(small, R)
+        last = lax.psum(last, "tm").astype(F32)
+    return (output.reshape(tokens.shape), dtok.reshape(tokens.shape)) + unpack_shard(shard, weights[:7]) + (last,) + shard_rows(small, R)
 
 
 def solution(mesh):

time: 738 us -> 689 us (0.934)
  Pallas kernels: 672 us -> 621 us
  between operations: 1.48 us -> 14.9 us
    pallas_call x1, Pallas kernels: 230 us -> 197 us  [scatter_call(): pl.pallas_call(functools.partial(scatter_kernel, units), out_shape=(jax.S...]
    pallas_call x1 -> x0, Pallas kernels: 21.5 us -> none  [attend(): pl.pallas_call(functools.partial(attend_kernel, 1.0 / math.sqrt(128)), ou...]
  transfers between devices with their start and end apart: 0 -> 1, of which waited for: 0 -> 0; matrix products, arithmetic and copies ran while one was open for 0% -> 1% of each run, Pallas kernels for 0% -> 17%
where the time goes in v1:
time: 689 us; the launch traced here: 686 us
  Pallas kernels  621 us (90%)
  local copies, waits for them, and re-layouts  37.9 us (6%)
  between operations  14.9 us (2%)
    pallas_call x1, Pallas kernels, front(): pl.pallas_call(functools.partial(front_kernel, tuple(blocks)), out_shape=...  214 us
    pallas_call x1, Pallas kernels, scatter_call(): pl.pallas_call(functools.partial(scatter_kernel, units), out_shape=(jax.S...  197 us
    pallas_call x1, Pallas kernels, middle(): pl.pallas_call(functools.partial(middle_kernel, frames), out_shape=[shape...  63.3 us
    pallas_call x1, Pallas kernels, rear(): pl.pallas_call(functools.partial(rear_kernel, halo), out_shape=[shape(cou...  51.4 us
    pallas_call x1, Pallas kernels, convolve_back(): pl.pallas_call(functools.partial(convolve_back_kernel, frames), out_shape...  34.7 us
    pallas_call x1, Pallas kernels, attend_back(): pl.pallas_call(functools.partial(attend_back_kernel, 1.0 / math.sqrt(128)...  30.6 us
    pallas_call x1, Pallas kernels, convolve(): pl.pallas_call(convolve_kernel, out_shape=[shape(count, 1024), shape(coun...  30.5 us
  transfers between devices with their start and end apart: 1, of which 0 were waited for; matrix products, arithmetic and copies ran while one was open for 1% of the time, Pallas kernels for 17%

profile of v1, /device:TPU:0, one launch (start us, length us, event | category | flops | bytes accessed | tf_op | source)
XLA Modules:
  0.0 685.6 jit_solution(9928901458005908626)
XLA Ops:
  7.2 1.3 fusion.6
  8.5 0.8 slice.142
  9.3 0.7 reshape.157
  10.0 5.4 all_gather.3
  15.4 1.5 copy.40.refs_11_.segq
  16.9 0.6 constant_dynamic-slice_fusion.refs_12_.segk
  17.6 0.8 broadcast_in_dim.45.seg
  18.4 0.6 broadcast_in_dim.43
  19.1 0.6 broadcast_in_dim.41
  19.8 0.9 convert_convert_fusion.refs_10_
  20.8 3.0 concatenate.68
  23.8 0.7 maximum_maximum_fusion.refs_0_
  24.5 213.7 %front.1 = (bf16[16,1472,1024]{2,1,0:T(8,128)(2,1)}, f32[40,1024]{1,0:T(8,128)}, f32[512,1024]{1,0:T(8,128)}, f32[512,4096]{1,0:T(8,128)}, bf16[512,1024]{1,0:T(...) custom-call(bf16[48,128]{1,0:T(8,128)(2,1)} %maximum_maximum_fusion., ...), custom_call_target="tpu_custom_call" | custom-call | tf_op jit(solution)/shard_map/front/pallas_call | solution.py:757
  238.3 30.5 %convolve.1 = (f32[512,1024]{1,0:T(8,128)}, f32[512,1024]{1,0:T(8,128)}, f32[512,1024]{1,0:T(8,128)}, f32[528,1024]{1,0:T(8,128)}, f32[512,1024]{1,0:T(8,128)}, /*index=5*/f32[2,1024]{1,0:T(2,128)}) custom-call(f32[512,1024]{1,0:T(8,128)} %get-tuple-element.53.x1, f32[512,1024]{1,0:T(8,128)} %get-tuple-element.54.o, f32[40,1024]{1,0:T(8,128)} %get-tuple-element.55.params, ...), custom_call_target="tpu_custom_call" | custom-call | tf_op jit(solution)/shard_map/convolve/pallas_call | solution.py:973
  268.8 63.3 %middle.1 = (f32[512,1024]{1,0:T(8,128)}, f32[512,1024]{1,0:T(8,128)}, f32[512,1024]{1,0:T(8,128)}, f32[2,1024]{1,0:T(2,128)}, f32[96,1024]{1,0:T(8,128)}, /*ind...) custom-call(f32[512,1024]{1,0:T(8,128)} %get-tuple-element.57.x2, f32[512,1024]{1,0:T(8,128)} %get-tuple-element.58.y, ...), custom_call_target="tpu_custom_call" | custom-call | tf_op jit(solution)/shard_map/middle/pallas_call | solution.py:1110
  332.1 0.8 copy-done.3
  332.9 0.7 reshape.163.window
  333.6 34.7 %convolve_back.1 = (f32[512,1024]{1,0:T(8,128)}, bf16[512,1024]{1,0:T(8,128)(2,1)}, f32[80,1024]{1,0:T(8,128)}, bf16[16,1216,1024]{2,1,0:T(8,128)(2,1)}) custom-call(f32[512,1024]{1,0:T(8,128)} %get-tuple-element.62.dn, f32[512,1024]{1,0:T(8,128)} %get-tuple-element.58.y, f32[2,1024]{1,0:T(2,128)} %get-tuple-element.59.sums, ...), custom_call_target="tpu_custom_call", output_to_operand_aliasing={{3}: (13, {})} | custom-call | tf_op jit(solution)/shard_map/convolve_back/pallas_call | solution.py:1200
  368.3 30.6 %attend_back.1 = (bf16[512,1024]{1,0:T(8,128)(2,1)}, bf16[896,1024]{1,0:T(8,128)(2,1)}, bf16[896,1024]{1,0:T(8,128)(2,1)}, f32[8,1,1920]{2,1,0:T(1,128)}) custom-call(s32[1]{0:T(128)} %bitcast.8.off, bf16[512,1024]{1,0:T(8,128)(2,1)} %get-tuple-element.70.q, bf16[896,1024]{1,0:T(8,128)(2,1)} %get-tuple-element.71.k, bf16[896,1024]{1,0:T(8,128)(2,1)} %get-tuple-element.72.v, ...), custom_call_target="tpu_custom_call" | custom-call | tf_op jit(solution)/shard_map/attend_back/pallas_call | solution.py:888
  398.9 51.4 %rear.1 = (f32[512,1024]{1,0:T(8,128)}, f32[88,1024]{1,0:T(8,128)}, bf16[16,1216,1024]{2,1,0:T(8,128)(2,1)}) custom-call(bf16[512,1024]{1,0:T(8,128)(2,1)} %bitcast.48, f32[512,1024]{1,0:T(8,128)} %get-tuple-element.53.x1, f32[512,4096]{1,0:T(8,128)} %get-tuple-element.61.z1, f32[512,1024]{1,0:T(8,128)} %get-tuple-element.69.g2, ...), custom_call_target="tpu_custom_call", output_to_operand_aliasing={{2}: (10, {})} | custom-call | tf_op jit(solution)/shard_map/rear/pallas_call | solution.py:1344
  450.2 1.1 bitcast_reduce_fusion.1
  451.3 1.1 bitcast_reduce_fusion.2
  452.4 1.1 bitcast_reduce_fusion
  453.6 1.4 fusion
  457.4 0.7 copy.54
  458.1 196.9 %scatter_grads.1 = (f32[1216,1024]{1,0:T(8,128)}, f32[8,384]{1,0:T(8,128)}, f32[256,1024]{1,0:T(8,128)}) custom-call(bf16[8,2,1216,1024]{3,2,1,0:T(8,128)(2,1)} %bitcast.46, f32[16,8,384]{2,1,0:T(8,128)} %bitcast.59, bf16[256,1024]{1,0:T(8,128)(2,1)} %bitcast.62), custom_call_target="tpu_custom_call" | custom-call | tf_op jit(solution)/shard_map/scatter_grads/pallas_call | solution.py:422
  655.0 0.7 slice_reduce_fusion.16
  655.8 0.7 reshape.182
  656.5 0.7 slice.178
  657.2 0.8 slice.176
  658.0 0.6 slice.207
  658.6 0.6 slice.205
  659.2 1.1 slice.171
  660.2 1.9 fusion.5
  662.1 1.2 slice.169
  663.3 3.1 fusion.4
  666.4 0.7 slice.175
  667.1 0.6 slice.208
  667.7 0.6 slice.206
  668.2 0.8 copy.52
  669.1 1.0 copy.53
  670.7 1.3 copy.55
  672.0 1.0 copy.51
  673.1 1.3 copy.86
  674.4 1.0 copy-done.1
  675.4 1.3 copy.87
  676.7 0.6 copy-done.2
  677.4 1.0 copy.88
  (78 shorter events, 3.1 us)
Async XLA Ops:
  7.2 450.9 %reduce-scatter.2.cloned.1.call-start = ((), (), s32[]{:S(2)}) async-start(), calls=%async_computation.1 | async-start | bytes 8912896 | tf_op jit(solution)/shard_map/reduce_scatter | solution.py:1451
  19.8 1.0 copy-start.4
  332.1 0.8 copy-start.3
  670.7 2.4 copy-start
  673.1 2.3 copy-start.1
  675.4 2.0 copy-start.2
Sparse Core Ops, SparseCore 0:
  332.2 102.7 reduce-scatter.1

commit v2 on v1

--- a/solution.py
+++ b/solution.py
@@ -211,11 +211,33 @@
 
 
 class Scatter:
-    def __init__(self, grads, out, units, bufs, sems):
-        self.grads, self.out, self.units = grads, out, units
-        self.own, self.obuf, self.cv, self.xv, self.yv, self.zv, self.fv = bufs
-        self.load, self.store, self.cr, self.xr, self.yr, self.zr, self.fr, self.snd = sems
+    LEAD = 3
+    RING = 10
+    EVENTS = (("sum_core", 0, ()), ("sum_x", 1, ()), ("sum_y", 2, ()), ("hop", 3, (1,)), ("hop", 4, (2,)), ("hop", 5, (3,)), ("exchange", 5, ()), ("conclude", 6, ()))
+    LAG = 6
+
+    def __init__(self, grads, out, units, ready, first, scratch):
+        self.grads, self.out, self.units, self.ready, self.first = grads, out, units, ready, first
+        (self.own, self.obuf, self.cv, self.xv, self.yv, self.zv, self.fv,
+         self.load, self.store, self.cr, self.xr, self.yr, self.zr, self.fr, self.core, self.snd, self.free) = scratch
         self.r, self.t, self.c, self.y, self.z = place()
+
+    @classmethod
+    def scratch(cls, units):
+        sem, vmem, n, bf = pltpu.SemaphoreType.DMA, pltpu.VMEM, cls.RING, jnp.bfloat16
+        return [vmem((2, 8, UNIT, 1024), bf), vmem((2, UNIT, 1024), jnp.float32), vmem((n, 8, UNIT, 1024), bf), vmem((n, 8, S_EDGE, 1024), bf),
+                vmem((n, 4, S_PLANE, 1024), bf), vmem((n, 5, S_PLANE, 1024), bf), vmem((n, S_PLANE, 1024), bf),
+                sem((2,)), sem((2,)), sem((units,)), sem((units,)), sem((units, 4)), sem((units, 5)), sem((units,)), sem, sem((cls.RING, 5)), pltpu.SemaphoreType.REGULAR((5,))]
+
+    def ring(self, unit):
+        return lax.rem(unit, self.RING)
+
+    def rows_of(self, unit):
+        late = self.units - self.ready
+        after = unit - self.ready
+        late_unit = after + late // 2 - jnp.where(after >= late // 2, late, 0)
+        number = jnp.where(unit < self.ready, unit + self.first, late_unit)
+        return pl.ds(pl.multiple_of(number * UNIT, UNIT), UNIT)
 
     def mine(self):
         return pl.ds(pl.multiple_of(self.t * S_EDGE, 16), S_PLANE)
@@ -223,22 +245,26 @@
     def edge(self, tm):
         return pl.ds(pl.multiple_of(tm * S_PLANE, 16), S_EDGE)
 
+    def granted(self, unit, kind):
+        @pl.when(unit >= self.RING)
+        def _():
+            pl.semaphore_wait(self.free.at[kind], 1)
+
     def own_copy(self, unit):
-        rows = pl.ds(pl.multiple_of(unit * UNIT, UNIT), UNIT)
-        return pltpu.make_async_copy(self.grads.at[:, self.c, rows], self.own.at[lax.rem(unit, 2)], self.load.at[lax.rem(unit, 2)])
+        return pltpu.make_async_copy(self.grads.at[:, self.c, self.rows_of(unit)], self.own.at[lax.rem(unit, 2)], self.load.at[lax.rem(unit, 2)])
 
     def send_core(self, unit):
-        rows = pl.ds(pl.multiple_of(unit * UNIT, UNIT), UNIT)
-        remote(self.grads.at[:, 1 - self.c, rows], self.cv.at[unit], self.snd.at[0], self.cr.at[unit], self.r + 1 - 2 * self.c, self.t)
+        self.granted(unit, 0)
+        remote(self.grads.at[:, 1 - self.c, self.rows_of(unit)], self.cv.at[self.ring(unit)], self.core, self.cr.at[unit], self.r + 1 - 2 * self.c, self.t)
 
     def add(self, a, b, n):
-        def one(i, carry):
+        def one(i):
             a[i] = (a[i].astype(jnp.float32) + b[i].astype(jnp.float32)).astype(jnp.bfloat16)
-            return carry
-        lax.fori_loop(0, n, one, 0)
+        loop(n, one)
 
     def sum_core(self, unit):
-        cv = self.cv.at[unit]
+        at = self.ring(unit)
+        cv = self.cv.at[at]
         landed(cv, self.cr.at[unit])
         self.own_copy(unit).wait()
         self.add(cv, self.own.at[lax.rem(unit, 2)], 8)
@@ -246,44 +272,47 @@
         @pl.when(unit + 2 < self.units)
         def _():
             self.own_copy(unit + 2).start()
-        remote(cv.at[:, self.edge(1 - self.t)], self.xv.at[unit], self.snd.at[1], self.xr.at[unit], self.r, 1 - self.t)
+        self.granted(unit, 1)
+        remote(cv.at[:, self.edge(1 - self.t)], self.xv.at[at], self.snd.at[at, 0], self.xr.at[unit], self.r, 1 - self.t)
 
     def sum_x(self, unit):
-        xv, cv = self.xv.at[unit], self.cv.at[unit]
+        at = self.ring(unit)
+        xv, cv = self.xv.at[at], self.cv.at[at]
         landed(xv, self.xr.at[unit])
         self.add(cv.at[:, self.edge(self.t)], xv, 8)
+        self.granted(unit, 2)
         for k in range(4):
-            remote(cv.at[k * 2 + 1 - self.y, self.mine()], self.yv.at[unit, k], self.snd.at[2], self.yr.at[unit, k], self.r + 2 - 4 * self.y, self.t)
+            remote(cv.at[k * 2 + 1 - self.y, self.mine()], self.yv.at[at, k], self.snd.at[at, 1], self.yr.at[unit, k], self.r + 2 - 4 * self.y, self.t)
 
     def at_z(self, unit, z):
-        return self.cv.at[unit, z * 2 + self.y, self.mine()]
+        return self.cv.at[self.ring(unit), z * 2 + self.y, self.mine()]
 
     def send_z(self, unit, target, up):
-        at = self.at_z(unit, target)
-        remote(at, self.zv.at[unit, target + (1 if up else 0)], self.snd.at[3 if up else 4], self.zr.at[unit, target + (1 if up else 0)],
-               self.r + (4 if up else -4), self.t)
+        at, entry = self.at_z(unit, target), target + (1 if up else 0)
+        remote(at, self.zv.at[self.ring(unit), entry], self.snd.at[self.ring(unit), 2 if up else 3], self.zr.at[unit, entry], self.r + (4 if up else -4), self.t)
 
     def take_z(self, unit, target, below):
-        at = self.at_z(unit, target)
-        entry = target + (1 if below else 0)
-        zv = self.zv.at[unit, entry]
+        at, entry = self.at_z(unit, target), target + (1 if below else 0)
+        zv = self.zv.at[self.ring(unit), entry]
         landed(zv, self.zr.at[unit, entry])
         at[...] = (at[...].astype(jnp.float32) + zv[...].astype(jnp.float32)).astype(jnp.bfloat16)
 
     def sum_y(self, unit):
         for k in range(4):
-            yv = self.yv.at[unit, k]
+            yv = self.yv.at[self.ring(unit), k]
             landed(yv, self.yr.at[unit, k])
             at = self.at_z(unit, k)
             at[...] = (at[...].astype(jnp.float32) + yv[...].astype(jnp.float32)).astype(jnp.bfloat16)
 
         @pl.when(self.z == 0)
         def _():
+            self.granted(unit, 3)
             for target in (3, 2, 1):
                 self.send_z(unit, target, True)
 
         @pl.when(self.z == 3)
         def _():
+            self.granted(unit, 4)
             for target in (0, 1, 2):
                 self.send_z(unit, target, False)
 
@@ -292,43 +321,69 @@
             @pl.when(self.z == z)
             def _(z=z):
                 if number == z:
+                    if z < 3:
+                        self.granted(unit, 3)
                     for target in range(3, z - 1, -1):
                         self.take_z(unit, target, True)
                         if target > z:
                             self.send_z(unit, target, True)
                 if number == 3 - z:
+                    if z > 0:
+                        self.granted(unit, 4)
                     for target in range(0, z + 1):
                         self.take_z(unit, target, False)
                         if target < z:
                             self.send_z(unit, target, False)
 
     def exchange(self, unit):
-        at = self.at_z(unit, self.z)
-        remote(at, self.fv.at[unit], self.snd.at[5], self.fr.at[unit], self.r, 1 - self.t)
+        at = self.ring(unit)
+        remote(self.at_z(unit, self.z), self.fv.at[at], self.snd.at[at, 4], self.fr.at[unit], self.r, 1 - self.t)
 
     def store_copy(self, unit):
-        return pltpu.make_async_copy(self.obuf.at[lax.rem(unit, 2)], self.out.at[pl.ds(pl.multiple_of(unit * UNIT, UNIT), UNIT)], self.store.at[lax.rem(unit, 2)])
+        return pltpu.make_async_copy(self.obuf.at[lax.rem(unit, 2)], self.out.at[self.rows_of(unit)], self.store.at[lax.rem(unit, 2)])
 
     def conclude(self, unit):
-        fv = self.fv.at[unit]
+        at = self.ring(unit)
+        fv, cv = self.fv.at[at], self.cv.at[at, self.z * 2 + self.y]
         landed(fv, self.fr.at[unit])
-        at = self.cv.at[unit, self.z * 2 + self.y]
 
         @pl.when(unit >= 2)
         def _():
             self.store_copy(unit - 2).wait()
         obuf = self.obuf.at[lax.rem(unit, 2)]
         middle = pl.ds(S_EDGE, S_MIDDLE)
-        obuf[middle] = at[middle].astype(jnp.float32) + fv[pl.ds(pl.multiple_of(self.t * S_EDGE, 16), S_MIDDLE)].astype(jnp.float32)
-        obuf[self.edge(self.t)] = at[self.edge(self.t)].astype(jnp.float32)
+        obuf[middle] = cv[middle].astype(jnp.float32) + fv[pl.ds(pl.multiple_of(self.t * S_EDGE, 16), S_MIDDLE)].astype(jnp.float32)
+        obuf[self.edge(self.t)] = cv[self.edge(self.t)].astype(jnp.float32)
         obuf[self.edge(1 - self.t)] = fv[pl.ds(pl.multiple_of((1 - self.t) * S_MIDDLE, 16), S_EDGE)].astype(jnp.float32)
         self.store_copy(unit).start()
-
-    LEAD = 3
-    EVENTS = (("sum_core", 0, ()), ("sum_x", 1, ()), ("sum_y", 2, ()), ("hop", 3, (1,)), ("hop", 4, (2,)), ("hop", 5, (3,)), ("exchange", 5, ()), ("conclude", 6, ()))
-
-    def ticks(self):
-        return self.units + max(e[1] for e in self.EVENTS)
+        landed(self.xv.at[at], self.snd.at[at, 0])
+        landed(self.yv.at[at], self.snd.at[at, 1])
+        for z in range(4):
+            @pl.when(self.z == z)
+            def _(z=z):
+                if z < 3:
+                    landed(self.zv.at[at, 0:3 - z], self.snd.at[at, 2])
+                if z > 0:
+                    landed(self.zv.at[at, 0:z], self.snd.at[at, 3])
+        landed(fv, self.snd.at[at, 4])
+        more = unit + self.RING < self.units
+
+        def free(kind, rows, tm):
+            pl.semaphore_signal(self.free.at[kind], inc=1, device_id=(rows, tm), device_id_type=MESH)
+
+        @pl.when(more)
+        def _():
+            free(0, self.r + 1 - 2 * self.c, self.t)
+            free(1, self.r, 1 - self.t)
+            free(2, self.r + 2 - 4 * self.y, self.t)
+
+        @pl.when(more & (self.z > 0))
+        def _():
+            free(3, self.r - 4, self.t)
+
+        @pl.when(more & (self.z < 3))
+        def _():
+            free(4, self.r + 4, self.t)
 
     def begin(self):
         for unit in range(min(2, self.units)):
@@ -336,105 +391,52 @@
         for unit in range(min(self.LEAD, self.units)):
             self.send_core(unit)
 
-    def tick(self, step):
-        for name, lag, args in self.EVENTS:
+    def part(self, step, quarter):
+        for name, lag, args in self.EVENTS[2 * quarter:2 * quarter + 2]:
             unit = step - lag
 
             @pl.when((unit >= 0) & (unit < self.units))
             def _(name=name, unit=unit, args=args):
                 getattr(self, name)(unit, *args)
-        unit = step + self.LEAD
-
-        @pl.when(unit < self.units)
-        def _():
-            self.send_core(unit)
+        if quarter == 3:
+            unit = step + self.LEAD
+
+            @pl.when(unit < self.units)
+            def _():
+                self.send_core(unit)
+
+    def tick(self, step):
+        for quarter in range(4):
+            self.part(step, quarter)
+
+    def run(self, first, last):
+        loop(last, self.tick, first)
 
     def finish(self):
-        units, z, grads = self.units, self.z, self.grads
-        for unit in range(max(0, units - 2), units):
+        for unit in range(max(0, self.units - 2), self.units):
             self.store_copy(unit).wait()
-        landed(grads.at[:, 0, 0:units * UNIT], self.snd.at[0])
-        landed(grads.at[:, 0, 0:units * S_EDGE], self.snd.at[1])
-        landed(grads.at[0:4, 0, 0:units * S_PLANE], self.snd.at[2])
-        for k in range(4):
-            @pl.when(z == k)
-            def _(k=k):
-                if k < 3:
-                    landed(grads.at[0:3 - k, 0, 0:units * S_PLANE], self.snd.at[3])
-                if k > 0:
-                    landed(grads.at[0:k, 0, 0:units * S_PLANE], self.snd.at[4])
-        landed(grads.at[0, 0, 0:units * S_PLANE], self.snd.at[5])
-
-
-def scatter_kernel(units, grads, small, last, out, small_out, last_out, lv, lout, lsem, own, obuf, cv, xv, yv, zv, fv, sown, sv, sx, load, store, cr, xr, yr, zr, fr, snd, sload, ssend, srecv, sxsem):
-    r, t, c, y, z = place()
-    R = lax.axis_size("rows")
-    cs = pltpu.make_async_copy(small, sown, sload.at[0])
-    cs.start()
-    greet([(lax.rem(r + d, R), t) for d in range(1, R)] + [(r, 1 - t)])
-    s = Scatter(grads, out, units, (own, obuf, cv, xv, yv, zv, fv), (load, store, cr, xr, yr, zr, fr, snd))
-    s.begin()
-    lc = pltpu.make_async_copy(last, lv.at[0], lsem.at[0])
-    lc.start()
-    lc.wait()
-    cs.wait()
+        landed(self.grads.at[:, 0, 0:self.units * UNIT], self.core)
+
+
+def spread(slots, landing, send, recv):
+    r, t, R = lax.axis_index("rows"), lax.axis_index("tm"), lax.axis_size("rows")
     for d in range(1, R):
         to = lax.rem(r + d, R)
-        remote(sown.at[to], sv.at[R - 1 - d], ssend, srecv, to, t)
-
-    pieces = last.shape[0] // 16
-
-    def step(i, carry):
-        @pl.when((i >= 2) & (i < pieces + 2))
-        def _():
-            rows = pl.ds(pl.multiple_of((i - 2) * 16, 16), 16)
-            remote(lv.at[0, rows], lv.at[1, rows], lsem.at[1], lsem.at[2], r, 1 - t)
-        s.tick(i)
-        return carry
-
-    lax.fori_loop(0, s.ticks(), step, 0)
-    landed(sown.at[0:R - 1], ssend)
-    landed(sv.at[0:R - 1], srecv)
-    total = sown[r]
+        remote(slots.at[to], landing.at[R - 1 - d], send, recv, to, t)
+
+
+def gathered(slots, landing, pair, sems, send, recv):
+    r, t, R = lax.axis_index("rows"), lax.axis_index("tm"), lax.axis_size("rows")
+    landed(slots.at[0:R - 1], send)
+    landed(landing.at[0:R - 1], recv)
+    total = slots[r]
     for d in range(R - 1):
-        total = total + sv[d]
-    sx[0] = total
-    pltpu.make_async_remote_copy(src_ref=sx.at[0], dst_ref=sx.at[1], send_sem=sxsem.at[0], recv_sem=sxsem.at[1], device_id=(r, 1 - t), device_id_type=MESH).start()
-    landed(sx.at[0], sxsem.at[0])
-    landed(sx.at[1], sxsem.at[1])
-    sx[0] = sx[0] + sx[1]
-    done = pltpu.make_async_copy(sx.at[0], small_out, sload.at[1])
-    done.start()
-    landed(lv.at[0], lsem.at[1])
-    landed(lv.at[1], lsem.at[2])
-    lout[...] = lv[0].astype(jnp.float32) + lv[1].astype(jnp.float32)
-    lc = pltpu.make_async_copy(lout, last_out, lsem.at[0])
-    lc.start()
-    s.finish()
-    done.wait()
-    lc.wait()
-
-
-def scatter_call(grads, small, last, cid):
-    R, rows, _ = grads.shape
-    units = rows // UNIT
-    bf = jnp.bfloat16
-    return pl.pallas_call(
-        functools.partial(scatter_kernel, units),
-        out_shape=(jax.ShapeDtypeStruct((rows, 1024), jnp.float32), jax.ShapeDtypeStruct(small.shape[1:], small.dtype), jax.ShapeDtypeStruct(last.shape, jnp.float32)),
-        in_specs=[pl.BlockSpec(memory_space=ANY)] * 3,
-        out_specs=(pl.BlockSpec(memory_space=ANY),) * 3,
-        scratch_shapes=[pltpu.VMEM((2,) + last.shape, bf), pltpu.VMEM(last.shape, jnp.float32), pltpu.SemaphoreType.DMA((3,)),
-                        pltpu.VMEM((2, 8, UNIT, 1024), bf), pltpu.VMEM((2, UNIT, 1024), jnp.float32),
-                        pltpu.VMEM((units, 8, UNIT, 1024), bf), pltpu.VMEM((units, 8, S_EDGE, 1024), bf), pltpu.VMEM((units, 4, S_PLANE, 1024), bf),
-                        pltpu.VMEM((units, 5, S_PLANE, 1024), bf), pltpu.VMEM((units, S_PLANE, 1024), bf),
-                        pltpu.VMEM(small.shape, small.dtype), pltpu.VMEM((R - 1,) + small.shape[1:], small.dtype), pltpu.VMEM((2,) + small.shape[1:], small.dtype),
-                        pltpu.SemaphoreType.DMA((2,)), pltpu.SemaphoreType.DMA((2,)), pltpu.SemaphoreType.DMA((units,)), pltpu.SemaphoreType.DMA((units,)),
-                        pltpu.SemaphoreType.DMA((units, 4)), pltpu.SemaphoreType.DMA((units, 5)), pltpu.SemaphoreType.DMA((units,)), pltpu.SemaphoreType.DMA((6,)),
-                        pltpu.SemaphoreType.DMA((2,)), pltpu.SemaphoreType.DMA, pltpu.SemaphoreType.DMA, pltpu.SemaphoreType.DMA((2,))],
-        compiler_params=pltpu.CompilerParams(collective_id=cid, has_side_effects=True, vmem_limit_bytes=67043328),
-        name="scatter_grads",
-    )(grads.reshape(R // 2, 2, rows, 1024), small, last)
+        total = total + landing[d]
+    pair[0] = total
+    remote(pair.at[0], pair.at[1], sems.at[0], sems.at[1], r, 1 - t)
+    landed(pair.at[0], sems.at[0])
+    landed(pair.at[1], sems.at[1])
+    pair[0] = pair[0] + pair[1]
 
 
 HALO = 384
@@ -505,7 +507,7 @@
 class Grads:
     def __init__(self, out, buf, sems):
         self.out, self.buf, self.sems, self.count = out, buf, sems, 0
-        self.R = out.shape[0]
+        self.R = 2 * out.shape[0]
         self.n = 1024 // self.R
 
     def put(self, unit, kind, index, left, right, out=None):
@@ -519,9 +521,9 @@
             buf[:, c] = dot(left, right(c), TN).astype(BF16)
         by_cols(1024, cols)
         if kind == "in":
-            pairs = [(buf.at[s * n:(s + 1) * n], out.at[s, (unit + index) * n:(unit + index + 1) * n]) for s in range(R)]
+            pairs = [(buf.at[s * n:(s + 1) * n], out.at[s // 2, s % 2, (unit + index) * n:(unit + index + 1) * n]) for s in range(R)]
         else:
-            pairs = [(buf.at[s * 4 * n:(s + 1) * 4 * n], out.at[index * (R // 4) + s, unit * n:(unit + 4) * n]) for s in range(R // 4)]
+            pairs = [(buf.at[s * 4 * n:(s + 1) * 4 * n], out.at[(index * (R // 4) + s) // 2, (index * (R // 4) + s) % 2, unit * n:(unit + 4) * n]) for s in range(R // 4)]
         for src, dst in pairs:
             pltpu.make_async_copy(src, dst, self.sems.at[slot]).start()
         self.count += 1
@@ -1109,7 +1111,7 @@
     bufs, sems = reduce_scratch()
     return pl.pallas_call(
         functools.partial(middle_kernel, frames),
-        out_shape=[shape(count, 1024), shape(count, 1024), shape(count, 1024), shape(2, 1024), shape(96, 1024), shape(full.shape[0], FO2 * 1024 // full.shape[0], 1024, dtype=BF16), shape(full.shape[0], 4096 // full.shape[0], 1024, dtype=BF16)],
+        out_shape=[shape(count, 1024), shape(count, 1024), shape(count, 1024), shape(2, 1024), shape(96, 1024), shape(full.shape[0] // 2, 2, FO2 * 1024 // full.shape[0], 1024, dtype=BF16), shape(full.shape[0] // 2, 2, 4096 // full.shape[0], 1024, dtype=BF16)],
         in_specs=[whole()] * 5 + [anywhere()], out_specs=[whole()] * 5 + [anywhere()] * 2,
         scratch_shapes=[pltpu.VMEM((9, 1024, 1024), BF16), pltpu.VMEM((count, 1024), BF16), pltpu.VMEM((count, 1024), BF16), pltpu.VMEM((count, 1024), BF16),
                         pltpu.VMEM((4, count, 1024), BF16), pltpu.VMEM((4, count, 1024), BF16), pltpu.VMEM((4, count, 1024), F32),
@@ -1210,20 +1212,19 @@
     )(dn, y, sums, totals, c1, c2, u, x2, g3, o, params, seg, full, grads)
 
 
-BLOCKS_E = tuple([(QKV, "in", j) for j in range(3)] + [(FO1, "out", j) for j in range(4)] + [(FI1, "in", j) for j in range(4)])
-
-
-def rear_kernel(halo, tokens, x1, z1, g2, dq, dk, dv, params, full, *refs):
+BLOCKS_E = tuple([(QKV, "in", j) for j in range(3)])
+BLOCKS_F = tuple([(FO1, "out", j) for j in range(4)] + [(FI1, "in", j) for j in range(4)])
+
+
+def rear_kernel(halo, x1, g2, dq, dk, dv, params, full, *refs):
     if halo:
-        beside, grads_in, dtok, small, grads, wbuf, a, d, dz, zbuf, hbuf, stage, da, back, got, wsem, zsem, gsem, esem = refs
+        beside, grads_in, g1, small, grads, wbuf, a, stage, da, back, got, wsem, gsem, esem = refs
     else:
-        grads_in, dtok, small, grads, wbuf, a, d, dz, zbuf, hbuf, stage, da, wsem, zsem, gsem = refs
+        grads_in, g1, small, grads, wbuf, a, stage, da, wsem, gsem = refs
     w = Weights(full, wbuf, wsem, BLOCKS_E)
     w.start()
     g = Grads(grads, stage, gsem)
-    count = tokens.shape[0]
-    for j in range(2):
-        pltpu.make_async_copy(z1.at[:, j * 1024:(j + 1) * 1024], zbuf.at[j], zsem.at[j]).start()
+    count = x1.shape[0]
     small[...] = jnp.zeros_like(small)
     own = 0
     if halo:
@@ -1266,7 +1267,7 @@
                 buf[:, c] = (dot(a[...], grad[mine, c], TN) + dot(beside[...], grad[pl.ds(other, HALO), c], TN)).astype(BF16)
             by_cols(1024, cols)
             for s in range(R):
-                pltpu.make_async_copy(buf.at[s * n:(s + 1) * n], grads.at[s, (QKV + j) * n:(QKV + j + 1) * n], gsem.at[slot]).start()
+                pltpu.make_async_copy(buf.at[s * n:(s + 1) * n], grads.at[s // 2, s % 2, (QKV + j) * n:(QKV + j + 1) * n], gsem.at[slot]).start()
             g.count += 1
         landed(back, esem.at[0])
         landed(got, esem.at[1])
@@ -1285,70 +1286,208 @@
         v = da[rows]
         small[16:24] += eight(v * vhat)
         small[24:32] += eight(v)
-        both = g2[rows] + norm_back(v, params[GAIN + 1:GAIN + 2], vhat, rs)
-        dtok[rows] = both
-        half = (0.5 * both).astype(BF16)
-        d[rows] = half
-        small[32:40] += eight(half.astype(F32))
-        vhat, _ = normalized(tokens[rows].astype(F32))
-        a[rows] = (vhat * params[GAIN:GAIN + 1] + params[SHIFT:SHIFT + 1]).astype(BF16)
+        g1[rows] = g2[rows] + norm_back(v, params[GAIN + 1:GAIN + 2], vhat, rs)
     by_rows(count, 256, resid)
-    w.wait(3, 4, 5, 6)
-    for j in range(4):
-        slot = j % 2
-        pltpu.make_async_copy(zbuf.at[slot], zbuf.at[slot], zsem.at[slot]).wait()
-
-        def cols(c, j=j, slot=slot):
-            v = zbuf[slot, :, c]
-            s = sigmoid(v)
-            hbuf[:, c] = (v * s).astype(BF16)
-            dh = (dot(d[...], wbuf[3 + j, c, :], NT) * (s * (1.0 + v * (1.0 - s)))).astype(BF16)
-            dz[j, :, c] = dh
-            small[40 + 8 * j:48 + 8 * j, c] += eight(dh.astype(F32))
-        by_cols(1024, cols)
-        if j + 2 < 4:
-            pltpu.make_async_copy(z1.at[:, (j + 2) * 1024:(j + 3) * 1024], zbuf.at[slot], zsem.at[slot]).start()
-        g.put(FO1, "out", j, hbuf[...], lambda c: d[:, c])
-    for j in range(4):
-        g.put(FI1, "in", j, a[...], lambda c, j=j: dz[j, :, c])
-    w.wait(7, 8, 9, 10)
-
-    def inward(c):
-        acc = dot(dz[0], wbuf[7, c, :], NT)
-        for j in range(1, 4):
-            acc = acc + dot(dz[j], wbuf[7 + j, c, :], NT)
-        da[:, c] = acc
-    by_cols(1024, inward)
-
-    def last(rows):
-        vhat, rs = normalized(tokens[rows].astype(F32))
-        v = da[rows]
-        small[72:80] += eight(v * vhat)
-        small[80:88] += eight(v)
-        dtok[rows] = dtok[rows] + norm_back(v, params[GAIN:GAIN + 1], vhat, rs)
-    by_rows(count, 256, last)
     g.finish()
 
 
-def rear(tokens, x1, z1, g2, dq, dk, dv, params, full, beside, grads, cid):
-    count = tokens.shape[0]
+def rear(x1, g2, dq, dk, dv, params, full, beside, grads, cid):
+    count = x1.shape[0]
     halo = beside is not None
-    scratch = [pltpu.VMEM((11, 1024, 1024), BF16), pltpu.VMEM((count, 1024), BF16), pltpu.VMEM((count, 1024), BF16), pltpu.VMEM((4, count, 1024), BF16),
-               pltpu.VMEM((2, count, 1024), F32), pltpu.VMEM((count, 1024), BF16), pltpu.VMEM((2, 1024, 1024), BF16), pltpu.VMEM((count, 1024), F32)]
+    scratch = [pltpu.VMEM((3, 1024, 1024), BF16), pltpu.VMEM((count, 1024), BF16), pltpu.VMEM((2, 1024, 1024), BF16), pltpu.VMEM((count, 1024), F32)]
     if halo:
         scratch += [pltpu.VMEM((HALO, 1024), BF16), pltpu.VMEM((HALO, 1024), BF16)]
-    scratch += [pltpu.SemaphoreType.DMA((11,)), pltpu.SemaphoreType.DMA((2,)), pltpu.SemaphoreType.DMA((2,))]
+    scratch += [pltpu.SemaphoreType.DMA((3,)), pltpu.SemaphoreType.DMA((2,))]
     if halo:
         scratch.append(pltpu.SemaphoreType.DMA((2,)))
-    specs = [whole(), whole(), anywhere()] + [whole()] * 5 + [anywhere()] + ([whole()] if halo else []) + [anywhere()]
+    specs = [whole()] * 6 + [anywhere()] + ([whole()] if halo else []) + [anywhere()]
     return pl.pallas_call(
         functools.partial(rear_kernel, halo),
-        out_shape=[shape(count, 1024), shape(88, 1024), shape(*grads.shape, dtype=BF16)],
+        out_shape=[shape(count, 1024), shape(32, 1024), shape(*grads.shape, dtype=BF16)],
         in_specs=specs, out_specs=[whole(), whole(), anywhere()], scratch_shapes=scratch,
         input_output_aliases={len(specs) - 1: 2},
         compiler_params=pltpu.CompilerParams(vmem_limit_bytes=VMEM_LIMIT, **({"collective_id": cid, "has_side_effects": True} if halo else {})),
         name="rear",
-    )(tokens, x1, z1, g2, dq, dk, dv, params, full, *((beside,) if halo else ()), grads)
+    )(x1, g2, dq, dk, dv, params, full, *((beside,) if halo else ()), grads)
+
+
+class Last:
+    def __init__(self, full, params, tokens, g1, z1, dtok, small, grads, scratch):
+        wbuf, self.a, self.d, self.dz, self.zbuf, self.hbuf, stage, self.da, wsem, self.zsem, gsem = scratch
+        self.w = Weights(full, wbuf, wsem, BLOCKS_F[:4])
+        self.w2 = Weights(full, wbuf, wsem, BLOCKS_F[4:])
+        self.g = Grads(grads, stage, gsem)
+        self.params, self.tokens, self.g1, self.z1, self.dtok, self.small = params, tokens, g1, z1, dtok, small
+
+    @staticmethod
+    def scratch(count):
+        sem, vmem = pltpu.SemaphoreType.DMA, pltpu.VMEM
+        return [vmem((4, 1024, 1024), BF16), vmem((count, 1024), BF16), vmem((count, 1024), BF16), vmem((4, count, 1024), BF16), vmem((2, count, 1024), F32),
+                vmem((count, 1024), BF16), vmem((2, 1024, 1024), BF16), vmem((count, 1024), F32), sem((4,)), sem((2,)), sem((2,))]
+
+    def z_copy(self, j):
+        return pltpu.make_async_copy(self.z1.at[:, j * 1024:(j + 1) * 1024], self.zbuf.at[j % 2], self.zsem.at[j % 2])
+
+    def start(self):
+        self.w.start()
+        self.z_copy(0).start()
+        self.z_copy(1).start()
+
+    def prepare(self):
+        self.small[...] = jnp.zeros_like(self.small)
+
+        def rows(rows):
+            half = (0.5 * self.g1[rows]).astype(BF16)
+            self.d[rows] = half
+            self.small[0:8] += eight(half.astype(F32))
+        by_rows(self.d.shape[0], 256, rows)
+        norm_tokens(self.tokens, self.params, self.a)
+
+    def hidden(self, j):
+        self.w.wait(j)
+        self.z_copy(j).wait()
+        v = self.zbuf[j % 2]
+        s = sigmoid(v)
+        self.hbuf[...] = (v * s).astype(BF16)
+        dh = (dot(self.d[...], self.w.buf[j], NT) * (s * (1.0 + v * (1.0 - s)))).astype(BF16)
+        self.dz[j] = dh
+        self.small[8 + 8 * j:16 + 8 * j] += eight(dh.astype(F32))
+        self.w2.start(j)
+        if j + 2 < 4:
+            self.z_copy(j + 2).start()
+
+    def outward(self, j):
+        self.g.put(FO1, "out", j, self.hbuf[...], lambda c: self.d[:, c])
+
+    def inward(self, j):
+        self.g.put(FI1, "in", j, self.a[...], lambda c: self.dz[j, :, c])
+
+    def through(self, j):
+        self.w2.wait(j)
+        part = dot(self.dz[j], self.w2.buf[j], NT)
+        self.da[...] = part if j == 0 else self.da[...] + part
+
+    def end(self):
+        def rows(rows):
+            vhat, rs = normalized(self.tokens[rows].astype(F32))
+            v = self.da[rows]
+            self.small[40:48] += eight(v * vhat)
+            self.small[48:56] += eight(v)
+            self.dtok[rows] = self.g1[rows] + norm_back(v, self.params[GAIN:GAIN + 1], vhat, rs)
+        by_rows(self.d.shape[0], 256, rows)
+
+
+def plain_last_kernel(tokens, g1, z1, params, full, grads_in, dtok, small, grads, *scratch):
+    f = Last(full, params, tokens, g1, z1, dtok, small, grads, scratch)
+    f.start()
+    f.prepare()
+    for j in range(4):
+        f.hidden(j)
+        f.outward(j)
+    for j in range(4):
+        f.inward(j)
+    for j in range(4):
+        f.through(j)
+    f.end()
+    f.g.finish()
+
+
+def plain_last(tokens, g1, z1, params, full, grads):
+    count = tokens.shape[0]
+    return pl.pallas_call(
+        plain_last_kernel,
+        out_shape=[shape(count, 1024), shape(56, 1024), shape(*grads.shape, dtype=BF16)],
+        in_specs=[whole(), whole(), anywhere(), whole(), anywhere(), anywhere()], out_specs=[whole(), whole(), anywhere()],
+        scratch_shapes=Last.scratch(count), input_output_aliases={5: 2},
+        compiler_params=pltpu.CompilerParams(vmem_limit_bytes=VMEM_LIMIT),
+        name="last",
+    )(tokens, g1, z1, params, full, grads)
+
+
+def last_kernel(units, ready, first, tokens, g1, z1, params, full, rows_in, share, grads_in, dtok, out, rows_out, late_out, share_out, grads,
+                small, lv, lout, sown, sv, sx, town, tv, tx, lsem, sload, ssend, srecv, sxsem, tsend, trecv, txsem, *scratch):
+    r, t, c, y, z = place()
+    R = lax.axis_size("rows")
+    n = len(Last.scratch(tokens.shape[0]))
+    f = Last(full, params, tokens, g1, z1, dtok, small, grads, scratch[:n])
+    f.start()
+    cs = pltpu.make_async_copy(rows_in, sown, sload.at[0])
+    cs.start()
+    lc = pltpu.make_async_copy(share, lv.at[0], lsem.at[0])
+    lc.start()
+    greet([(lax.rem(r + d, R), t) for d in range(1, R)] + [(r, 1 - t)])
+    s = Scatter(grads, out, units, ready, first, scratch[n:])
+    s.begin()
+    cs.wait()
+    spread(sown, sv, ssend, srecv)
+    lc.wait()
+    pieces = share.shape[0] // 16
+
+    def piece(i):
+        @pl.when((i >= 2) & (i < pieces + 2))
+        def _():
+            rows = pl.ds(pl.multiple_of((i - 2) * 16, 16), 16)
+            remote(lv.at[0, rows], lv.at[1, rows], lsem.at[1], lsem.at[2], r, 1 - t)
+
+    def late_rows():
+        town[...] = jnp.zeros_like(town)
+        sums = [jnp.sum(small[8 * i:8 * i + 8], axis=0, keepdims=True) for i in range(7)]
+        for to in range(R):
+            pair = slice(to // 2 * 128, to // 2 * 128 + 128)
+            for row, which in ((0, 0), (1, 5), (2, 6)):
+                town[to, row:row + 1] = sums[which][:, pair]
+            for half in range(2):
+                at = (to % 4) * 256 + half * 128
+                town[to, 3 + half:4 + half] = sums[1 + to // 4][:, at:at + 128]
+        spread(town, tv, tsend, trecv)
+
+    work = {(0, 2): f.prepare, (5, 0): lambda: f.inward(0), (5, 2): lambda: f.inward(1), (6, 0): lambda: f.inward(2), (6, 2): lambda: f.inward(3), (7, 0): f.g.finish,
+            (7, 1): lambda: f.through(0), (7, 3): lambda: f.through(1), (8, 1): lambda: f.through(2), (8, 3): lambda: f.through(3), (9, 1): f.end, (10, 1): late_rows}
+    for j in range(4):
+        work[1 + j, 0] = lambda j=j: f.hidden(j)
+        work[1 + j, 2] = lambda j=j: f.outward(j)
+    for step in range(11):
+        piece(step)
+        for quarter in range(4):
+            s.part(step, quarter)
+            if (step, quarter) in work:
+                work[step, quarter]()
+
+    def rest(step):
+        piece(step)
+        s.tick(step)
+    loop(units + s.LAG, rest, 11)
+    gathered(sown, sv, sx, sxsem, ssend, srecv)
+    gathered(town, tv, tx, txsem, tsend, trecv)
+    done = [pltpu.make_async_copy(sx.at[0], rows_out, sload.at[0]), pltpu.make_async_copy(tx.at[0], late_out, sload.at[1])]
+    landed(lv.at[0], lsem.at[1])
+    landed(lv.at[1], lsem.at[2])
+    lout[...] = lv[0].astype(F32) + lv[1].astype(F32)
+    done.append(pltpu.make_async_copy(lout, share_out, lsem.at[0]))
+    for copy in done:
+        copy.start()
+    s.finish()
+    for copy in done:
+        copy.wait()
+
+
+def last(tokens, g1, z1, params, full, rows, share, grads, cid):
+    count, R = tokens.shape[0], full.shape[0]
+    units, ready = FO2, FO2 - QKV
+    sem, vmem = pltpu.SemaphoreType.DMA, pltpu.VMEM
+    late = (8, 128)
+    return pl.pallas_call(
+        functools.partial(last_kernel, units, ready, QKV),
+        out_shape=[shape(count, 1024), shape(units * UNIT, 1024), shape(*rows.shape[1:]), shape(*late), shape(*share.shape), shape(*grads.shape, dtype=BF16)],
+        in_specs=[whole(), whole(), anywhere(), whole()] + [anywhere()] * 4, out_specs=[whole()] + [anywhere()] * 5,
+        scratch_shapes=[vmem((56, 1024), F32), vmem((2,) + share.shape, BF16), vmem(share.shape, F32),
+                        vmem(rows.shape, F32), vmem((R - 1,) + rows.shape[1:], F32), vmem((2,) + rows.shape[1:], F32),
+                        vmem((R,) + late, F32), vmem((R - 1,) + late, F32), vmem((2,) + late, F32),
+                        sem((3,)), sem((2,)), sem, sem, sem((2,)), sem, sem, sem((2,))] + Last.scratch(count) + Scatter.scratch(units),
+        input_output_aliases={7: 5},
+        compiler_params=pltpu.CompilerParams(vmem_limit_bytes=VMEM_LIMIT, collective_id=cid, has_side_effects=True),
+        name="last",
+    )(tokens, g1, z1, params, full, rows, share, grads)
 
 
 def pack_rows(gains, shifts, ffn_bias, conv_kernel, rel_table):
@@ -1382,10 +1521,8 @@
     return jnp.pad(flat, ((0, 0), (0, 8 * 384 - 34 * n))).reshape(R, 8, 384)
 
 
-def shard_rows(small, R):
-    n = 1024 // R
-    rows = small.reshape(-1)[: 34 * n].reshape(34, n)
-    return (rows[:6], rows[6:20], rows[20:28].reshape(2, 4 * n), rows[28:33], rows[33])
+def split_rows(rows):
+    return (rows[:6], rows[6:20], rows[20:28].reshape(2, -1), rows[28:33], rows[33])
 
 
 def pack_weights(weights):
@@ -1448,29 +1585,40 @@
         o, lse = attend(q, k, v, windows, segq, segk, off)
     x2, c1, c2, u, y, sums = convolve(x1, o, params, segx, full, 3)
     output, g3, dn, totals, small_d, grads, grads_b = middle(x2, y, sums, cotangent.reshape(count, width), params, full, frames, 4)
-    last = lax.psum_scatter(grads_b, "rows", scatter_dimension=0, tiled=False)
+    share = lax.psum_scatter(grads_b.reshape(R, -1, 1024), "rows", scatter_dimension=0, tiled=False)
     g2, dob, small_c, grads = convolve_back(dn, y, sums, totals, c1, c2, u, x2, g3, o, params, segx, full, grads, frames, 5)
     dq, dk, dv, dtable = attend_back(q, k, v, windows, segq, segk, off, o, lse, dob)
     if not links:
         dk = lax.psum_scatter(dk, "tm", scatter_dimension=0, tiled=True)
         dv = lax.psum_scatter(dv, "tm", scatter_dimension=0, tiled=True)
-    dtok, small_e, grads = rear(tok, x1, z1, g2, dq, dk, dv, params, full, beside, grads, 6)
+    g1, small_e, grads = rear(x1, g2, dq, dk, dv, params, full, beside, grads, 6)
 
     rel = lax.dot_general(dtable.reshape(HEADS, length), hot, (((1,), (1,)), ((), ())), precision=HIGH).reshape(1, 1024)
     d = jnp.sum(small_d.reshape(12, 8, 1024), axis=1)
     c = jnp.sum(small_c.reshape(10, 8, 1024), axis=1)
-    e = jnp.sum(small_e.reshape(11, 8, 1024), axis=1)
+    e = jnp.sum(small_e.reshape(4, 8, 1024), axis=1)
+    if links:
+        l = jnp.zeros((7, 1024), F32)
+    else:
+        dtok, small_l, grads = plain_last(tok, g1, z1, params, full, grads)
+        l = jnp.sum(small_l.reshape(7, 8, 1024), axis=1)
     rows = jnp.concatenate([
-        e[9:10], e[2:3], c[7:8], d[7:8], d[0:1], d[10:11],
-        e[10:11], e[3:4], c[8:9], d[8:9], d[1:2], d[11:12], e[4:5], e[0:2], c[9:10], c[5:7], d[9:10], d[2:3],
-        e[5:9], d[3:7], c[0:5], rel])
+        l[5:6], e[2:3], c[7:8], d[7:8], d[0:1], d[10:11],
+        l[6:7], e[3:4], c[8:9], d[8:9], d[1:2], d[11:12], l[0:1], e[0:2], c[9:10], c[5:7], d[9:10], d[2:3],
+        l[1:5], d[3:7], c[0:5], rel])
+    slots = slot_rows(rows, R)
     if links:
-        shard, small, last = scatter_call(grads, slot_rows(rows, R), last, 1)
+        dtok, shard, small, late, share, _ = last(tok, g1, z1, params, full, slots, share, grads, 1)
     else:
-        shard = lax.psum(lax.psum_scatter(grads, "rows", scatter_dimension=0, tiled=False), "tm").astype(F32)
-        small = lax.psum(lax.psum_scatter(slot_rows(rows, R), "rows", scatter_dimension=0, tiled=False), "tm")
-        last = lax.psum(last, "tm").astype(F32)
-    return (output.reshape(tokens.shape), dtok.reshape(tokens.shape)) + unpack_shard(shard, weights[:7]) + (last,) + shard_rows(small, R)
+        shard = lax.psum(lax.psum_scatter(grads.reshape(R, -1, 1024), "rows", scatter_dimension=0, tiled=False), "tm").astype(F32)
+        small = lax.psum(lax.psum_scatter(slots, "rows", scatter_dimension=0, tiled=False), "tm")
+        share = lax.psum(share, "tm").astype(F32)
+    rows = small.reshape(-1)[: 34 * (1024 // R)].reshape(34, 1024 // R)
+    if links:
+        odd = lax.rem(lax.axis_index("rows"), 2) == 1
+        mine = jnp.where(odd, late[0:3, 64:], late[0:3, :64])
+        rows = jnp.concatenate([mine[1:2], rows[1:6], mine[2:3], rows[7:12], mine[0:1], rows[13:20], late[3:5].reshape(4, 64), rows[24:]])
+    return (output.reshape(tokens.shape), dtok.reshape(tokens.shape)) + unpack_shard(shard, weights[:7]) + (share,) + split_rows(rows)
 
 
 def solution(mesh):

time: 689 us -> 679 us (0.985)
  Pallas kernels: 621 us -> 602 us
    pallas_call x1, Pallas kernels: 51.4 us -> 25.9 us  [rear(): pl.pallas_call(functools.partial(rear_kernel, halo), out_shape=[shape(cou...]
    pallas_call x1, Pallas kernels: 197 us -> 204 us  [last(): pl.pallas_call(functools.partial(last_kernel, units, ready, QKV), out_sha...]
  transfers between devices with their start and end apart: 1 -> 1, of which waited for: 0 -> 0; matrix products, arithmetic and copies ran while one was open for 1% -> 2% of each run, Pallas kernels for 17% -> 13%
where the time goes in v2:
time: 679 us; the launch traced here: 675 us
  Pallas kernels  602 us (89%)
  local copies, waits for them, and re-layouts  44.1 us (6%)
  between operations  14.9 us (2%)
    pallas_call x1, Pallas kernels, front(): pl.pallas_call(functools.partial(front_kernel, tuple(blocks)), out_shape=...  214 us
    pallas_call x1, Pallas kernels, last(): pl.pallas_call(functools.partial(last_kernel, units, ready, QKV), out_sha...  204 us
    pallas_call x1, Pallas kernels, middle(): pl.pallas_call(functools.partial(middle_kernel, frames), out_shape=[shape...  63 us
    pallas_call x1, Pallas kernels, convolve_back(): pl.pallas_call(functools.partial(convolve_back_kernel, frames), out_shape...  34.5 us
    pallas_call x1, Pallas kernels, convolve(): pl.pallas_call(convolve_kernel, out_shape=[shape(count, 1024), shape(coun...  30.7 us
    pallas_call x1, Pallas kernels, attend_back(): pl.pallas_call(functools.partial(attend_back_kernel, 1.0 / math.sqrt(128)...  30.4 us
    pallas_call x1, Pallas kernels, rear(): pl.pallas_call(functools.partial(rear_kernel, halo), out_shape=[shape(cou...  25.9 us
  transfers between devices with their start and end apart: 1, of which 0 were waited for; matrix products, arithmetic and copies ran while one was open for 2% of the time, Pallas kernels for 13%

profile of v2, /device:TPU:0, one launch (start us, length us, event | category | flops | bytes accessed | tf_op | source)
XLA Modules:
  0.0 674.8 jit_solution(7655850243447366065)
XLA Ops:
  7.2 1.3 fusion.7
  8.5 0.8 slice.161
  9.3 0.7 reshape.164
  10.0 5.4 all_gather.3
  15.4 1.5 copy.41.refs_11_.segq
  17.6 0.8 broadcast_in_dim.45.seg
  19.1 0.6 broadcast_in_dim.41
  19.8 0.9 convert_convert_fusion.refs_10_
  20.8 3.0 concatenate.72
  23.8 0.7 maximum_maximum_fusion.refs_0_
  24.5 213.8 %front.1 = (bf16[16,1472,1024]{2,1,0:T(8,128)(2,1)}, f32[40,1024]{1,0:T(8,128)}, f32[512,1024]{1,0:T(8,128)}, f32[512,4096]{1,0:T(8,128)}, bf16[512,1024]{1,0:T(...) custom-call(bf16[48,128]{1,0:T(8,128)(2,1)} %maximum_maximum_fusion., ...), custom_call_target="tpu_custom_call" | custom-call | tf_op jit(solution)/shard_map/front/pallas_call | solution.py:759
  238.3 30.7 %convolve.1 = (f32[512,1024]{1,0:T(8,128)}, f32[512,1024]{1,0:T(8,128)}, f32[512,1024]{1,0:T(8,128)}, f32[528,1024]{1,0:T(8,128)}, f32[512,1024]{1,0:T(8,128)}, /*index=5*/f32[2,1024]{1,0:T(2,128)}) custom-call(f32[512,1024]{1,0:T(8,128)} %get-tuple-element.55.x1, f32[512,1024]{1,0:T(8,128)} %get-tuple-element.56.o, f32[40,1024]{1,0:T(8,128)} %get-tuple-element.57.params, ...), custom_call_target="tpu_custom_call" | custom-call | tf_op jit(solution)/shard_map/convolve/pallas_call | solution.py:975
  269.0 63.0 %middle.1 = (f32[512,1024]{1,0:T(8,128)}, f32[512,1024]{1,0:T(8,128)}, f32[512,1024]{1,0:T(8,128)}, f32[2,1024]{1,0:T(2,128)}, f32[96,1024]{1,0:T(8,128)}, /*ind...) custom-call(f32[512,1024]{1,0:T(8,128)} %get-tuple-element.59.x2, f32[512,1024]{1,0:T(8,128)} %get-tuple-element.60.y, ...), custom_call_target="tpu_custom_call" | custom-call | tf_op jit(solution)/shard_map/middle/pallas_call | solution.py:1112
  332.1 34.5 %convolve_back.1 = (f32[512,1024]{1,0:T(8,128)}, bf16[512,1024]{1,0:T(8,128)(2,1)}, f32[80,1024]{1,0:T(8,128)}, bf16[8,2,1216,1024]{3,2,1,0:T(8,128)(2,1)}) custom-call(f32[512,1024]{1,0:T(8,128)} %get-tuple-element.63.dn, f32[512,1024]{1,0:T(8,128)} %get-tuple-element.60.y, f32[2,1024]{1,0:T(2,128)} %get-tuple-element.61.sums, ...), custom_call_target="tpu_custom_call", output_to_operand_aliasing={{3}: (13, {})} | custom-call | tf_op jit(solution)/shard_map/convolve_back/pallas_call | solution.py:1202
  366.6 1.1 bitcast_reduce_fusion.1
  368.9 1.5 reshape.170.window
  370.4 1.1 bitcast_reduce_fusion
  372.8 0.7 concatenate.92
  373.5 30.4 %attend_back.1 = (bf16[512,1024]{1,0:T(8,128)(2,1)}, bf16[896,1024]{1,0:T(8,128)(2,1)}, bf16[896,1024]{1,0:T(8,128)(2,1)}, f32[8,1,1920]{2,1,0:T(1,128)}) custom-call(s32[1]{0:T(128)} %bitcast.8.off, bf16[512,1024]{1,0:T(8,128)(2,1)} %get-tuple-element.71.q, bf16[896,1024]{1,0:T(8,128)(2,1)} %get-tuple-element.72.k, bf16[896,1024]{1,0:T(8,128)(2,1)} %get-tuple-element.73.v, ...), custom_call_target="tpu_custom_call" | custom-call | tf_op jit(solution)/shard_map/attend_back/pallas_call | solution.py:890
  403.8 1.4 fusion
  405.2 0.7 concatenate.94
  405.9 25.9 %rear.1 = (f32[512,1024]{1,0:T(8,128)}, f32[32,1024]{1,0:T(8,128)}, bf16[8,2,1216,1024]{3,2,1,0:T(8,128)(2,1)}) custom-call(f32[512,1024]{1,0:T(8,128)} %get-tuple-element.55.x1, f32[512,1024]{1,0:T(8,128)} %get-tuple-element.70.g2, bf16[512,1024]{1,0:T(8,128)(2,1)} %get-tuple-element.77.dq, ...), custom_call_target="tpu_custom_call", output_to_operand_aliasing={{2}: (8, {})} | custom-call | tf_op jit(solution)/shard_map/rear/pallas_call | solution.py:1304
  431.9 0.9 bitcast_reduce_fusion.2
  433.1 1.1 slice_reduce_fusion
  435.0 0.8 concatenate.93
  435.8 0.8 concatenate.89
  436.8 0.8 constant_dynamic-update-slice_fusion.2
  437.5 0.7 constant_dynamic-update-slice_fusion
  438.3 0.7 concatenate.96
  439.4 0.7 copy.55
  440.1 203.8 %last.1 = (f32[512,1024]{1,0:T(8,128)}, f32[1216,1024]{1,0:T(8,128)}, f32[8,384]{1,0:T(8,128)}, f32[8,128]{1,0:T(8,128)}, f32[256,1024]{1,0:T(8,128)}, /*index=5*/bf16[8,2,1216,1024]{3,2,1,0:T(8,128)(2,1)}) custom-call(bf16[512,1024]{1,0:T(8,128)(2,1)} %bitcast.48, f32[512,1024]{1,0:T(8,128)} %get-tuple-element.82.g1, ...), custom_call_target="tpu_custom_call", output_to_operand_aliasing={{5}: (7, {})} | custom-call | tf_op jit(solution)/shard_map/last/pallas_call | solution.py:1479
  643.9 0.7 slice.199
  644.6 0.8 slice_select_fusion
  645.4 0.7 reshape.191
  646.2 0.8 slice.193
  647.5 1.1 slice.187
  648.6 1.9 fusion.5
  650.5 1.2 slice.185
  651.7 3.1 fusion.4
  655.5 0.7 reshape.190
  656.1 0.8 copy.53
  657.0 1.0 copy.54
  658.5 1.3 copy.56
  659.9 1.0 copy.52
  662.1 1.3 copy.88
  663.5 1.0 copy-done.1
  664.5 1.3 copy.89
  666.4 1.0 copy.90
  (82 shorter events, 9.1 us)
Async XLA Ops:
  7.2 432.9 %reduce-scatter.2.cloned.1.call-start = ((), (), s32[]{:S(2)}) async-start(), calls=%async_computation.1 | async-start | bytes 8912896 | tf_op jit(solution)/shard_map/reduce_scatter | solution.py:1588
  19.8 1.0 copy-start.6
  367.7 0.6 copy-start.3
  371.5 0.6 copy-start.4
  372.2 0.6 copy-start.5
  658.5 3.6 copy-start
  662.1 2.3 copy-start.1
  664.5 2.0 copy-start.2
Sparse Core Ops, SparseCore 0:
  332.2 102.7 reduce-scatter.1

commit v3 on v2

--- a/solution.py
+++ b/solution.py
@@ -219,7 +219,7 @@
     def __init__(self, grads, out, units, ready, first, scratch):
         self.grads, self.out, self.units, self.ready, self.first = grads, out, units, ready, first
         (self.own, self.obuf, self.cv, self.xv, self.yv, self.zv, self.fv,
-         self.load, self.store, self.cr, self.xr, self.yr, self.zr, self.fr, self.core, self.snd, self.free) = scratch
+         self.load, self.storing, self.cr, self.xr, self.yr, self.zr, self.fr, self.core, self.snd, self.free) = scratch
         self.r, self.t, self.c, self.y, self.z = place()
 
     @classmethod
@@ -232,12 +232,14 @@
     def ring(self, unit):
         return lax.rem(unit, self.RING)
 
-    def rows_of(self, unit):
+    def number(self, unit):
         late = self.units - self.ready
         after = unit - self.ready
         late_unit = after + late // 2 - jnp.where(after >= late // 2, late, 0)
-        number = jnp.where(unit < self.ready, unit + self.first, late_unit)
-        return pl.ds(pl.multiple_of(number * UNIT, UNIT), UNIT)
+        return jnp.where(unit < self.ready, unit + self.first, late_unit)
+
+    def rows_of(self, unit):
+        return pl.ds(pl.multiple_of(self.number(unit) * UNIT, UNIT), UNIT)
 
     def mine(self):
         return pl.ds(pl.multiple_of(self.t * S_EDGE, 16), S_PLANE)
@@ -339,8 +341,25 @@
         at = self.ring(unit)
         remote(self.at_z(unit, self.z), self.fv.at[at], self.snd.at[at, 4], self.fr.at[unit], self.r, 1 - self.t)
 
-    def store_copy(self, unit):
-        return pltpu.make_async_copy(self.obuf.at[lax.rem(unit, 2)], self.out.at[self.rows_of(unit)], self.store.at[lax.rem(unit, 2)])
+    def store(self, unit):
+        number, slot, first = self.number(unit), lax.rem(unit, 2), 0
+        for out in self.out:
+            rows, cols = out.shape
+            count = rows * cols // (UNIT * 1024)
+
+            @pl.when((number >= first) & (number < first + count))
+            def _(out=out, first=first, rows=rows):
+                at = number - first
+                if rows == UNIT:
+                    dst = out.at[:, pl.ds(pl.multiple_of(at * 1024, 1024), 1024)]
+                else:
+                    dst = out.at[pl.ds(pl.multiple_of(at * UNIT, UNIT), UNIT)]
+                pltpu.make_async_copy(self.obuf.at[slot], dst, self.storing.at[slot]).start()
+            first += count
+
+    def stored(self, unit):
+        slot = lax.rem(unit, 2) if not isinstance(unit, int) else unit % 2
+        landed(self.obuf.at[slot], self.storing.at[slot])
 
     def conclude(self, unit):
         at = self.ring(unit)
@@ -349,13 +368,13 @@
 
         @pl.when(unit >= 2)
         def _():
-            self.store_copy(unit - 2).wait()
+            self.stored(unit)
         obuf = self.obuf.at[lax.rem(unit, 2)]
         middle = pl.ds(S_EDGE, S_MIDDLE)
         obuf[middle] = cv[middle].astype(jnp.float32) + fv[pl.ds(pl.multiple_of(self.t * S_EDGE, 16), S_MIDDLE)].astype(jnp.float32)
         obuf[self.edge(self.t)] = cv[self.edge(self.t)].astype(jnp.float32)
         obuf[self.edge(1 - self.t)] = fv[pl.ds(pl.multiple_of((1 - self.t) * S_MIDDLE, 16), S_EDGE)].astype(jnp.float32)
-        self.store_copy(unit).start()
+        self.store(unit)
         landed(self.xv.at[at], self.snd.at[at, 0])
         landed(self.yv.at[at], self.snd.at[at, 1])
         for z in range(4):
@@ -414,7 +433,7 @@
 
     def finish(self):
         for unit in range(max(0, self.units - 2), self.units):
-            self.store_copy(unit).wait()
+            self.stored(unit)
         landed(self.grads.at[:, 0, 0:self.units * UNIT], self.core)
 
 
@@ -655,8 +674,8 @@
 def front_kernel(blocks, *refs):
     small, *refs = refs
     ws, refs = refs[:8], refs[8:]
-    (tokens, hot, segq, segk, full, params, x1, z1, q, k, v, beside, o, lse, windows, own, slab, slabs, table, strip, wbuf, a, h, zbuf,
-     load, keep, ssend, srecv, wsem, zsem, esem, *sems) = refs
+    (tokens, hot, segq, segrow, full, params, x1, z1, q, k, v, beside, o, lse, windows, segk, own, slab, slabs, table, strip, wbuf, a, h, zbuf,
+     load, keep, ssend, srecv, wsem, zsem, esem, idsem, *sems) = refs
     r, t, c, y, z = place()
     units, R, count = len(blocks), lax.axis_size("rows"), tokens.shape[0]
     copies = []
@@ -667,6 +686,8 @@
     cs = pltpu.make_async_copy(small, slab, keep)
     cs.start()
     greet([(lax.rem(r + d, R), t) for d in range(1, R)] + [(r, 1 - t)])
+    ids = segrow.at[:, pl.ds(pl.multiple_of((1 - t) * (count - HALO), 128), HALO)]
+    remote(ids, segk.at[:, pl.ds(pl.multiple_of(t * count, 128), HALO)], idsem.at[0], idsem.at[1], r, 1 - t)
     cs.wait()
     for d in range(1, R):
         remote(slab, slabs.at[r], ssend, srecv, lax.rem(r + d, R), t)
@@ -709,6 +730,9 @@
         f.mix(1, beside, None, k, other)
 
     def bias_rows():
+        landed(segrow.at[:, pl.ds(0, HALO)], idsem.at[0])
+        landed(segk.at[:, pl.ds(pl.multiple_of((1 - t) * count, 128), HALO)], idsem.at[1])
+        segk[:, pl.ds(pl.multiple_of(t * HALO, 128), count)] = segrow[...]
         for head in range(HEADS):
             table[head:head + 1] = params[REL:REL + 1, head * NB:(head + 1) * NB].astype(BF16)
         windows[...] = dot(table[...], hot[...])
@@ -748,7 +772,7 @@
         f.stored(slot)
 
 
-def front(small, weights, tokens, hot, segq, segk, cid):
+def front(small, weights, tokens, hot, segq, segrow, cid):
     length = hot.shape[1]
     count, R, blocks = tokens.shape[0], lax.axis_size("rows"), []
     near = count + HALO
@@ -760,14 +784,14 @@
         functools.partial(front_kernel, tuple(blocks)),
         out_shape=[shape(R, units * UNIT, 1024, dtype=BF16), shape(40, 1024), shape(count, 1024), shape(count, 4096), shape(count, 1024, dtype=BF16),
                    shape(near, 1024, dtype=BF16), shape(near, 1024, dtype=BF16), shape(HALO, 1024, dtype=BF16),
-                   shape(count, 1024), shape(HEADS, count, 128), shape(HEADS, length)],
-        in_specs=[anywhere()] * 9 + [whole()] * 4, out_specs=[anywhere(), whole(), whole(), anywhere()] + [whole()] * 7,
+                   shape(count, 1024), shape(HEADS, count, 128), shape(HEADS, length), shape(1, near, dtype=jnp.int32)],
+        in_specs=[anywhere()] * 9 + [whole()] * 4, out_specs=[anywhere(), whole(), whole(), anywhere()] + [whole()] * 8,
         scratch_shapes=[pltpu.VMEM((units * UNIT, 1024), BF16), pltpu.VMEM(small.shape, BF16), pltpu.VMEM((R,) + small.shape, BF16), pltpu.VMEM((HEADS, NB), BF16), pltpu.VMEM((QB, length), F32),
                         pltpu.VMEM((11, 1024, 1024), BF16), pltpu.VMEM((count, 1024), BF16), pltpu.VMEM((4, count, 1024), BF16), pltpu.VMEM((2, count, 1024), F32),
-                        sem((units,)), sem, sem, sem, sem((11,)), sem((2,)), sem((2,))] + Gather.scratch(units),
+                        sem((units,)), sem, sem, sem, sem((11,)), sem((2,)), sem((2,)), sem((2,))] + Gather.scratch(units),
         compiler_params=pltpu.CompilerParams(vmem_limit_bytes=VMEM_LIMIT, collective_id=cid, has_side_effects=True),
         name="front",
-    )(small, *weights, tokens, hot, segq, segk)
+    )(small, *weights, tokens, hot, segq, segrow)
 
 
 def plain_front_kernel(tokens, params, full, x1, z1, q, k, v, wbuf, a, h, zbuf, wsem, zsem):
@@ -1404,8 +1428,10 @@
     )(tokens, g1, z1, params, full, grads)
 
 
-def last_kernel(units, ready, first, tokens, g1, z1, params, full, rows_in, share, grads_in, dtok, out, rows_out, late_out, share_out, grads,
-                small, lv, lout, sown, sv, sx, town, tv, tx, lsem, sload, ssend, srecv, sxsem, tsend, trecv, txsem, *scratch):
+def last_kernel(units, ready, first, tokens, g1, z1, params, full, rows_in, share, grads_in, dtok, *refs):
+    out, refs = refs[:7], refs[7:]
+    (rows_out, late_out, share_out, grads,
+     small, lv, lout, sown, sv, sx, town, tv, tx, lsem, sload, ssend, srecv, sxsem, tsend, trecv, txsem, *scratch) = refs
     r, t, c, y, z = place()
     R = lax.axis_size("rows")
     n = len(Last.scratch(tokens.shape[0]))
@@ -1471,20 +1497,20 @@
         copy.wait()
 
 
-def last(tokens, g1, z1, params, full, rows, share, grads, cid):
+def last(tokens, g1, z1, params, full, rows, share, grads, shapes, cid):
     count, R = tokens.shape[0], full.shape[0]
     units, ready = FO2, FO2 - QKV
     sem, vmem = pltpu.SemaphoreType.DMA, pltpu.VMEM
     late = (8, 128)
     return pl.pallas_call(
         functools.partial(last_kernel, units, ready, QKV),
-        out_shape=[shape(count, 1024), shape(units * UNIT, 1024), shape(*rows.shape[1:]), shape(*late), shape(*share.shape), shape(*grads.shape, dtype=BF16)],
-        in_specs=[whole(), whole(), anywhere(), whole()] + [anywhere()] * 4, out_specs=[whole()] + [anywhere()] * 5,
+        out_shape=[shape(count, 1024)] + [shape(*dims) for dims in shapes] + [shape(*rows.shape[1:]), shape(*late), shape(*share.shape), shape(*grads.shape, dtype=BF16)],
+        in_specs=[whole(), whole(), anywhere(), whole()] + [anywhere()] * 4, out_specs=[whole()] + [anywhere()] * 11,
         scratch_shapes=[vmem((56, 1024), F32), vmem((2,) + share.shape, BF16), vmem(share.shape, F32),
                         vmem(rows.shape, F32), vmem((R - 1,) + rows.shape[1:], F32), vmem((2,) + rows.shape[1:], F32),
                         vmem((R,) + late, F32), vmem((R - 1,) + late, F32), vmem((2,) + late, F32),
                         sem((3,)), sem((2,)), sem, sem, sem((2,)), sem, sem, sem((2,))] + Last.scratch(count) + Scatter.scratch(units),
-        input_output_aliases={7: 5},
+        input_output_aliases={7: 11},
         compiler_params=pltpu.CompilerParams(vmem_limit_bytes=VMEM_LIMIT, collective_id=cid, has_side_effects=True),
         name="last",
     )(tokens, g1, z1, params, full, rows, share, grads)
@@ -1551,16 +1577,12 @@
     links = R == 16 and T == 2 and count == 512
     frames = R * T * count * packed_rows
     weights = (ffn1_in, ffn1_out, qkv_weight, attn_out, glu_in, conv_out, ffn2_in, ffn2_out)
-    seg_all = lax.all_gather(segment_ids, "tm", axis=1, tiled=True)[0]
-    seg_far = jnp.pad(seg_all, (HALO, HALO), constant_values=-1)
-    segx = lax.dynamic_slice_in_dim(seg_far, HALO + t * count - 8, count + 16)[:, None]
     segq = segment_ids.reshape(count, 1)
     if links:
         near, off = count + HALO, t * HALO
-        segk = lax.dynamic_slice_in_dim(seg_all, t * (count - HALO), near)[None]
     else:
         near, off = T * count, t * count
-        segk = seg_all[None]
+        segk = lax.all_gather(segment_ids, "tm", axis=1, tiled=True)
     length = 2 * near + QB
     places = np.clip(np.arange(length) - (near + QB), -MAXD, MAXD) + MAXD
     before, after = int(np.argmax(places > 0)), int(np.argmax(places >= 2 * MAXD))
@@ -1569,7 +1591,7 @@
     off = off.astype(jnp.int32).reshape(1)
     tok = tokens.reshape(count, width)
     if links:
-        full, params, x1, z1, q, k, v, beside, o, lse, windows = front(slab_rows(gains, shifts, ffn_bias, conv_kernel, rel_table), weights, tok, hot.astype(BF16), segq, segk, 0)
+        full, params, x1, z1, q, k, v, beside, o, lse, windows, segk = front(slab_rows(gains, shifts, ffn_bias, conv_kernel, rel_table), weights, tok, hot.astype(BF16), segq, segment_ids, 0)
         windows = windows.reshape(HEADS, 1, length)
     else:
         full = lax.all_gather(pack_weights(weights), "rows", axis=0)
@@ -1583,6 +1605,7 @@
         k = lax.all_gather(k, "tm", axis=0, tiled=True)
         v = lax.all_gather(v, "tm", axis=0, tiled=True)
         o, lse = attend(q, k, v, windows, segq, segk, off)
+    segx = lax.dynamic_slice_in_dim(jnp.pad(segk[0], (8, 8), constant_values=-1), off[0], count + 16)[:, None]
     x2, c1, c2, u, y, sums = convolve(x1, o, params, segx, full, 3)
     output, g3, dn, totals, small_d, grads, grads_b = middle(x2, y, sums, cotangent.reshape(count, width), params, full, frames, 4)
     share = lax.psum_scatter(grads_b.reshape(R, -1, 1024), "rows", scatter_dimension=0, tiled=False)
@@ -1608,9 +1631,11 @@
         l[1:5], d[3:7], c[0:5], rel])
     slots = slot_rows(rows, R)
     if links:
-        dtok, shard, small, late, share, _ = last(tok, g1, z1, params, full, slots, share, grads, 1)
+        dtok, *shards, small, late, share, _ = last(tok, g1, z1, params, full, slots, share, grads, [w.shape for w in weights[:7]], 1)
+        shards = tuple(shards)
     else:
         shard = lax.psum(lax.psum_scatter(grads.reshape(R, -1, 1024), "rows", scatter_dimension=0, tiled=False), "tm").astype(F32)
+        shards = unpack_shard(shard, weights[:7])
         small = lax.psum(lax.psum_scatter(slots, "rows", scatter_dimension=0, tiled=False), "tm")
         share = lax.psum(share, "tm").astype(F32)
     rows = small.reshape(-1)[: 34 * (1024 // R)].reshape(34, 1024 // R)
@@ -1618,7 +1643,7 @@
         odd = lax.rem(lax.axis_index("rows"), 2) == 1
         mine = jnp.where(odd, late[0:3, 64:], late[0:3, :64])
         rows = jnp.concatenate([mine[1:2], rows[1:6], mine[2:3], rows[7:12], mine[0:1], rows[13:20], late[3:5].reshape(4, 64), rows[24:]])
-    return (output.reshape(tokens.shape), dtok.reshape(tokens.shape)) + unpack_shard(shard, weights[:7]) + (share,) + split_rows(rows)
+    return (output.reshape(tokens.shape), dtok.reshape(tokens.shape)) + shards + (share,) + split_rows(rows)
 
 
 def solution(mesh):

time: 679 us -> 670 us (0.987)
    slice x4 -> x0, local copies, waits for them, and re-layouts: 7.25 us -> none  [unpack_shard(): shard[row:row + count].reshape(cols // 1024, n, 1024).transpose(1, 0, 2)]
    unnamed x40 -> x58, local copies, waits for them, and re-layouts: 9.39 us -> 15.7 us
  transfers between devices with their start and end apart: 1 -> 1, of which waited for: 0 -> 0; matrix products, arithmetic and copies ran while one was open for 2% -> 2% of each run, Pallas kernels for 13% -> 14%
where the time goes in v3:
time: 670 us; the launch traced here: 666 us
  Pallas kernels  603 us (90%)
  local copies, waits for them, and re-layouts  39.2 us (6%)
  between operations  14.8 us (2%)
  other arithmetic  7.43 us (1%)
    pallas_call x1, Pallas kernels, front(): pl.pallas_call(functools.partial(front_kernel, tuple(blocks)), out_shape=...  215 us
    pallas_call x1, Pallas kernels, last(): pl.pallas_call(functools.partial(last_kernel, units, ready, QKV), out_sha...  204 us
    pallas_call x1, Pallas kernels, middle(): pl.pallas_call(functools.partial(middle_kernel, frames), out_shape=[shape...  63 us
    pallas_call x1, Pallas kernels, convolve_back(): pl.pallas_call(functools.partial(convolve_back_kernel, frames), out_shape...  34.5 us
    pallas_call x1, Pallas kernels, convolve(): pl.pallas_call(convolve_kernel, out_shape=[shape(count, 1024), shape(coun...  30.7 us
    pallas_call x1, Pallas kernels, attend_back(): pl.pallas_call(functools.partial(attend_back_kernel, 1.0 / math.sqrt(128)...  30.4 us
    pallas_call x1, Pallas kernels, rear(): pl.pallas_call(functools.partial(rear_kernel, halo), out_shape=[shape(cou...  26 us
    unnamed x58, local copies, waits for them, and re-layouts  15.7 us
  transfers between devices with their start and end apart: 1, of which 0 were waited for; matrix products, arithmetic and copies ran while one was open for 2% of the time, Pallas kernels for 14%

profile of v3, /device:TPU:0, one launch (start us, length us, event | category | flops | bytes accessed | tf_op | source)
XLA Modules:
  0.0 666.1 jit_solution(18081138878381905187)
XLA Ops:
  7.2 1.3 fusion.5
  8.5 0.8 slice.140
  9.3 0.7 reshape.138
  10.0 1.5 copy.37.refs_11_.segq
  11.5 0.6 broadcast_in_dim.42
  12.2 0.6 broadcast_in_dim.40
  12.9 0.9 convert_convert_fusion.refs_10_
  13.8 3.0 concatenate.72
  16.9 0.7 maximum_maximum_fusion.refs_0_
  17.6 214.8 %front.1 = (bf16[16,1472,1024]{2,1,0:T(8,128)(2,1)}, f32[40,1024]{1,0:T(8,128)}, f32[512,1024]{1,0:T(8,128)}, f32[512,4096]{1,0:T(8,128)}, bf16[512,1024]{1,0:T(...) custom-call(bf16[48,128]{1,0:T(8,128)(2,1)} %maximum_maximum_fusion., ...), custom_call_target="tpu_custom_call" | custom-call | tf_op jit(solution)/shard_map/front/pallas_call | solution.py:783
  232.4 0.7 reduce
  233.1 0.8 broadcast_in_dim.44.seg
  234.0 30.7 %convolve.1 = (f32[512,1024]{1,0:T(8,128)}, f32[512,1024]{1,0:T(8,128)}, f32[512,1024]{1,0:T(8,128)}, f32[528,1024]{1,0:T(8,128)}, f32[512,1024]{1,0:T(8,128)}, /*index=5*/f32[2,1024]{1,0:T(2,128)}) custom-call(f32[512,1024]{1,0:T(8,128)} %get-tuple-element.62.x1, f32[512,1024]{1,0:T(8,128)} %get-tuple-element.63.o, f32[40,1024]{1,0:T(8,128)} %get-tuple-element.64.params, ...), custom_call_target="tpu_custom_call" | custom-call | tf_op jit(solution)/shard_map/convolve/pallas_call | solution.py:999
  264.7 63.0 %middle.1 = (f32[512,1024]{1,0:T(8,128)}, f32[512,1024]{1,0:T(8,128)}, f32[512,1024]{1,0:T(8,128)}, f32[2,1024]{1,0:T(2,128)}, f32[96,1024]{1,0:T(8,128)}, /*ind...) custom-call(f32[512,1024]{1,0:T(8,128)} %get-tuple-element.67.x2, f32[512,1024]{1,0:T(8,128)} %get-tuple-element.68.y, ...), custom_call_target="tpu_custom_call" | custom-call | tf_op jit(solution)/shard_map/middle/pallas_call | solution.py:1136
  327.8 34.5 %convolve_back.1 = (f32[512,1024]{1,0:T(8,128)}, bf16[512,1024]{1,0:T(8,128)(2,1)}, f32[80,1024]{1,0:T(8,128)}, bf16[8,2,1216,1024]{3,2,1,0:T(8,128)(2,1)}) custom-call(f32[512,1024]{1,0:T(8,128)} %get-tuple-element.71.dn, f32[512,1024]{1,0:T(8,128)} %get-tuple-element.68.y, f32[2,1024]{1,0:T(2,128)} %get-tuple-element.69.sums, ...), custom_call_target="tpu_custom_call", output_to_operand_aliasing={{3}: (13, {})} | custom-call | tf_op jit(solution)/shard_map/convolve_back/pallas_call | solution.py:1226
  362.3 1.1 bitcast_reduce_fusion.1
  364.6 1.5 reshape.144.window
  366.1 1.1 bitcast_reduce_fusion
  368.4 0.7 concatenate.92
  369.1 30.4 %attend_back.1 = (bf16[512,1024]{1,0:T(8,128)(2,1)}, bf16[896,1024]{1,0:T(8,128)(2,1)}, bf16[896,1024]{1,0:T(8,128)(2,1)}, f32[8,1,1920]{2,1,0:T(1,128)}) custom-call(s32[1]{0:T(128)} %bitcast.7.off, bf16[512,1024]{1,0:T(8,128)(2,1)} %get-tuple-element.79.q, bf16[896,1024]{1,0:T(8,128)(2,1)} %get-tuple-element.80.k, bf16[896,1024]{1,0:T(8,128)(2,1)} %get-tuple-element.81.v, ...), custom_call_target="tpu_custom_call" | custom-call | tf_op jit(solution)/shard_map/attend_back/pallas_call | solution.py:914
  399.5 1.4 fusion
  400.9 0.7 concatenate.94
  401.6 26.0 %rear.1 = (f32[512,1024]{1,0:T(8,128)}, f32[32,1024]{1,0:T(8,128)}, bf16[8,2,1216,1024]{3,2,1,0:T(8,128)(2,1)}) custom-call(f32[512,1024]{1,0:T(8,128)} %get-tuple-element.62.x1, f32[512,1024]{1,0:T(8,128)} %get-tuple-element.78.g2, bf16[512,1024]{1,0:T(8,128)(2,1)} %get-tuple-element.85.dq, ...), custom_call_target="tpu_custom_call", output_to_operand_aliasing={{2}: (8, {})} | custom-call | tf_op jit(solution)/shard_map/rear/pallas_call | solution.py:1328
  427.5 0.9 bitcast_reduce_fusion.2
  428.8 1.2 slice_reduce_fusion
  430.8 0.8 concatenate.93
  431.6 0.8 concatenate.89
  432.5 0.8 constant_dynamic-update-slice_fusion.2
  433.3 0.7 constant_dynamic-update-slice_fusion
  434.0 0.7 concatenate.96
  435.1 0.7 copy.44
  435.9 203.9 %last.1 = (f32[512,1024]{1,0:T(8,128)}, f32[64,4096]{1,0:T(8,128)}, f32[256,1024]{1,0:T(8,128)}, f32[64,3072]{1,0:T(8,128)}, f32[64,1024]{1,0:T(8,128)}, /*index...) custom-call(bf16[512,1024]{1,0:T(8,128)(2,1)} %bitcast.28, ...), custom_call_target="tpu_custom_call", output_to_operand_aliasing={{11}: (7, {})} | custom-call | tf_op jit(solution)/shard_map/last/pallas_call | solution.py:1505
  639.8 0.7 slice.171
  640.5 0.8 slice_select_fusion
  641.3 0.7 reshape.157
  642.0 0.8 slice.165
  644.1 0.7 reshape.156
  645.9 3.3 copy.83
  649.3 1.3 copy.84
  650.6 0.6 copy-done.4
  651.2 1.0 copy.85
  652.8 1.0 copy.86
  653.8 0.9 copy.87
  654.7 0.7 copy.88
  655.4 0.8 copy.89
  656.2 0.7 copy.90
  656.9 1.0 copy.91
  657.9 1.0 copy.92
  (91 shorter events, 7.4 us)
Async XLA Ops:
  7.2 428.7 %reduce-scatter.2.cloned.1.call-start = ((), (), s32[]{:S(2)}) async-start(), calls=%async_computation.1 | async-start | bytes 8912896 | tf_op jit(solution)/shard_map/reduce_scatter | solution.py:1611
  12.9 1.0 copy-start.12
  363.3 0.6 copy-start.9
  367.2 0.6 copy-start.10
  367.8 0.6 copy-start.11
  645.9 3.3 copy-start
  649.2 2.0 copy-start.4
  651.2 1.6 copy-start.3
  651.2 2.6 copy-start.5
  652.8 1.9 copy-start.8
  652.8 2.6 copy-start.6
  652.8 3.4 copy-start.7
  653.8 3.1 copy-start.2
  654.7 3.2 copy-start.1
Sparse Core Ops, SparseCore 0:
  327.9 102.7 reduce-scatter.1

commit v4 on v3

--- a/solution.py
+++ b/solution.py
@@ -1523,11 +1523,12 @@
 
 
 def slab_rows(gains, shifts, ffn_bias, conv_kernel, rel_table):
-    rows = jnp.concatenate([gains, shifts, jnp.zeros((8, 64), BF16), conv_kernel, rel_table[None], jnp.zeros((6, 64), BF16)], axis=0)
-    zero = jnp.zeros_like(rows)
+    parts = ((0, gains), (6, shifts), (28, conv_kernel), (33, rel_table[None]))
+    rows = sum(jnp.pad(part, ((at, 48 - at - part.shape[0]), (0, 0))) for at, part in parts)
     odd = lax.rem(lax.axis_index("rows"), 2) == 1
-    wide = jnp.concatenate([jnp.where(odd, zero, rows), jnp.where(odd, rows, zero)], axis=1)
-    return jnp.concatenate([wide, ffn_bias.reshape(4, 128), jnp.zeros((4, 128), BF16)], axis=0)
+    wide = jnp.tile(rows, (1, 2))
+    keep = (lax.broadcasted_iota(jnp.int32, wide.shape, 1) >= 64) == odd
+    return jnp.where(keep, wide, jnp.zeros_like(wide)) + jnp.pad(ffn_bias.reshape(4, 128), ((40, 4), (0, 0)))
 
 
 def wide_rows(smalls):

time: 670 us -> 667 us (level)
  no operation moved by 1% of the time
where the time goes in v4:
time: 667 us; the launch traced here: 664 us
  Pallas kernels  603 us (90%)
  local copies, waits for them, and re-layouts  36.2 us (5%)
  between operations  14.8 us (2%)
  other arithmetic  8.1 us (1%)
    pallas_call x1, Pallas kernels, front(): pl.pallas_call(functools.partial(front_kernel, tuple(blocks)), out_shape=...  215 us
    pallas_call x1, Pallas kernels, last(): pl.pallas_call(functools.partial(last_kernel, units, ready, QKV), out_sha...  204 us
    pallas_call x1, Pallas kernels, middle(): pl.pallas_call(functools.partial(middle_kernel, frames), out_shape=[shape...  63.1 us
    pallas_call x1, Pallas kernels, convolve_back(): pl.pallas_call(functools.partial(convolve_back_kernel, frames), out_shape...  34.5 us
    pallas_call x1, Pallas kernels, convolve(): pl.pallas_call(convolve_kernel, out_shape=[shape(count, 1024), shape(coun...  30.7 us
    pallas_call x1, Pallas kernels, attend_back(): pl.pallas_call(functools.partial(attend_back_kernel, 1.0 / math.sqrt(128)...  30.4 us
    pallas_call x1, Pallas kernels, rear(): pl.pallas_call(functools.partial(rear_kernel, halo), out_shape=[shape(cou...  25.9 us
    unnamed x58, local copies, waits for them, and re-layouts  15.7 us
  transfers between devices with their start and end apart: 1, of which 0 were waited for; matrix products, arithmetic and copies ran while one was open for 2% of the time, Pallas kernels for 14%

profile of v4, /device:TPU:0, one launch (start us, length us, event | category | flops | bytes accessed | tf_op | source)
XLA Modules:
  0.0 663.8 jit_solution(16293306764347466929)
XLA Ops:
  7.2 1.3 fusion.5
  8.5 0.8 slice.140
  9.3 0.7 reshape.142
  10.0 0.7 pad_add_fusion.1
  10.8 1.5 copy.37.refs_11_.segq
  12.4 0.6 broadcast_in_dim.30
  13.0 0.6 broadcast_in_dim.28
  13.8 0.9 convert_convert_fusion.refs_10_
  15.2 214.8 %front.1 = (bf16[16,1472,1024]{2,1,0:T(8,128)(2,1)}, f32[40,1024]{1,0:T(8,128)}, f32[512,1024]{1,0:T(8,128)}, f32[512,4096]{1,0:T(8,128)}, bf16[512,1024]{1,0:T(...) custom-call(bf16[48,128]{1,0:T(8,128)(2,1)} %pad_add_fusion.refs_0_,, ...), custom_call_target="tpu_custom_call" | custom-call | tf_op jit(solution)/shard_map/front/pallas_call | solution.py:783
  230.0 0.7 reduce
  230.8 0.8 broadcast_in_dim.32.seg
  231.6 30.7 %convolve.1 = (f32[512,1024]{1,0:T(8,128)}, f32[512,1024]{1,0:T(8,128)}, f32[512,1024]{1,0:T(8,128)}, f32[528,1024]{1,0:T(8,128)}, f32[512,1024]{1,0:T(8,128)}, /*index=5*/f32[2,1024]{1,0:T(2,128)}) custom-call(f32[512,1024]{1,0:T(8,128)} %get-tuple-element.62.x1, f32[512,1024]{1,0:T(8,128)} %get-tuple-element.63.o, f32[40,1024]{1,0:T(8,128)} %get-tuple-element.64.params, ...), custom_call_target="tpu_custom_call" | custom-call | tf_op jit(solution)/shard_map/convolve/pallas_call | solution.py:999
  262.3 63.1 %middle.1 = (f32[512,1024]{1,0:T(8,128)}, f32[512,1024]{1,0:T(8,128)}, f32[512,1024]{1,0:T(8,128)}, f32[2,1024]{1,0:T(2,128)}, f32[96,1024]{1,0:T(8,128)}, /*ind...) custom-call(f32[512,1024]{1,0:T(8,128)} %get-tuple-element.67.x2, f32[512,1024]{1,0:T(8,128)} %get-tuple-element.68.y, ...), custom_call_target="tpu_custom_call" | custom-call | tf_op jit(solution)/shard_map/middle/pallas_call | solution.py:1136
  325.4 34.5 %convolve_back.1 = (f32[512,1024]{1,0:T(8,128)}, bf16[512,1024]{1,0:T(8,128)(2,1)}, f32[80,1024]{1,0:T(8,128)}, bf16[8,2,1216,1024]{3,2,1,0:T(8,128)(2,1)}) custom-call(f32[512,1024]{1,0:T(8,128)} %get-tuple-element.71.dn, f32[512,1024]{1,0:T(8,128)} %get-tuple-element.68.y, f32[2,1024]{1,0:T(2,128)} %get-tuple-element.69.sums, ...), custom_call_target="tpu_custom_call", output_to_operand_aliasing={{3}: (13, {})} | custom-call | tf_op jit(solution)/shard_map/convolve_back/pallas_call | solution.py:1226
  359.9 1.1 bitcast_reduce_fusion.1
  362.2 1.5 reshape.148.window
  363.7 1.1 bitcast_reduce_fusion
  366.1 0.7 concatenate.80
  366.8 30.4 %attend_back.1 = (bf16[512,1024]{1,0:T(8,128)(2,1)}, bf16[896,1024]{1,0:T(8,128)(2,1)}, bf16[896,1024]{1,0:T(8,128)(2,1)}, f32[8,1,1920]{2,1,0:T(1,128)}) custom-call(s32[1]{0:T(128)} %bitcast.7.off, bf16[512,1024]{1,0:T(8,128)(2,1)} %get-tuple-element.79.q, bf16[896,1024]{1,0:T(8,128)(2,1)} %get-tuple-element.80.k, bf16[896,1024]{1,0:T(8,128)(2,1)} %get-tuple-element.81.v, ...), custom_call_target="tpu_custom_call" | custom-call | tf_op jit(solution)/shard_map/attend_back/pallas_call | solution.py:914
  397.2 1.4 fusion
  398.5 0.7 concatenate.82
  399.2 25.9 %rear.1 = (f32[512,1024]{1,0:T(8,128)}, f32[32,1024]{1,0:T(8,128)}, bf16[8,2,1216,1024]{3,2,1,0:T(8,128)(2,1)}) custom-call(f32[512,1024]{1,0:T(8,128)} %get-tuple-element.62.x1, f32[512,1024]{1,0:T(8,128)} %get-tuple-element.78.g2, bf16[512,1024]{1,0:T(8,128)(2,1)} %get-tuple-element.85.dq, ...), custom_call_target="tpu_custom_call", output_to_operand_aliasing={{2}: (8, {})} | custom-call | tf_op jit(solution)/shard_map/rear/pallas_call | solution.py:1328
  425.2 1.0 bitcast_reduce_fusion.2
  426.4 1.2 slice_reduce_fusion
  428.4 0.8 concatenate.81
  429.2 0.8 concatenate.77
  430.2 0.8 constant_dynamic-update-slice_fusion.2
  431.0 0.7 constant_dynamic-update-slice_fusion
  431.7 0.7 concatenate.84
  432.8 0.7 copy.44
  433.5 203.9 %last.1 = (f32[512,1024]{1,0:T(8,128)}, f32[64,4096]{1,0:T(8,128)}, f32[256,1024]{1,0:T(8,128)}, f32[64,3072]{1,0:T(8,128)}, f32[64,1024]{1,0:T(8,128)}, /*index...) custom-call(bf16[512,1024]{1,0:T(8,128)(2,1)} %bitcast.28, ...), custom_call_target="tpu_custom_call", output_to_operand_aliasing={{11}: (7, {})} | custom-call | tf_op jit(solution)/shard_map/last/pallas_call | solution.py:1505
  637.4 0.7 slice.171
  638.1 0.8 slice_select_fusion
  639.0 0.7 reshape.161
  639.7 0.8 slice.165
  641.7 0.7 reshape.160
  643.6 3.3 copy.83
  646.9 1.3 copy.84
  648.2 0.6 copy-done.4
  648.9 1.0 copy.85
  649.8 0.6 copy-done.3
  650.5 1.0 copy.86
  651.4 0.9 copy.87
  652.3 0.7 copy.88
  653.0 0.8 copy.89
  653.8 0.7 copy.90
  654.5 1.0 copy.91
  655.5 1.0 copy.92
  (89 shorter events, 7.4 us)
Async XLA Ops:
  7.2 426.3 %reduce-scatter.2.cloned.1.call-start = ((), (), s32[]{:S(2)}) async-start(), calls=%async_computation.1 | async-start | bytes 8912896 | tf_op jit(solution)/shard_map/reduce_scatter | solution.py:1612
  13.8 1.5 copy-start.12
  361.0 0.6 copy-start.9
  364.8 0.6 copy-start.10
  365.5 0.6 copy-start.11
  643.6 3.3 copy-start
  646.9 2.0 copy-start.4
  648.9 1.6 copy-start.3
  648.9 2.6 copy-start.5
  650.5 1.9 copy-start.8
  650.5 2.6 copy-start.6
  650.5 3.4 copy-start.7
  651.4 3.1 copy-start.2
  652.3 3.2 copy-start.1
Sparse Core Ops, SparseCore 0:
  325.6 102.7 reduce-scatter.1
